TPU v7x, 32 devices: a whole 2x2x4 slice. The times are simulated.
32 devices in a mesh: dp: 8 (over z, core), seq: 4 (over y, x).
Axes of the slice: x: 2, y: 2, z: 4, core: 2. Of those that a mesh axis runs over, the one named last changes fastest.
Arguments:
- layer_input: bfloat16 [16, 2048, 1024], P('dp', 'seq'), may hold values from -6 to 6
- cotangent: bfloat16 [16, 2048, 1024], P('dp', 'seq'), may hold values from -6 to 6
- doc_ids: int32 [16, 2048], P('dp'), may hold values from 0 to 5, never falling along the last dimension, each value on 1 to 1024 neighbouring positions
- resets: int32 [16, 2048], P('dp'), may hold values 0 or 1
- mix_weight: bfloat16 [1024, 4224], P(('dp', 'seq')), may hold values from -0.1875 to 0.1875
- value_weight: bfloat16 [1024, 2048], P(('dp', 'seq')), may hold values from -0.1875 to 0.1875
- head_weight: bfloat16 [2048, 1024], P(('dp', 'seq')), may hold values from -0.5 to 0.5
- expand_weight: bfloat16 [1024, 4096], P(('dp', 'seq')), may hold values from -0.1875 to 0.1875
- shrink_weight: bfloat16 [4096, 1024], P(('dp', 'seq')), may hold values from -0.09375 to 0.09375
- chan_vectors: float32 [3, 1024], replicated, may hold values from 0.25 to 1.75
- ema_logits: float32 [2, 1024, 16], replicated, may hold values from -5 to 0
- ema_beta_eta: float32 [2, 1024, 16], replicated, may hold values from -3 to 3
- z_affine: float32 [3, 128], replicated, may hold values from -6 to 6
Outputs:
- output: bfloat16 [16, 2048, 1024], P('dp', 'seq')
- x_grad: float32 [16, 2048, 1024], P('dp', 'seq')
- mix_grad: float32 [1024, 4224], P(('dp', 'seq'))
- value_grad: float32 [1024, 2048], P(('dp', 'seq'))
- head_grad: float32 [2048, 1024], P(('dp', 'seq'))
- expand_grad: float32 [1024, 4096], P(('dp', 'seq'))
- shrink_grad: float32 [4096, 1024], P(('dp', 'seq'))
- chan_grad: float32 [3, 1024], replicated
- logits_grad: float32 [2, 1024, 16], replicated
- coef_grad: float32 [2, 1024, 16], replicated
- affine_grad: float32 [3, 128], replicated
All inputs are finite; a program needn't handle non-finite values. No bound on the sum of `resets` on one device may be relied on, other than what follows from the above.
Results may differ from a plain program's by a relative error of at most 0.023.
The roundings to bfloat16 on the way count: a program that leaves them out, or rounds other values in their place, can miss the bound.
Values may be sent and summed in bfloat16 or wider, within the bound.
A program may use at most 576 MiB of HBM per device.

v0:
```python
import jax
import jax.numpy as jnp
from jax import lax
from jax.sharding import PartitionSpec as P

Z = 128
V = 2048
MICRO = 2


HIGH_MODE = lax.Precision.HIGHEST
NEG_FILL = -1000000000.0


def layer_norm(values):
    center = values - jnp.mean(values, axis=-1, keepdims=True)
    spread = jnp.mean(center * center, axis=-1, keepdims=True)
    return center * lax.rsqrt(spread + 1e-05)


def scaled_norm(values, gain):
    return layer_norm(values) * gain


def silu_slope(values):
    squash = jax.nn.sigmoid(values)
    return squash * (1.0 + values * (1.0 - squash))


def product(left, right):
    return jnp.dot(left, right, preferred_element_type=jnp.float32)


def against(left, right):
    return lax.dot_general(
        left, right, (((1,), (1,)), ((), ())), preferred_element_type=jnp.float32
    )


def transposed(left, right):
    return lax.dot_general(
        left, right, (((0,), (0,)), ((), ())), preferred_element_type=jnp.float32
    )


def round_trip(values):
    return lax.optimization_barrier(values.astype(jnp.bfloat16)).astype(jnp.float32)


def ema_blocks(inputs, reset_rows, logit_part, coef_part):
    rows, length, chans = inputs.shape
    block = min(128, length)
    count = length // block
    rate = jax.nn.sigmoid(logit_part[0])
    damping = jax.nn.sigmoid(logit_part[1])
    decay = 1.0 - rate * damping
    weight_in = rate * coef_part[0]
    weight_out = coef_part[1]
    steps_up = jnp.arange(block + 1).astype(jnp.float32)
    powers = decay[None] ** steps_up[:, None, None]
    kernel = jnp.einsum("nch,ch->nc", powers[:block], weight_in * weight_out, precision=HIGH_MODE)
    later = jnp.arange(block)[:, None]
    earlier = jnp.arange(block)[None, :]
    lower = (later >= earlier).astype(jnp.float32)
    toeplitz = jnp.take(kernel, jnp.maximum(later - earlier, 0), axis=0) * lower[:, :, None]
    carry_out = weight_out[None] * powers[1:]
    feed_in = weight_in[None] * powers[:block][::-1]
    end_decay = powers[block]

    def advance(state, item):
        piece, flags = item
        segment = jnp.cumsum(flags, axis=1)
        same = (segment[:, :, None] == segment[:, None, :]).astype(jnp.float32)
        intra = jnp.einsum("tsc,rts,rsc->rtc", toeplitz, same, piece, precision=HIGH_MODE)
        alive = (segment == 0).astype(jnp.float32)
        inter = (
            jnp.einsum("tch,rch->rtc", carry_out, state, precision=HIGH_MODE) * alive[:, :, None]
        )
        tail = (segment == segment[:, -1:]).astype(jnp.float32)
        fresh = jnp.einsum("rs,sch,rsc->rch", tail, feed_in, piece, precision=HIGH_MODE)
        state = alive[:, -1][:, None, None] * end_decay[None] * state + fresh
        return (state, intra + inter)

    pieces = inputs.reshape(rows, count, block, chans).transpose(1, 0, 2, 3)
    flag_pieces = reset_rows.reshape(rows, count, block).transpose(1, 0, 2)
    start = jnp.zeros((rows, chans, decay.shape[1]), jnp.float32)
    _, outputs = lax.scan(jax.checkpoint(advance), start, (pieces, flag_pieces))
    return outputs.transpose(1, 0, 2, 3).reshape(rows, length, chans)


def on_device(
    layer_input,
    cotangent,
    doc_ids,
    resets,
    mix_weight,
    value_weight,
    head_weight,
    expand_weight,
    shrink_weight,
    chan_vectors,
    ema_logits,
    ema_beta_eta,
    z_affine,
):
    seq_count = lax.axis_size("seq")
    seq_place = lax.axis_index("seq")
    all_rows, places, width = layer_input.shape
    length = doc_ids.shape[1]
    batch_rows = all_rows // MICRO
    chans = width // seq_count
    tokens = batch_rows * places
    scale = Z ** (-0.5)
    local_logits = lax.dynamic_slice_in_dim(ema_logits, seq_place * chans, chans, 1)
    local_coefs = lax.dynamic_slice_in_dim(ema_beta_eta, seq_place * chans, chans, 1)
    query_places = seq_place * places + jnp.arange(places)
    key_places = jnp.arange(length)
    causal = key_places[None, :] <= query_places[:, None]
    weight_sums = None
    small_sums = None
    out_parts = []
    grad_parts = []
    for batch in range(MICRO):
        lower_row = batch * batch_rows
        upper_row = lower_row + batch_rows
        mix_full, value_full, head_full, expand_full, shrink_full = (
            lax.all_gather(mix_weight, ("dp", "seq"), axis=0, tiled=True),
            lax.all_gather(value_weight, ("dp", "seq"), axis=0, tiled=True),
            lax.all_gather(head_weight, ("dp", "seq"), axis=0, tiled=True),
            lax.all_gather(expand_weight, ("dp", "seq"), axis=0, tiled=True),
            lax.all_gather(shrink_weight, ("dp", "seq"), axis=0, tiled=True),
        )
        input_batch = layer_input[lower_row:upper_row]
        doc_batch = doc_ids[lower_row:upper_row]
        reset_batch = resets[lower_row:upper_row]
        inputs32 = input_batch.astype(jnp.float32)
        normed, first_pull = jax.vjp(scaled_norm, inputs32, chan_vectors[0])
        normed_low = normed.astype(jnp.bfloat16)
        spread = lax.all_to_all(normed_low, "seq", split_axis=2, concat_axis=1, tiled=True)

        def ema_local(feed, logit_part, coef_part):
            return ema_blocks(feed, reset_batch, logit_part, coef_part)

        ema_out, ema_pull = jax.vjp(
            ema_local, spread.astype(jnp.float32), local_logits, local_coefs
        )
        returned = lax.all_to_all(
            ema_out.astype(jnp.bfloat16), "seq", split_axis=1, concat_axis=2, tiled=True
        ).astype(jnp.float32)
        premix = (returned + chan_vectors[2] * normed).reshape(tokens, width)
        mixed_low = jax.nn.silu(premix).astype(jnp.bfloat16)
        projected = product(mixed_low, mix_full)
        shared_pre = projected[:, :Z]
        reset_pre = projected[:, Z : Z + V]
        head_base = projected[:, Z + V : Z + V + width]
        update_pre = projected[:, Z + V + width :]
        shared = jax.nn.silu(shared_pre)
        queries_low = (shared * z_affine[0] + z_affine[1]).astype(jnp.bfloat16)
        keys_low = (shared * z_affine[2]).astype(jnp.bfloat16)
        normed_flat = normed_low.reshape(tokens, width)
        value_pre = product(normed_flat, value_full)
        values_low = jax.nn.silu(value_pre).astype(jnp.bfloat16)
        reset_gate = jax.nn.silu(reset_pre)
        update_gate = jax.nn.sigmoid(update_pre)
        query_rows = queries_low.reshape(batch_rows, places, Z)
        key_rows = keys_low.reshape(batch_rows, places, Z)
        value_rows = values_low.reshape(batch_rows, places, V)
        key_all, value_all = (
            lax.all_gather(key_rows, "seq", axis=1, tiled=True),
            lax.all_gather(value_rows, "seq", axis=1, tiled=True),
        )
        query_docs = lax.dynamic_slice_in_dim(doc_batch, seq_place * places, places, 1)
        allowed = causal[None] & (query_docs[:, :, None] == doc_batch[:, None, :])
        scores = (
            jnp.einsum("rid,rjd->rij", query_rows, key_all, preferred_element_type=jnp.float32)
            * scale
        )
        scores = jnp.where(allowed, scores, NEG_FILL)
        peak = jnp.max(scores, axis=-1, keepdims=True)
        expo = jnp.exp(scores - peak)
        total = jnp.sum(expo, axis=-1, keepdims=True)
        probs = expo / total
        probs_low = probs.astype(jnp.bfloat16)
        attended = jnp.einsum(
            "rij,rjv->riv", probs_low, value_all, preferred_element_type=jnp.float32
        ).reshape(tokens, V)
        gated_low = (reset_gate * attended).astype(jnp.bfloat16)
        head_pre = head_base + product(gated_low, head_full)
        candidate = jax.nn.silu(head_pre)
        residual_in = inputs32.reshape(tokens, width)
        first = residual_in + update_gate * (candidate - residual_in)
        second, second_pull = jax.vjp(scaled_norm, first, chan_vectors[1])
        second_low = second.astype(jnp.bfloat16)
        expand_pre = product(second_low, expand_full)
        hidden_low = jax.nn.silu(expand_pre).astype(jnp.bfloat16)
        result = first + product(hidden_low, shrink_full)
        out_parts.append(result.astype(jnp.bfloat16).reshape(batch_rows, places, width))
        cot_low = cotangent[lower_row:upper_row].reshape(tokens, width)
        d_hidden = against(cot_low, shrink_full)
        g_shrink = transposed(hidden_low, cot_low)
        d_expand = (d_hidden * silu_slope(expand_pre)).astype(jnp.bfloat16)
        d_second = against(d_expand, expand_full)
        g_expand = transposed(second_low, d_expand)
        d_first_norm, d_gain_two = second_pull(d_second)
        d_first = cot_low.astype(jnp.float32) + d_first_norm
        d_update = d_first * (candidate - residual_in)
        d_direct = d_first * (1.0 - update_gate)
        d_head = d_first * update_gate * silu_slope(head_pre)
        d_head_low = d_head.astype(jnp.bfloat16)
        d_gated = against(d_head_low, head_full)
        g_head = transposed(gated_low, d_head_low)
        d_reset = d_gated * attended * silu_slope(reset_pre)
        d_attended = (d_gated * reset_gate).astype(jnp.bfloat16).reshape(batch_rows, places, V)
        d_probs = jnp.einsum(
            "riv,rjv->rij", d_attended, value_all, preferred_element_type=jnp.float32
        )
        balance = jnp.sum(probs * d_probs, axis=-1)
        d_scores = (probs * (d_probs - balance[..., None])).astype(jnp.bfloat16)
        d_queries = scale * jnp.einsum(
            "rij,rjd->rid", d_scores, key_all, preferred_element_type=jnp.float32
        )
        key_term = scale * jnp.einsum(
            "rij,rid->rjd", d_scores, query_rows, preferred_element_type=jnp.float32
        )
        value_term = jnp.einsum(
            "rij,riv->rjv", probs_low, d_attended, preferred_element_type=jnp.float32
        )
        d_keys, d_values = (
            lax.psum_scatter(
                key_term.astype(jnp.bfloat16), "seq", scatter_dimension=1, tiled=True
            ).astype(jnp.float32),
            lax.psum_scatter(
                value_term.astype(jnp.bfloat16), "seq", scatter_dimension=1, tiled=True
            ).astype(jnp.float32),
        )
        d_keys32 = round_trip(d_keys).reshape(tokens, Z)
        d_values32 = round_trip(d_values).reshape(tokens, V)
        d_value_pre = (d_values32 * silu_slope(value_pre)).astype(jnp.bfloat16)
        d_normed_value = against(d_value_pre, value_full)
        g_value = transposed(normed_flat, d_value_pre)
        d_query_flat = d_queries.reshape(tokens, Z)
        d_shared = d_query_flat * z_affine[0] + d_keys32 * z_affine[2]
        g_affine = jnp.stack(
            [
                jnp.sum(d_query_flat * shared, axis=0),
                jnp.sum(d_query_flat, axis=0),
                jnp.sum(d_keys32 * shared, axis=0),
            ]
        )
        d_projected = jnp.concatenate(
            [
                d_shared * silu_slope(shared_pre),
                d_reset,
                d_head,
                d_update * update_gate * (1.0 - update_gate),
            ],
            axis=1,
        ).astype(jnp.bfloat16)
        d_mixed = against(d_projected, mix_full)
        g_mix = transposed(mixed_low, d_projected)
        d_premix = d_mixed * silu_slope(premix)
        normed_rows = normed.reshape(tokens, width)
        g_omega = jnp.sum(d_premix * normed_rows, axis=0)
        d_premix_rows = d_premix.reshape(batch_rows, places, width)
        grad_spread = lax.all_to_all(
            d_premix_rows.astype(jnp.bfloat16), "seq", split_axis=2, concat_axis=1, tiled=True
        )
        d_feed, g_logit_part, g_coef_part = ema_pull(grad_spread.astype(jnp.float32))
        grad_back = lax.all_to_all(
            d_feed.astype(jnp.bfloat16), "seq", split_axis=1, concat_axis=2, tiled=True
        ).astype(jnp.float32)
        d_normed = (d_premix * chan_vectors[2] + d_normed_value).reshape(
            batch_rows, places, width
        ) + grad_back
        d_input_norm, d_gain_one = first_pull(d_normed)
        grad_parts.append(d_direct.reshape(batch_rows, places, width) + d_input_norm)
        g_logits = lax.dynamic_update_slice_in_dim(
            jnp.zeros(ema_logits.shape, jnp.float32), g_logit_part, seq_place * chans, 1
        )
        g_coefs = lax.dynamic_update_slice_in_dim(
            jnp.zeros(ema_beta_eta.shape, jnp.float32), g_coef_part, seq_place * chans, 1
        )
        g_chan = jnp.stack([d_gain_one, d_gain_two, g_omega])
        new_weights = (g_mix, g_value, g_head, g_expand, g_shrink)
        new_small = (g_chan, g_logits, g_coefs, g_affine)
        if weight_sums is None:
            weight_sums = new_weights
            small_sums = new_small
        else:
            weight_sums = tuple((left + right for left, right in zip(weight_sums, new_weights)))
            small_sums = tuple((left + right for left, right in zip(small_sums, new_small)))
    mix_grad, value_grad, head_grad, expand_grad, shrink_grad = lax.psum_scatter(
        weight_sums, ("dp", "seq"), scatter_dimension=0, tiled=True
    )
    chan_grad, logits_grad, coef_grad, affine_grad = lax.psum(small_sums, ("dp", "seq"))
    output = jnp.concatenate(out_parts, axis=0)
    x_grad = jnp.concatenate(grad_parts, axis=0)
    return (
        output,
        x_grad,
        mix_grad,
        value_grad,
        head_grad,
        expand_grad,
        shrink_grad,
        chan_grad,
        logits_grad,
        coef_grad,
        affine_grad,
    )


def solution(mesh):
    placed = (
        P("dp", "seq", None),
        P("dp", "seq", None),
        P("dp", None),
        P("dp", None),
        P(("dp", "seq"), None),
        P(("dp", "seq"), None),
        P(("dp", "seq"), None),
        P(("dp", "seq"), None),
        P(("dp", "seq"), None),
        P(),
        P(),
        P(),
        P(),
    )
    return jax.shard_map(
        on_device,
        mesh=mesh,
        in_specs=placed,
        out_specs=(
            P("dp", "seq", None),
            P("dp", "seq", None),
            P(("dp", "seq"), None),
            P(("dp", "seq"), None),
            P(("dp", "seq"), None),
            P(("dp", "seq"), None),
            P(("dp", "seq"), None),
            P(),
            P(),
            P(),
            P(),
        ),
        check_vma=False,
    )
```

profile of v0, /device:TPU:0, one launch (start us, length us, event | category | flops | bytes accessed | tf_op | source)
XLA Modules:
  0.0 3869.5 jit_solution(3828353300833909383)
XLA Ops:
  14.2 61.4 %all-gather.14.cloned.1.call-done = bf16[1024,2048]{1,0:T(8,128)(2,1)} async-done(((bf16[32,2048]{1,0:T(8,128)(2,1)}), bf16[1024,2048]{1,0:T(8,128)(2,1)}) %all-gather.14.cloned.1.call-update) | async-done | bytes 4194320 | tf_op jit(solution)/shard_map/all_gather | solution.py:128
  121.4 61.7 %gather_fusion = f32[16384,256]{1,0:T(8,128)} fusion(f32[128,256]{1,0:T(8,128)S(1)} %bitcast.837, s32[16384]{0:T(1024)S(1)} %broadcast_clamp_fusion), kind=kCustom, calls=%fused_computation.clone | custom fusion | bytes 33619968 | tf_op jit(solution)/shard_map/jvp(jit(_take))/gather | solution.py:65
  183.1 11.9 select_multiply_fusion
  232.8 10.7 all-to-all-done.2
  257.6 255.2 %while.81 = (s32[]{:T(128)}, f32[1,256,16]{1,2,0:T(8,128)S(1)}, bf16[16,1,128,256]{3,2,1,0:T(8,128)(2,1)S(1)}, f32[16,1,256,16]{2,3,1,0:T(8,128)}, s32[16,1,128]...) while((s32[]{:T(128)}, f32[1,256,16]{1,2,0:T(8,128)S(1)}, ...), condition=%wide.region_13.15_spmd.clone, body=%wide.region_11.14_spmd.clone.sunk | while | flops 14778884 | bytes 22697780 | solution.py:87
  512.9 12.9 copy.180
  525.8 12.0 reduce.59
  544.8 260.6 %while.80 = (s32[]{:T(128)}, f32[1,256,16]{1,2,0:T(8,128)S(1)}, bf16[16,1,128,256]{3,2,1,0:T(8,128)(2,1)}, f32[16,1,256,16]{2,3,1,0:T(8,128)}, s32[16,1,128]{2,1...) while((s32[]{:T(128)}, f32[1,256,16]{1,2,0:T(8,128)S(1)}, ...), condition=%wide.region_4.6_spmd.clone, body=%wide.region_2.5_spmd.clone.sunk | while | flops 14778884 | bytes 22697780 | solution.py:87
  809.8 12.5 reduce.57
  833.3 10.2 all-to-all-done.1
  849.0 9.6 fusion.152
  864.3 10.7 all-gather
  891.4 13.1 multiply_convert_fusion.10
  911.7 13.0 multiply_convert_fusion.12
  934.8 12.0 fusion.149
  946.8 10.0 multiply_convert_fusion.1
  961.5 10.5 fusion.150
  971.9 10.6 multiply_convert_fusion
  982.5 12.2 multiply_reduce_fusion.23
  1027.3 10.0 multiply_convert_fusion.9
  1051.4 11.0 convert_bitcast_fusion
  1064.4 14.1 reduce-scatter.10.cloned.1.call-done
  1085.0 10.7 multiply_multiply_fusion.1
  1095.8 9.7 multiply_multiply_fusion
  1123.0 9.6 convert_bitcast_fusion.1
  1191.7 494.5 %while.83 = (s32[]{:T(128)}, f32[128,128,256]{2,1,0:T(8,128)}, f32[128,256,16]{1,2,0:T(8,128)}, f32[128,256,16]{1,2,0:T(8,128)}, f32[256,16]{0,1:T(8,128)S(1)}, ...) while((s32[]{:T(128)}, f32[128,128,256]{2,1,0:T(8,128)}, ...), condition=%wide.region_35.37_spmd.clone, body=%wide.region_33.36_spmd.clone.sunk | while | flops 34746884 | bytes 242031136 | solution.py:87
  1687.6 486.9 %while.82 = (s32[]{:T(128)}, f32[128,128,256]{2,1,0:T(8,128)}, f32[128,256,16]{1,2,0:T(8,128)}, f32[128,256,16]{1,2,0:T(8,128)}, f32[256,16]{0,1:T(8,128)S(1)}, ...) while((s32[]{:T(128)}, f32[128,128,256]{2,1,0:T(8,128)}, ...), condition=%wide.region_25.27_spmd.clone, body=%wide.region_23.26_spmd.clone.sunk | while | flops 34746884 | bytes 242031136 | solution.py:87
  2184.1 21.9 broadcast_multiply_fusion.1
  2206.0 98.6 %scatter_custom_fusion = f32[128,256]{1,0:T(8,128)S(1)} fusion(s32[16384]{0:T(1024)} %fusion.115, f32[16384,256]{1,0:T(8,128)} %bitcast.846, f32[]{:T(128)} %constant.194.clone.1), kind=kCustom, calls=%fused_computation.324 | custom fusion | flops 4194304 | bytes 131584 | tf_op jit(solution)/shard_map/transpose(jvp(jit(_take)))/scatter-add | solution.py:65
  2304.7 99.1 %scatter_custom_fusion.1 = f32[128,256]{1,0:T(8,128)S(1)} fusion(s32[16384]{0:T(1024)} %fusion.115, f32[16384,256]{1,0:T(8,128)} %bitcast.845, f32[]{:T(128)} %constant.194.clone.1), kind=kCustom, calls=%fused_computation.322 | custom fusion | flops 4194304 | bytes 131584 | tf_op jit(solution)/shard_map/transpose(jvp(jit(_take)))/scatter-add | solution.py:65
  2424.5 14.1 fusion.100
  2438.6 18.8 convolution_add_fusion
  2472.3 12.0 fusion.80
  2484.3 14.8 convolution_add_fusion.2
  2499.7 13.5 fusion.148
  2513.2 11.7 convolution_add_fusion.1
  2526.2 12.9 copy.178
  2539.0 11.6 reduce.61
  2556.2 12.1 fusion.76
  2568.3 12.9 copy.179
  2581.2 12.5 reduce.63
  2601.6 10.5 fusion.77
  2648.1 42.9 %all-reduce.16 = (f32[3,1024]{1,0:T(4,128)}, f32[3,128]{1,0:T(4,128)}) all-reduce(f32[3,1024]{1,0:T(4,128)S(1)} %maximum_add_fusion, f32[3,128]{1,0:T(4,128)S(1)} %maximum_add_fusion.1), channel_id=1, replica_groups=mesh['dp'=8,'seq'=4] {'dp','seq'}, use_global_device_ids=true, to_apply=%region_49.51 | all-reduce | flops 3456 | bytes 27648 | tf_op jit(solution)/shard_map/psum | solution.py:295
  2701.2 47.8 %reduce-scatter.22.cloned.1.call-done = f32[64,1024]{1,0:T(8,128)} async-done(((f32[2048,1024]{1,0:T(8,128)}), f32[64,1024]{1,0:T(8,128)}) %reduce-scatter.22.cloned.1.call-update) | async-done | bytes 262160 | tf_op jit(solution)/shard_map/reduce_scatter | solution.py:292
  2749.1 202.3 %reduce-scatter.18.cloned.1.call-done = f32[32,4224]{1,0:T(8,128)} async-done(((f32[1024,4224]{1,0:T(8,128)}), f32[32,4224]{1,0:T(8,128)}) %reduce-scatter.18.cloned.1.call-update) | async-done | bytes 540688 | tf_op jit(solution)/shard_map/reduce_scatter | solution.py:292
  2951.4 185.2 %reduce-scatter.20.cloned.1.call-done = f32[32,2048]{1,0:T(8,128)} async-done(((f32[1024,2048]{1,0:T(8,128)}), f32[32,2048]{1,0:T(8,128)}) %reduce-scatter.20.cloned.1.call-update) | async-done | bytes 262160 | tf_op jit(solution)/shard_map/reduce_scatter | solution.py:292
  3136.5 361.4 %reduce-scatter.26.cloned.1.call-done = f32[128,1024]{1,0:T(8,128)} async-done(((f32[4096,1024]{1,0:T(8,128)}), f32[128,1024]{1,0:T(8,128)}) %reduce-scatter.26.cloned.1.call-update) | async-done | bytes 524304 | tf_op jit(solution)/shard_map/reduce_scatter | solution.py:292
  3497.9 361.7 %reduce-scatter.24.cloned.1.call-done = f32[32,4096]{1,0:T(8,128)} async-done(((f32[1024,4096]{1,0:T(8,128)}), f32[32,4096]{1,0:T(8,128)}) %reduce-scatter.24.cloned.1.call-update) | async-done | bytes 524304 | tf_op jit(solution)/shard_map/reduce_scatter | solution.py:292
  (2163 shorter events, 1865.3 us)
Async XLA Ops:
  7.2 68.5 %all-gather.14.cloned.1.call-start = ((), (), s32[]{:S(2)}) async-start(), calls=%async_computation.18 | async-start | bytes 4325376 | tf_op jit(solution)/shard_map/all_gather | solution.py:128
  7.9 840.3 %all-gather.12.cloned.1.call-start = ((), (), s32[]{:S(2)}) async-start(), calls=%async_computation.17 | async-start | bytes 8921088 | tf_op jit(solution)/shard_map/all_gather | solution.py:127
  8.7 882.7 %all-gather.24.cloned.1.call-start = ((), (), s32[]{:S(2)}) async-start(), calls=%async_computation.32 | async-start | bytes 10485760 | tf_op jit(solution)/shard_map/all_gather | solution.py:170
  14.2 182.1 %copy-start.50 = (bf16[1,512,1024]{2,1,0:T(8,128)(2,1)}, bf16[1,512,1024]{2,1,0:T(8,128)(2,1)S(1)}, u32[]{:S(2)}) copy-start(bf16[1,512,1024]{2,1,0:T(8,128)(2,1)S(1)} %get-tuple-element.1107) | copy-start | bytes 3145732
  83.2 821.3 %all-gather.16.cloned.1.call-start = ((), (), s32[]{:S(2)}) async-start(), calls=%async_computation.19 | async-start | bytes 4325376 | tf_op jit(solution)/shard_map/all_gather | solution.py:129
  83.8 827.8 %all-gather.22.cloned.1.call-start = ((), (), s32[]{:S(2)}) async-start(), calls=%async_computation.31 | async-start | bytes 10485760 | tf_op jit(solution)/shard_map/all_gather | solution.py:170
  92.2 842.7 %all-gather.18.cloned.1.call-start = ((), (), s32[]{:S(2)}) async-start(), calls=%async_computation.20 | async-start | bytes 8650752 | tf_op jit(solution)/shard_map/all_gather | solution.py:130
  109.6 103.7 %all-to-all-start = ((bf16[4,2,65536]{2,1,0:T(2,128)(2,1)}), bf16[4,2,65536]{2,1,0:T(2,128)(2,1)}, u32[]{:S(2)}, u32[]{:S(2)}) async-start(bf16[4,2,65536]{2,1,0:T(2,128)(2,1)} %reshape.1442), calls=%async_computation | async-start | bytes 2097152 | tf_op jit(solution)/shard_map/all_to_all | solution.py:139
  113.8 833.0 %all-gather.20.cloned.1.call-start = ((), (), s32[]{:S(2)}) async-start(), calls=%async_computation.21 | async-start | bytes 8650752 | tf_op jit(solution)/shard_map/all_gather | solution.py:131
  115.4 94.7 %copy-start.113 = (f32[256,16]{0,1:T(8,128)}, f32[256,16]{0,1:T(8,128)S(1)}, u32[]{:S(2)}) copy-start(f32[256,16]{0,1:T(8,128)S(1)} %get-tuple-element.1124) | copy-start | bytes 49156
  116.8 66.3 %copy-start.84 = (f32[128,128]{1,0:T(8,128)}, f32[128,128]{1,0:T(8,128)S(1)}, u32[]{:S(2)}) copy-start(f32[128,128]{1,0:T(8,128)S(1)} %fusion.117) | copy-start | bytes 196612
  213.3 30.1 all-to-all-start.2
  512.9 24.9 copy-start.151
  539.4 286.4 %all-to-all-start.3 = ((bf16[4,2,65536]{2,1,0:T(2,128)(2,1)}), bf16[4,2,65536]{2,1,0:T(2,128)(2,1)S(1)}, u32[]{:S(2)}, u32[]{:S(2)}) async-start(bf16[4,2,65536]{2,1,0:T(2,128)(2,1)} %reshape.1440), calls=%async_computation.3 | async-start | bytes 2097152 | tf_op jit(solution)/shard_map/all_to_all | solution.py:147
  805.4 17.0 copy-start
  805.4 17.0 copy-start.150
  825.8 17.7 all-to-all-start.1
  830.1 234.4 %reduce-scatter.14.cloned.1.call-start = ((), (), s32[]{:S(2)}) async-start(), calls=%async_computation.24 | async-start | bytes 655360 | tf_op jit(solution)/shard_map/reduce_scatter | solution.py:229
  830.2 33.9 copy-start.156
  830.2 57.1 %copy-start.166 = (f32[128]{0:T(128)}, f32[128]{0:T(128)S(1)}, u32[]{:S(2)}) copy-start(f32[128]{0:T(128)S(1)} %get-tuple-element.1141) | copy-start | bytes 1540
  830.2 57.1 %copy-start.168 = (f32[128]{0:T(128)}, f32[128]{0:T(128)S(1)}, u32[]{:S(2)}) copy-start(f32[128]{0:T(128)S(1)} %get-tuple-element.1143) | copy-start | bytes 1540
  858.6 25.4 copy-start.58
  864.1 23.2 copy-start.59
  932.8 62.0 %copy-start.129 = (f32[512]{0:T(512)}, f32[512]{0:T(512)S(1)}, u32[]{:S(2)}) copy-start(f32[512]{0:T(512)S(1)} %broadcast_multiply_fusion.6) | copy-start | bytes 6148
  933.1 61.6 %copy-start.137 = (f32[512]{0:T(512)}, f32[512]{0:T(512)S(1)}, u32[]{:S(2)}) copy-start(f32[512]{0:T(512)S(1)} %broadcast_multiply_fusion.8) | copy-start | bytes 6148
  934.8 60.0 %copy-start.131 = (f32[512]{0:T(512)}, f32[512]{0:T(512)S(1)}, u32[]{:S(2)}) copy-start(f32[512]{0:T(512)S(1)} %fusion.137) | copy-start | bytes 6148
  934.8 60.0 %copy-start.148 = (f32[512]{0:T(512)}, f32[512]{0:T(512)S(1)}, u32[]{:S(2)}) copy-start(f32[512]{0:T(512)S(1)} %fusion.135) | copy-start | bytes 6148
  1006.0 89.8 %copy-start.34 = (bf16[512,1024]{1,0:T(8,128)(2,1)}, bf16[512,1024]{1,0:T(8,128)(2,1)S(1)}, u32[]{:S(2)}) copy-start(bf16[512,1024]{1,0:T(8,128)(2,1)S(1)} %get-tuple-element.1101) | copy-start | bytes 3145732
  1027.2 51.3 %reduce-scatter.10.cloned.1.call-start = ((), (), s32[]{:S(2)}) async-start(), calls=%async_computation.22 | async-start | bytes 655360 | tf_op jit(solution)/shard_map/reduce_scatter | solution.py:229
  1050.9 1406.8 %reduce-scatter.16.cloned.1.call-start = ((), (), s32[]{:S(2)}) async-start(), calls=%async_computation.25 | async-start | bytes 10485760 | tf_op jit(solution)/shard_map/reduce_scatter | solution.py:232
  1062.4 16.1 copy-start.157
  1119.2 29.7 all-to-all-start.4
  1149.0 30.2 all-to-all-start.6
  1153.4 1304.3 %reduce-scatter.12.cloned.1.call-start = ((), (), s32[]{:S(2)}) async-start(), calls=%async_computation.23 | async-start | bytes 10485760 | tf_op jit(solution)/shard_map/reduce_scatter | solution.py:232
  1161.2 1540.1 %all-reduce.20.cloned.1.call-start = ((), (), s32[]{:S(2)}) async-start(), calls=%async_computation.33 | async-start | bytes 524288 | tf_op jit(solution)/shard_map/psum | solution.py:295
  1191.7 495.9 %copy-start.86 = (f32[256,16]{0,1:T(8,128)S(1)}, f32[256,16]{0,1:T(8,128)}, u32[]{:S(2)}) copy-start(f32[256,16]{0,1:T(8,128)} %custom-call.5) | copy-start | bytes 49156
  1191.7 495.8 %copy-start.90 = (f32[1,256,16]{1,2,0:T(8,128)S(1)}, f32[1,256,16]{1,2,0:T(8,128)}, u32[]{:S(2)}) copy-start(f32[1,256,16]{1,2,0:T(8,128)} %custom-call.6) | copy-start | bytes 49156
  1687.5 487.0 %copy-start.114 = (f32[256,16]{0,1:T(8,128)S(1)}, f32[256,16]{0,1:T(8,128)}, u32[]{:S(2)}) copy-start(f32[256,16]{0,1:T(8,128)} %copy-done.113) | copy-start | bytes 49156
  2184.1 219.6 %copy-start.23 = (f32[129,256,16]{1,2,0:T(8,128)S(1)}, f32[129,256,16]{1,2,0:T(8,128)}, u32[]{:S(2)}) copy-start(f32[129,256,16]{1,2,0:T(8,128)} %copy-done.22) | copy-start | bytes 6340612
  2184.1 219.6 %copy-start.110 = (f32[256,16]{0,1:T(8,128)S(1)}, f32[256,16]{0,1:T(8,128)}, u32[]{:S(2)}) copy-start(f32[256,16]{0,1:T(8,128)} %copy-done.109) | copy-start | bytes 49156
  2413.8 335.3 %reduce-scatter.22.cloned.1.call-start = ((), (), s32[]{:S(2)}) async-start(), calls=%async_computation.28 | async-start | bytes 8650752 | tf_op jit(solution)/shard_map/reduce_scatter | solution.py:292
  2423.0 528.4 %reduce-scatter.18.cloned.1.call-start = ((), (), s32[]{:S(2)}) async-start(), calls=%async_computation.26 | async-start | bytes 17842176 | tf_op jit(solution)/shard_map/reduce_scatter | solution.py:292
  2457.5 679.1 %reduce-scatter.20.cloned.1.call-start = ((), (), s32[]{:S(2)}) async-start(), calls=%async_computation.27 | async-start | bytes 8650752 | tf_op jit(solution)/shard_map/reduce_scatter | solution.py:292
  2470.7 1027.3 %reduce-scatter.26.cloned.1.call-start = ((), (), s32[]{:S(2)}) async-start(), calls=%async_computation.30 | async-start | bytes 17301504 | tf_op jit(solution)/shard_map/reduce_scatter | solution.py:292
  2499.1 1360.5 %reduce-scatter.24.cloned.1.call-start = ((), (), s32[]{:S(2)}) async-start(), calls=%async_computation.29 | async-start | bytes 17301504 | tf_op jit(solution)/shard_map/reduce_scatter | solution.py:292
  2552.3 44.9 %all-to-all-start.7 = ((bf16[4,2,65536]{2,1,0:T(2,128)(2,1)}), bf16[4,2,65536]{2,1,0:T(2,128)(2,1)S(1)}, u32[]{:S(2)}, u32[]{:S(2)}) async-start(bf16[4,2,65536]{2,1,0:T(2,128)(2,1)} %reshape.1452), calls=%async_computation.11 | async-start | bytes 2097152 | tf_op jit(solution)/shard_map/all_to_all | solution.py:269
  2597.2 30.1 all-to-all-start.5
  2645.8 45.3 %copy-start.136 = (f32[512]{0:T(512)S(1)}, f32[512]{0:T(512)}, u32[]{:S(2)}) copy-start(f32[512]{0:T(512)} %copy-done.135) | copy-start | bytes 6148
  (374 other events, 2753.6 us)
Sparse Core Ops, SparseCore 0:
  10.9 64.7 all-gather.13
  78.6 77.7 all-gather.11
  158.2 97.8 all-gather.23
  258.8 62.0 all-gather.15
  322.6 86.1 all-gather.21
  411.5 77.6 all-gather.17
  492.0 87.4 all-gather.19
  1027.4 22.6 reduce-scatter.13
  1053.7 24.7 reduce-scatter.9
  1081.4 107.8 reduce-scatter.15
  1192.7 86.3 reduce-scatter.11
  2413.9 125.2 all-reduce.19
  2542.1 206.9 reduce-scatter.21
  2755.9 195.4 reduce-scatter.17
  2954.1 182.3 reduce-scatter.19
  3139.3 358.6 reduce-scatter.25
  3500.7 358.9 reduce-scatter.23
where the time goes:
time: 3890 us; the launch traced here: 3870 us
  other arithmetic  1340 us (34%)
  waiting for transfers between devices  1270 us (33%)
  local copies, waits for them, and re-layouts  727 us (19%)
  matrix products  366 us (9%)
  blocking collectives  62.6 us (2%)
  loops' own time  49.4 us (1%)
    reduce_scatter x5, waiting for transfers between devices, on_device(): lax.psum_scatter(weight_sums, ('dp', 'seq'), scatter_dimension=0, tiled=T...  1160 us
    dot_general x64, other arithmetic, advance(): jnp.einsum('tsc,rts,rsc->rtc', toeplitz, same, piece, precision=HIGH_MODE)  513 us
    while x480, local copies, waits for them, and re-layouts  319 us
    scatter-add x2, other arithmetic, ema_blocks(): jnp.take(kernel, jnp.maximum(later - earlier, 0), axis=0)  198 us
    add_any x96, other arithmetic, ema_blocks(): _, outputs = lax.scan(jax.checkpoint(advance), start, (pieces, flag_pieces))  185 us
    dot_general x10, matrix products, transposed(): lax.dot_general(left, right, (((0,), (0,)), ((), ())), preferred_element_...  113 us
    squeeze x160, local copies, waits for them, and re-layouts, ema_blocks(): _, outputs = lax.scan(jax.checkpoint(advance), start, (pieces, flag_pieces))  102 us
    dot_general x10, matrix products, product(): return jnp.dot(left, right, preferred_element_type=jnp.float32)  90.4 us
  transfers between devices with their start and end apart: 25, of which 11 were waited for; matrix products, arithmetic and copies ran while one was open for 53% of the time, Pallas kernels for 0%

commit v1 on v0

v1 whole, which is shorter than its diff:
```python
import functools
import jax
import jax.numpy as jnp
from jax import lax
from jax.experimental import pallas as pl
from jax.experimental.pallas import tpu as pltpu
from jax.sharding import PartitionSpec as P

LANES = 128
EMA_STEP = 16
EMA_WIDTH = 512


def lane(group):
    return slice(group * LANES, (group + 1) * LANES)


def half_of(group, half):
    return (slice(half * 8, half * 8 + 8), lane(group))


def row_of(ref, step, group):
    return ref[group, pl.ds(step, 8, stride=0), :]


def widen(low_ref, wide_ref):
    for group in range(wide_ref.shape[0]):
        wide_ref[group] = low_ref[0, :, lane(group)].astype(jnp.float32)


def fold_rows(part_ref, group):
    halves = []
    for half in range(EMA_STEP // 8):
        base = group * EMA_STEP * 8 + half * 64
        total = part_ref[pl.ds(base, 8, stride=8), :]
        for sub in range(1, 8):
            total = total + part_ref[pl.ds(base + sub, 8, stride=8), :]
        halves.append(total)
    return jnp.concatenate(halves, axis=0)


def ema_last_kernel(reverse, feed_ref, keep_ref, decay_ref, last_ref, feed32):
    length, width = feed_ref.shape[1:]
    groups = width // LANES
    widen(feed_ref, feed32)
    pairs = [(g, h) for g in range(groups) for h in range(2)]

    def body(index, states):
        states = list(states)
        block = (length // EMA_STEP - 1 - index) if reverse else index
        base = pl.multiple_of(block * EMA_STEP, EMA_STEP)
        for offset in range(EMA_STEP):
            step = base + (EMA_STEP - 1 - offset if reverse else offset)
            keep = row_of(keep_ref, step, 0)
            for at, (g, h) in enumerate(pairs):
                feed = row_of(feed32, step, g)
                kept = keep * decay_ref[half_of(g, h)]
                if reverse:
                    states[at] = kept * (states[at] + feed)
                else:
                    states[at] = kept * states[at] + feed
        return tuple(states)

    zero = jnp.zeros((8, LANES), jnp.float32)
    states = lax.fori_loop(0, length // EMA_STEP, body, (zero,) * len(pairs))
    for at, (g, h) in enumerate(pairs):
        last_ref[(0,) + half_of(g, h)] = states[at]


def ema_forward_kernel(feed_ref, keep_ref, decay_ref, gain_ref, start_ref, out_ref, feed32, part_ref):
    length, width = feed_ref.shape[1:]
    groups = width // LANES
    widen(feed_ref, feed32)
    pairs = [(g, h) for g in range(groups) for h in range(2)]

    def body(index, states):
        states = list(states)
        base = pl.multiple_of(index * EMA_STEP, EMA_STEP)
        for offset in range(EMA_STEP):
            keep = row_of(keep_ref, base + offset, 0)
            for g in range(groups):
                feed = row_of(feed32, base + offset, g)
                both = []
                for h in range(2):
                    at = g * 2 + h
                    states[at] = (keep * decay_ref[half_of(g, h)]) * states[at] + feed
                    both.append(gain_ref[half_of(g, h)] * states[at])
                spot = g * EMA_STEP * 8 + offset * 8
                part_ref[spot : spot + 8, :] = both[0] + both[1]
        for g in range(groups):
            out_ref[0, pl.ds(base, EMA_STEP), lane(g)] = fold_rows(part_ref, g).astype(jnp.bfloat16)
        return tuple(states)

    start = tuple(start_ref[(0,) + half_of(g, h)] for g, h in pairs)
    lax.fori_loop(0, length // EMA_STEP, body, start)


def ema_backward_kernel(
    feed_ref, grad_ref, keep_ref, decay_ref, gain_ref, start_ref, end_ref,
    back_ref, gain_grad_ref, decay_grad_ref, feed32, grad32, part_ref, held_ref,
):
    length, width = feed_ref.shape[1:]
    groups = width // LANES
    widen(feed_ref, feed32)
    widen(grad_ref, grad32)
    pairs = [(g, h) for g in range(groups) for h in range(2)]
    blocks = length // EMA_STEP

    def forward(index, states):
        states = list(states)
        base = pl.multiple_of(index * EMA_STEP, EMA_STEP)
        for offset in range(EMA_STEP):
            keep = row_of(keep_ref, base + offset, 0)
            for at, (g, h) in enumerate(pairs):
                kept = keep * states[at]
                held_ref[pl.ds((base + offset) * 16 + h * 8, 8), lane(g)] = kept
                states[at] = decay_ref[half_of(g, h)] * kept + row_of(feed32, base + offset, g)
        return tuple(states)

    start = tuple(start_ref[(0,) + half_of(g, h)] for g, h in pairs)
    lax.fori_loop(0, blocks, forward, start)

    def backward(index, carried):
        pulls, gains, decays = (list(c) for c in carried)
        base = pl.multiple_of((blocks - 1 - index) * EMA_STEP, EMA_STEP)
        for offset in reversed(range(EMA_STEP)):
            step = base + offset
            keep = row_of(keep_ref, step, 0)
            for g in range(groups):
                grad = row_of(grad32, step, g)
                feed = row_of(feed32, step, g)
                both = []
                for h in range(2):
                    at = g * 2 + h
                    local = pulls[at] + grad
                    both.append(gain_ref[half_of(g, h)] * local)
                    gains[at] = gains[at] + local * feed
                    held = held_ref[pl.ds(step * 16 + h * 8, 8), lane(g)]
                    decays[at] = decays[at] + local * held
                    pulls[at] = (keep * decay_ref[half_of(g, h)]) * local
                spot = g * EMA_STEP * 8 + offset * 8
                part_ref[spot : spot + 8, :] = both[0] + both[1]
        for g in range(groups):
            back_ref[0, pl.ds(base, EMA_STEP), lane(g)] = fold_rows(part_ref, g).astype(jnp.bfloat16)
        return (tuple(pulls), tuple(gains), tuple(decays))

    end = tuple(end_ref[(0,) + half_of(g, h)] for g, h in pairs)
    zeros = (jnp.zeros((8, LANES), jnp.float32),) * len(pairs)
    _, gains, decays = lax.fori_loop(0, blocks, backward, (end, zeros, zeros))
    for at, (g, h) in enumerate(pairs):
        gain_grad_ref[(0,) + half_of(g, h)] = gains[at]
        decay_grad_ref[(0,) + half_of(g, h)] = decays[at]


def ema_specs(length, width):
    rows = pl.BlockSpec((1, length, width), lambda r, c: (r, 0, c))
    keep = pl.BlockSpec((1, length, LANES), lambda r, c: (r, 0, 0))
    coef = pl.BlockSpec((16, width), lambda r, c: (0, c))
    state = pl.BlockSpec((1, 16, width), lambda r, c: (r, 0, c))
    return rows, keep, coef, state


def ema_call(kernel, name, ins, outs, args, shapes, scratch, ops):
    rows, length, chans = args[0].shape
    width = min(EMA_WIDTH, chans)
    specs = dict(zip("rkcs", ema_specs(length, width)))
    sizes = {"r": (rows, length, chans), "s": (rows, 16, chans)}
    kinds = {"r": jnp.bfloat16, "s": jnp.float32}
    scratches = [pltpu.VMEM((width // LANES, length, LANES), jnp.float32)] * scratch[0]
    if scratch[1]:
        scratches.append(pltpu.VMEM((width // LANES * EMA_STEP * 8, LANES), jnp.float32))
    if scratch[2]:
        scratches.append(pltpu.VMEM((length * 16, width), jnp.float32))
    return pl.pallas_call(
        kernel,
        out_shape=[jax.ShapeDtypeStruct(sizes[o], kinds[o]) for o in outs],
        grid=(rows, chans // width),
        in_specs=[specs[i] for i in ins],
        out_specs=[specs[o] for o in outs],
        scratch_shapes=scratches,
        compiler_params=pltpu.CompilerParams(vmem_limit_bytes=(40 if scratch[2] else 16) * 2**20),
        cost_estimate=pl.CostEstimate(
            flops=ops * rows * length * chans * 16, bytes_accessed=4 * rows * length * chans, transcendentals=0
        ),
        name=name,
    )(*args)


def ema_last(feed, keep, decay, reverse):
    return ema_call(
        functools.partial(ema_last_kernel, reverse), "ema_back_last" if reverse else "ema_last",
        "rkc", "s", (feed, keep, decay), None, (1, 0, 0), 4)[0]


def ema_forward(feed, keep, decay, gain, start):
    return ema_call(ema_forward_kernel, "ema_forward", "rkccs", "r", (feed, keep, decay, gain, start), None, (1, 1, 0), 6)[0]


def ema_backward(feed, grad, keep, decay, gain, start, end):
    return ema_call(
        ema_backward_kernel, "ema_backward", "rrkccss", "rss",
        (feed, grad, keep, decay, gain, start, end), None, (2, 1, 1), 16)


Z = 128
V = 2048
REACH = 1024
NEG_FILL = -1000000000.0
BOTH = ("dp", "seq")


def layer_norm(values):
    center = values - jnp.mean(values, axis=-1, keepdims=True)
    spread = jnp.mean(center * center, axis=-1, keepdims=True)
    return center * lax.rsqrt(spread + 1e-05)


def scaled_norm(values, gain):
    return layer_norm(values) * gain


def silu_slope(values):
    squash = jax.nn.sigmoid(values)
    return squash * (1.0 + values * (1.0 - squash))


def product(left, right):
    return jnp.dot(left, right, preferred_element_type=jnp.float32)


def against(left, right):
    return lax.dot_general(left, right, (((1,), (1,)), ((), ())), preferred_element_type=jnp.float32)


def transposed(left, right):
    return lax.dot_general(left, right, (((0,), (0,)), ((), ())), preferred_element_type=jnp.float32)


def low(values):
    return values.astype(jnp.bfloat16)


def shift_seq(values, by):
    count = lax.axis_size("seq")
    pairs = [(i, i + by) for i in range(count) if 0 <= i + by < count]
    return lax.ppermute(values, "seq", pairs)


def gather_weight(shard):
    return lax.all_gather(shard, BOTH, axis=0, tiled=True)


def scatter_grad(grad):
    return lax.psum_scatter(low(grad), BOTH, scatter_dimension=0, tiled=True).astype(jnp.float32)


def carried(last, alive, decay_all, forward):
    count = lax.axis_size("seq")
    place = lax.axis_index("seq")
    total = jnp.zeros_like(last)
    through = jnp.ones((last.shape[0], 1, 1), jnp.float32)
    power = None
    for away in range(1, count):
        arrived = shift_seq(last, away if forward else -away)
        factor = through if power is None else through * power
        total = total + factor * arrived
        at = jnp.clip(place - away if forward else place + away, 0, count - 1)
        through = through * lax.dynamic_slice_in_dim(alive, at, 1, 1)[:, :, None]
        power = decay_all if power is None else power * decay_all
    return total


def on_device(
    layer_input,
    cotangent,
    doc_ids,
    resets,
    mix_weight,
    value_weight,
    head_weight,
    expand_weight,
    shrink_weight,
    chan_vectors,
    ema_logits,
    ema_beta_eta,
    z_affine,
):
    seq_count = lax.axis_size("seq")
    seq_place = lax.axis_index("seq")
    rows, places, width = layer_input.shape
    tokens = rows * places
    scale = Z ** (-0.5)
    halo = min(-(-(REACH - 1) // places), seq_count - 1)
    window = (halo + 1) * places

    value_full = gather_weight(value_weight)
    mix_full = gather_weight(mix_weight)
    head_full = gather_weight(head_weight)
    expand_full = gather_weight(expand_weight)
    shrink_full = gather_weight(shrink_weight)

    inputs32 = layer_input.astype(jnp.float32)
    normed, first_pull = jax.vjp(scaled_norm, inputs32, chan_vectors[0])
    normed_low = low(normed)
    normed_parts = [shift_seq(normed_low, by) for by in range(halo, 0, -1)] + [normed_low]
    normed_window = jnp.concatenate(normed_parts, axis=1).reshape(rows * window, width)

    rate = jax.nn.sigmoid(ema_logits[0])
    damping = jax.nn.sigmoid(ema_logits[1])
    decay = (1.0 - rate * damping).T
    weight_in = rate * ema_beta_eta[0]
    weight_out = ema_beta_eta[1]
    gain = (weight_in * weight_out).T
    decay_all = decay
    reach = 1
    while reach < places:
        decay_all = decay_all * decay_all
        reach *= 2
    keep_row = 1.0 - resets.astype(jnp.float32)
    keep_own = lax.dynamic_slice_in_dim(keep_row, seq_place * places, places, 1)
    keep = jnp.broadcast_to(keep_own[:, None, :, None], (rows, 1, places, LANES)).reshape(rows, places, LANES)
    alive = jnp.min(keep_row.reshape(rows, seq_count, places), axis=2)

    last = ema_last(normed_low, keep, decay, False)
    start = carried(last, alive, decay_all, True)
    ema_low = ema_forward(normed_low, keep, decay, gain, start)

    premix = (ema_low.astype(jnp.float32) + chan_vectors[2] * normed).reshape(tokens, width)
    mixed_low = low(jax.nn.silu(premix))
    value_pre = product(normed_window, value_full)
    values_low = low(jax.nn.silu(value_pre)).reshape(rows, window, V)
    projected = product(mixed_low, mix_full)
    shared_pre = projected[:, :Z]
    reset_pre = projected[:, Z : Z + V]
    head_base = projected[:, Z + V : Z + V + width]
    update_pre = projected[:, Z + V + width :]
    shared = jax.nn.silu(shared_pre)
    queries_low = low(shared * z_affine[0] + z_affine[1]).reshape(rows, places, Z)
    keys_low = low(shared * z_affine[2]).reshape(rows, places, Z)
    key_window = jnp.concatenate([shift_seq(keys_low, by) for by in range(halo, 0, -1)] + [keys_low], axis=1)
    reset_gate = jax.nn.silu(reset_pre)
    update_gate = jax.nn.sigmoid(update_pre)

    padded_docs = jnp.pad(doc_ids, ((0, 0), (halo * places, 0)), constant_values=-1)
    key_docs = lax.dynamic_slice_in_dim(padded_docs, seq_place * places, window, 1)
    query_docs = key_docs[:, halo * places :]
    causal = jnp.arange(window)[None, :] <= jnp.arange(places)[:, None] + halo * places
    allowed = causal[None] & (query_docs[:, :, None] == key_docs[:, None, :])
    scores = jnp.einsum("rid,rjd->rij", queries_low, key_window, preferred_element_type=jnp.float32) * scale
    scores = jnp.where(allowed, scores, NEG_FILL)
    peak = jnp.max(scores, axis=-1, keepdims=True)
    expo = jnp.exp(scores - peak)
    total = jnp.sum(expo, axis=-1, keepdims=True)
    probs = expo / total
    probs_low = low(probs)
    attended = jnp.einsum(
        "rij,rjv->riv", probs_low, values_low, preferred_element_type=jnp.float32
    ).reshape(tokens, V)
    gated_low = low(reset_gate * attended)
    head_pre = head_base + product(gated_low, head_full)
    candidate = jax.nn.silu(head_pre)
    residual_in = inputs32.reshape(tokens, width)
    first = residual_in + update_gate * (candidate - residual_in)
    second, second_pull = jax.vjp(scaled_norm, first, chan_vectors[1])
    second_low = low(second)
    expand_pre = product(second_low, expand_full)
    hidden_low = low(jax.nn.silu(expand_pre))
    output = low(first + product(hidden_low, shrink_full)).reshape(rows, places, width)

    cot_low = cotangent.reshape(tokens, width)
    shrink_grad = scatter_grad(transposed(hidden_low, cot_low))
    d_expand = low(against(cot_low, shrink_full) * silu_slope(expand_pre))
    expand_grad = scatter_grad(transposed(second_low, d_expand))
    d_first_norm, d_gain_two = second_pull(against(d_expand, expand_full))
    d_first = cot_low.astype(jnp.float32) + d_first_norm
    d_update = d_first * (candidate - residual_in) * update_gate * (1.0 - update_gate)
    d_direct = d_first * (1.0 - update_gate)
    d_head = d_first * update_gate * silu_slope(head_pre)
    d_head_low = low(d_head)
    head_grad = scatter_grad(transposed(gated_low, d_head_low))
    d_gated = against(d_head_low, head_full)
    d_reset = d_gated * attended * silu_slope(reset_pre)
    d_attended = low(d_gated * reset_gate).reshape(rows, places, V)
    d_probs = jnp.einsum("riv,rjv->rij", d_attended, values_low, preferred_element_type=jnp.float32)
    balance = jnp.sum(probs * d_probs, axis=-1, keepdims=True)
    d_scores = low(probs * (d_probs - balance))
    d_queries = scale * jnp.einsum("rij,rjd->rid", d_scores, key_window, preferred_element_type=jnp.float32)
    key_term = scale * jnp.einsum("rij,rid->rjd", d_scores, queries_low, preferred_element_type=jnp.float32)
    d_keys = key_term[:, halo * places :]
    for by in range(1, halo + 1):
        begin = (halo - by) * places
        d_keys = d_keys + shift_seq(low(key_term[:, begin : begin + places]), -by).astype(jnp.float32)
    d_keys32 = low(d_keys).astype(jnp.float32).reshape(tokens, Z)
    d_values = jnp.einsum("rij,riv->rjv", probs_low, d_attended, preferred_element_type=jnp.float32)
    d_value_pre = low(d_values.reshape(rows * window, V) * silu_slope(value_pre))
    value_grad = scatter_grad(transposed(normed_window, d_value_pre))
    value_term = against(d_value_pre, value_full).reshape(rows, window, width)
    d_normed_value = value_term[:, halo * places :]
    for by in range(1, halo + 1):
        begin = (halo - by) * places
        d_normed_value = d_normed_value + shift_seq(low(value_term[:, begin : begin + places]), -by).astype(jnp.float32)
    d_query_flat = d_queries.reshape(tokens, Z)
    d_shared = d_query_flat * z_affine[0] + d_keys32 * z_affine[2]
    affine_part = jnp.stack(
        [
            jnp.sum(d_query_flat * shared, axis=0),
            jnp.sum(d_query_flat, axis=0),
            jnp.sum(d_keys32 * shared, axis=0),
        ]
    )
    d_projected = low(
        jnp.concatenate([d_shared * silu_slope(shared_pre), d_reset, d_head, d_update], axis=1)
    )
    mix_grad = scatter_grad(transposed(mixed_low, d_projected))
    d_premix = against(d_projected, mix_full) * silu_slope(premix)
    omega_part = jnp.sum(d_premix * normed.reshape(tokens, width), axis=0)
    d_premix = d_premix.reshape(rows, places, width)
    d_ema = low(d_premix)
    back_last = ema_last(d_ema, keep, decay, True)
    end = carried(back_last, alive, decay_all, False)
    d_feed, gain_parts, decay_parts = ema_backward(normed_low, d_ema, keep, decay, gain, start, end)
    d_normed = d_premix * chan_vectors[2] + d_normed_value + d_feed.astype(jnp.float32)
    d_input_norm, d_gain_one = first_pull(d_normed)
    x_grad = d_direct.reshape(rows, places, width) + d_input_norm

    chan_grad, gain_sum, decay_sum, affine_grad = lax.psum(
        (
            jnp.stack([d_gain_one, d_gain_two, omega_part]),
            jnp.sum(gain_parts, axis=0),
            jnp.sum(decay_parts, axis=0),
            affine_part,
        ),
        BOTH,
    )
    d_gain = gain_sum.T
    d_decay = (decay_sum * gain).T
    d_weight_in = d_gain * weight_out
    coef_grad = jnp.stack([d_weight_in * rate, d_gain * weight_in])
    d_rate = d_weight_in * ema_beta_eta[0] - d_decay * damping
    d_damping = -d_decay * rate
    logits_grad = jnp.stack([d_rate * rate * (1.0 - rate), d_damping * damping * (1.0 - damping)])
    return (
        output,
        x_grad,
        mix_grad,
        value_grad,
        head_grad,
        expand_grad,
        shrink_grad,
        chan_grad,
        logits_grad,
        coef_grad,
        affine_grad,
    )


def solution(mesh):
    placed = (
        P("dp", "seq", None),
        P("dp", "seq", None),
        P("dp", None),
        P("dp", None),
        P(BOTH, None),
        P(BOTH, None),
        P(BOTH, None),
        P(BOTH, None),
        P(BOTH, None),
        P(),
        P(),
        P(),
        P(),
    )
    return jax.shard_map(
        on_device,
        mesh=mesh,
        in_specs=placed,
        out_specs=(
            P("dp", "seq", None),
            P("dp", "seq", None),
            P(BOTH, None),
            P(BOTH, None),
            P(BOTH, None),
            P(BOTH, None),
            P(BOTH, None),
            P(),
            P(),
            P(),
            P(),
        ),
        check_vma=False,
    )
```

time: 3890 us -> 1570 us (0.40)
  other arithmetic: 1340 us -> 97.5 us
  local copies, waits for them, and re-layouts: 727 us -> 28.1 us
  waiting for transfers between devices: 1270 us -> 939 us
  Pallas kernels: 0 us -> 69.2 us
  matrix products: 366 us -> 298 us
  loops' own time: 49.4 us -> 0 us
    dot_general x226 -> x0, other arithmetic: 621 us -> none  [the longest x64 513 us: advance(): jnp.einsum('tsc,rts,rsc->rtc', toeplitz, same, piece, precision=HIGH_MODE)]
    reduce_scatter x9 -> x5, waiting for transfers between devices: 1170 us -> 601 us  [scatter_grad(): lax.psum_scatter(low(grad), BOTH, scatter_dimension=0, tiled=True)]
    while x480 -> x0, local copies, waits for them, and re-layouts: 319 us -> none
    scatter-add x2 -> x0, other arithmetic: 198 us -> none  [ema_blocks(): jnp.take(kernel, jnp.maximum(later - earlier, 0), axis=0)]
    add_any x128 -> x0, other arithmetic: 186 us -> none  [the longest x96 185 us: ema_blocks(): _, outputs = lax.scan(jax.checkpoint(advance), start, (pieces, flag_pieces))]
    ppermute x0 -> x14, waiting for transfers between devices: none -> 170 us  [shift_seq(): return lax.ppermute(values, 'seq', pairs)]
    all_gather x7 -> x5, waiting for transfers between devices: 61.5 us -> 166 us  [gather_weight(): return lax.all_gather(shard, BOTH, axis=0, tiled=True)]
    squeeze x161 -> x0, local copies, waits for them, and re-layouts: 104 us -> none  [the longest x160 102 us: ema_blocks(): _, outputs = lax.scan(jax.checkpoint(advance), start, (pieces, flag_pieces))]
  transfers between devices with their start and end apart: 25 -> 25, of which waited for: 11 -> 17; matrix products, arithmetic and copies ran while one was open for 53% -> 19% of each run, Pallas kernels for 0% -> 1%
where the time goes in v1:
time: 1570 us; the launch traced here: 1560 us
  waiting for transfers between devices  939 us (60%)
  matrix products  298 us (19%)
  other arithmetic  97.5 us (6%)
  blocking collectives  77.8 us (5%)
  Pallas kernels  69.2 us (4%)
  starting transfers between devices  32.9 us (2%)
  local copies, waits for them, and re-layouts  28.1 us (2%)
    reduce_scatter x5, waiting for transfers between devices, scatter_grad(): lax.psum_scatter(low(grad), BOTH, scatter_dimension=0, tiled=True)  601 us
    ppermute x14, waiting for transfers between devices, shift_seq(): return lax.ppermute(values, 'seq', pairs)  170 us
    all_gather x5, waiting for transfers between devices, gather_weight(): return lax.all_gather(shard, BOTH, axis=0, tiled=True)  166 us
    dot_general x5, matrix products, product(): return jnp.dot(left, right, preferred_element_type=jnp.float32)  87.2 us
    dot_general x5, matrix products, against(): lax.dot_general(left, right, (((1,), (1,)), ((), ())), preferred_element_...  86 us
    psum x1, blocking collectives, on_device(): lax.psum((jnp.stack([d_gain_one, d_gain_two, omega_part]), jnp.sum(gain_p...  77.8 us
    dot_general x5, matrix products, transposed(): lax.dot_general(left, right, (((0,), (0,)), ((), ())), preferred_element_...  69.9 us
    pallas_call x4, Pallas kernels, ema_call(): pl.pallas_call(kernel, out_shape=[jax.ShapeDtypeStruct(sizes[o], kinds[o]...  69.2 us
  transfers between devices with their start and end apart: 25, of which 17 were waited for; matrix products, arithmetic and copies ran while one was open for 19% of the time, Pallas kernels for 1%

profile of v1, /device:TPU:0, one launch (start us, length us, event | category | flops | bytes accessed | tf_op | source)
XLA Modules:
  0.0 1557.4 jit_solution(3728227886427581187)
XLA Ops:
  15.3 7.4 ema_last.1
  22.7 5.8 collective-permute-start.2
  47.3 15.2 ema_forward.1
  68.9 18.5 %collective-permute-done.6 = bf16[2,512,1024]{2,1,0:T(8,128)(2,1)} collective-permute-done((bf16[2,512,1024]{2,1,0:T(8,128)(2,1)S(1)}, bf16[2,512,1024]{2,1,0:T(8,128)(2,1)}, u32[]{:S(2)}, u32[]{:S(2)}) %collective-permute-start.6) | collective-permute-done | bytes 2097184 | tf_op jit(solution)/shard_map/ppermute | solution.py:246
  87.4 57.1 %collective-permute-done.5 = bf16[2,512,1024]{2,1,0:T(8,128)(2,1)} collective-permute-done((bf16[2,512,1024]{2,1,0:T(8,128)(2,1)S(1)}, bf16[2,512,1024]{2,1,0:T(8,128)(2,1)}, u32[]{:S(2)}, u32[]{:S(2)}) %collective-permute-start.5) | collective-permute-done | bytes 2097184 | tf_op jit(solution)/shard_map/ppermute | solution.py:246
  144.6 5.4 pad_maximum_fusion.1
  150.0 13.3 fusion.85
  163.3 5.9 copy-done.16
  171.5 5.4 collective-permute-start.3
  176.9 36.4 %all-gather.8.cloned.1.call-done = bf16[1024,2048]{1,0:T(8,128)(2,1)} async-done(((bf16[32,2048]{1,0:T(8,128)(2,1)}), bf16[1024,2048]{1,0:T(8,128)(2,1)}) %all-gather.8.cloned.1.call-update) | async-done | bytes 4194320 | tf_op jit(solution)/shard_map/all_gather | solution.py:250
  213.3 25.4 %multiply_convert_fusion = (bf16[3072,2048]{1,0:T(8,128)(2,1)}, f32[3072,2048]{1,0:T(8,128)}) fusion(bf16[3072,1024]{1,0:T(8,128)(2,1)} %bitcast.212, bf16[1024,2048]{1,0:T(8,128)(2,1)} %all-gather.8.cloned.1.call-done), kind=kOutput, calls=%fused_computation.3 | convolution fusion | flops 12916359168 | bytes 48234496 | tf_op jit(solution)/shard_map/dot_general | solution.py:228
  238.7 6.6 fusion.82
  245.3 14.7 fusion.38
  260.1 8.9 fusion.2
  269.0 7.9 all-gather.10.cloned.1.call-done
  276.8 13.9 fusion.77
  293.3 62.3 %all-gather.12.cloned.1.call-done = bf16[1024,4096]{1,0:T(8,128)(2,1)} async-done(((bf16[32,4096]{1,0:T(8,128)(2,1)}), bf16[1024,4096]{1,0:T(8,128)(2,1)}) %all-gather.12.cloned.1.call-update) | async-done | bytes 8388624 | tf_op jit(solution)/shard_map/all_gather | solution.py:250
  355.6 19.8 %multiply_convert_fusion.2 = (bf16[1024,4096]{1,0:T(8,128)(2,1)}, f32[1024,4096]{1,0:T(8,128)}) fusion(bf16[1024,4096]{1,0:T(8,128)(2,1)} %all-gather.12.cloned.1.call-done, f32[1024,1024]{1,0:T(8,128)} %copy-done.11, f32[1024]{0:T(1024)S(1)} %bitcast.237, f32[1024]{0:T(1024)S(1)} %fusion.63, f32[1024]{0:T(1024)S(1)} %broadcast_multiply_fusion), kind=kOutput, calls=%fused_computation.6 | convolution fusion | flops 8615100416 | bytes 37761024 | tf_op jit(solution)/shard_map/dot_general | solution.py:228
  375.4 59.1 %all-gather.14.cloned.1.call-done = bf16[4096,1024]{1,0:T(8,128)(2,1)} async-done(((bf16[128,1024]{1,0:T(8,128)(2,1)}), bf16[4096,1024]{1,0:T(8,128)(2,1)}) %all-gather.14.cloned.1.call-update) | async-done | bytes 8388624 | tf_op jit(solution)/shard_map/all_gather | solution.py:250
  434.5 19.2 %multiply_convert_fusion.1 = bf16[1024,4096]{1,0:T(8,128)(2,1)} fusion(f32[1024,4096]{1,0:T(8,128)} %get-tuple-element.69, bf16[1024,1024]{1,0:T(8,128)(2,1)} %bitcast.216, bf16[4096,1024]{1,0:T(8,128)(2,1)} %all-gather.14.cloned.1.call-done), kind=kOutput, calls=%fused_computation.5 | convolution fusion | flops 8627683328 | bytes 35651584 | tf_op jit(solution)/shard_map/dot_general | solution.py:232
  453.7 16.0 %multiply_reduce_fusion.1 = (f32[1024]{0:T(1024)}, f32[1024]{0:T(1024)S(1)}, f32[1024,1024]{1,0:T(8,128)S(1)}) fusion(f32[1024,1024]{1,0:T(8,128)} %copy-done.11, f32[1024]{0:T(1024)S(1)} %fusion.63, f32[1024]{0:T(1024)S(1)} %broadcast_multiply_fusion, f32[1024]{0:T(1024)S(1)} %bitcast.238, bf16[1024,4096]{1,0:T(8,128)(2,1)} %multiply_convert_fusion.1, ...), kind=kOutput, calls=%fused_computation.62 | convolution fusion | flops 8597272576 | bytes 25186304 | tf_op jit(solution)/shard_map/dot_general | solution.py:232
  472.5 8.2 multiply_convert_fusion.6
  480.7 13.4 multiply_convert_fusion.3
  494.1 14.2 multiply_reduce_fusion
  508.2 5.2 multiply_convert_fusion.4
  520.1 5.1 collective-permute-done.7
  530.3 18.3 %fusion.13 = (f32[1024]{0:T(1024)}, f32[1024,1024]{1,0:T(8,128)}) fusion(f32[2,512,1024]{2,1,0:T(8,128)} %get-tuple-element.49, f32[2,512,1024]{2,1,0:T(8,128)} %copy-done.14, bf16[1024,4224]{1,0:T(8,128)(2,1)} %all-gather.6.cloned.1.call-done, bf16[1024,1024]{1,0:T(8,128)(2,1)} %get-tuple-element.40, bf16[1024,1024]{1,0:T(8,128)(2,1)} %copy-done.20, ...), kind=kOutput, calls=%fused_computation.38 | convolution fusion | flops 8903457792 | bytes 29888512 | tf_op jit(solution)/shard_map/dot_general | solution.py:232
  551.1 7.6 ema_back_last.1
  562.7 5.9 collective-permute-done.13
  572.2 39.0 %ema_backward.1 = (bf16[2,512,1024]{2,1,0:T(8,128)(2,1)S(1)}, f32[2,16,1024]{2,1,0:T(8,128)S(1)}, f32[2,16,1024]{2,1,0:T(8,128)S(1)}) custom-call(bf16[2,512,1024]{2,1,0:T(8,128)(2,1)S(1)} %fusion.42.feed_ref, bf16[2,512,1024]{2,1,0:T(8,128)(2,1)S(1)} %bitcast_convert_fusion.feed_ref.grad_ref, f32[2,512,128]{2,1,0:T(8,128)S(1)} %reshape.214.keep_ref, ...), custom_call_target="tpu_custom_call" | custom-call | flops 268435456 | bytes 4194304 | tf_op jit(solution)/shard_map/ema_backward/pallas_call | solution.py:174
  614.1 9.4 convolution_convert_fusion.4
  624.1 15.4 fusion.36
  639.5 17.8 %fusion.1 = bf16[3072,2048]{1,0:T(8,128)(2,1)S(1)} fusion(f32[2,1536,2048]{2,1,0:T(8,128)} %fusion.36, f32[3072,2048]{1,0:T(8,128)} %get-tuple-element.64), kind=kLoop, calls=%fused_computation.2 | loop fusion | flops 56623104 | bytes 62914560 | tf_op jit(solution)/shard_map/convert_element_type | solution.py:240
  661.9 15.4 convolution_convert_fusion.3
  678.8 14.8 convolution_convert_fusion
  694.4 15.7 %convolution_convert_fusion.2 = bf16[1024,4096]{1,0:T(8,128)(2,1)} fusion(bf16[1024,4096]{1,0:T(8,128)(2,1)} %multiply_convert_fusion.1, f32[1024,1024]{1,0:T(8,128)} %copy-done.11, f32[1024]{0:T(1024)S(1)} %bitcast.240, f32[1024]{0:T(1024)S(1)} %copy-done.49, f32[1024]{0:T(1024)S(1)} %copy-done.47), kind=kOutput, calls=%fused_computation.19 | convolution fusion | flops 8598323200 | bytes 20983808 | tf_op jit(solution)/shard_map/dot_general | solution.py:236
  711.6 14.6 convolution_convert_fusion.1
  726.3 19.2 %fusion.86 = f32[3072,1024]{1,0:T(8,128)} fusion(bf16[3072,2048]{1,0:T(8,128)(2,1)} %copy-done.15, bf16[1024,2048]{1,0:T(8,128)(2,1)} %all-gather.8.cloned.1.call-done), kind=kOutput, calls=%fused_computation.183 | convolution fusion | flops 12884901888 | bytes 29360128 | tf_op jit(solution)/shard_map/dot_general | solution.py:232
  745.5 5.6 convert.23
  756.6 14.9 add_convert_fusion
  773.2 76.0 %collective-permute-done.9 = bf16[2,512,1024]{2,1,0:T(8,128)(2,1)} collective-permute-done((bf16[2,512,1024]{2,1,0:T(8,128)(2,1)}, bf16[2,512,1024]{2,1,0:T(8,128)(2,1)}, u32[]{:S(2)}, u32[]{:S(2)}) %collective-permute-start.9) | collective-permute-done | bytes 2097184 | tf_op jit(solution)/shard_map/ppermute | solution.py:246
  849.3 6.5 fusion.29
  858.1 77.8 %all-reduce.1 = (f32[3,1024]{1,0:T(4,128)}, f32[3,128]{1,0:T(4,128)}) all-reduce(f32[3,1024]{1,0:T(4,128)S(1)} %pad_maximum_fusion.7, f32[3,128]{1,0:T(4,128)S(1)} %pad_maximum_fusion.8), channel_id=1, replica_groups=mesh['dp'=8,'seq'=4] {'dp','seq'}, use_global_device_ids=true, to_apply=%region_20.21 | all-reduce | flops 3456 | bytes 27648 | tf_op jit(solution)/shard_map/psum | solution.py:426
  935.9 5.6 add_add_fusion.2
  943.1 98.4 %reduce-scatter.8.cloned.1.call-done = bf16[32,2048]{1,0:T(8,128)(2,1)} async-done(((bf16[1024,2048]{1,0:T(8,128)(2,1)}), bf16[32,2048]{1,0:T(8,128)(2,1)}) %reduce-scatter.8.cloned.1.call-update) | async-done | bytes 131088 | tf_op jit(solution)/shard_map/reduce_scatter | solution.py:254
  1043.1 134.2 %reduce-scatter.6.cloned.1.call-done = bf16[32,4224]{1,0:T(8,128)(2,1)} async-done(((bf16[1024,4224]{1,0:T(8,128)(2,1)}), bf16[32,4224]{1,0:T(8,128)(2,1)}) %reduce-scatter.6.cloned.1.call-update) | async-done | bytes 270352 | tf_op jit(solution)/shard_map/reduce_scatter | solution.py:254
  1179.1 182.9 %reduce-scatter.12.cloned.1.call-done = bf16[32,4096]{1,0:T(8,128)(2,1)} async-done(((bf16[1024,4096]{1,0:T(8,128)(2,1)}), bf16[32,4096]{1,0:T(8,128)(2,1)}) %reduce-scatter.12.cloned.1.call-update) | async-done | bytes 262160 | tf_op jit(solution)/shard_map/reduce_scatter | solution.py:254
  1363.8 185.1 %reduce-scatter.14.cloned.1.call-done = bf16[128,1024]{1,0:T(8,128)(2,1)} async-done(((bf16[4096,1024]{1,0:T(8,128)(2,1)}), bf16[128,1024]{1,0:T(8,128)(2,1)}) %reduce-scatter.14.cloned.1.call-update) | async-done | bytes 262160 | tf_op jit(solution)/shard_map/reduce_scatter | solution.py:254
  (251 shorter events, 92.3 us)
Async XLA Ops:
  7.2 142.8 %all-gather.6.cloned.1.call-start = ((), (), s32[]{:S(2)}) async-start(), calls=%async_computation.5 | async-start | bytes 8921088 | tf_op jit(solution)/shard_map/all_gather | solution.py:250
  7.9 205.4 %all-gather.8.cloned.1.call-start = ((), (), s32[]{:S(2)}) async-start(), calls=%async_computation.6 | async-start | bytes 4325376 | tf_op jit(solution)/shard_map/all_gather | solution.py:250
  8.7 268.1 %all-gather.10.cloned.1.call-start = ((), (), s32[]{:S(2)}) async-start(), calls=%async_computation.7 | async-start | bytes 4325376 | tf_op jit(solution)/shard_map/all_gather | solution.py:250
  9.4 346.1 %all-gather.12.cloned.1.call-start = ((), (), s32[]{:S(2)}) async-start(), calls=%async_computation.8 | async-start | bytes 8650752 | tf_op jit(solution)/shard_map/all_gather | solution.py:250
  10.0 424.5 %all-gather.14.cloned.1.call-start = ((), (), s32[]{:S(2)}) async-start(), calls=%async_computation.9 | async-start | bytes 8650752 | tf_op jit(solution)/shard_map/all_gather | solution.py:250
  12.9 50.2 %copy-start.34 = (f32[2,512]{1,0:T(2,128)}, f32[2,512]{1,0:T(2,128)S(1)}, u32[]{:S(2)}) copy-start(f32[2,512]{1,0:T(2,128)S(1)} %broadcast_multiply_fusion.1) | copy-start | bytes 12292
  13.7 49.5 %copy-start.38 = (f32[2,512]{1,0:T(2,128)}, f32[2,512]{1,0:T(2,128)S(1)}, u32[]{:S(2)}) copy-start(f32[2,512]{1,0:T(2,128)S(1)} %fusion.64) | copy-start | bytes 12292
  14.3 48.8 %copy-start.36 = (f32[1,1024]{1,0:T(1,128)}, f32[1,1024]{1,0:T(1,128)S(1)}, u32[]{:S(2)}) copy-start(f32[1,1024]{1,0:T(1,128)S(1)} %get-tuple-element.58) | copy-start | bytes 12292
  14.3 48.9 %copy-start.42 = (f32[1,1024]{1,0:T(1,128)}, f32[1,1024]{1,0:T(1,128)S(1)}, u32[]{:S(2)}) copy-start(f32[1,1024]{1,0:T(1,128)S(1)} %get-tuple-element.59) | copy-start | bytes 12292
  14.3 31.9 %copy-start.27 = (f32[16,1024]{1,0:T(8,128)}, f32[16,1024]{1,0:T(8,128)S(1)}, u32[]{:S(2)}) copy-start(f32[16,1024]{1,0:T(8,128)S(1)} %get-tuple-element.37) | copy-start | bytes 196612
  14.4 25.4 %copy-start.41 = (s32[2,2048]{1,0:T(2,128)S(1)}, s32[2,2048]{1,0:T(2,128)}, u32[]{:S(2)}) copy-start(s32[2,2048]{1,0:T(2,128)} %param.15) | copy-start | bytes 49156
  14.4 26.0 %copy-start.29 = (f32[2,1024,16]{1,2,0:T(8,128)S(1)}, f32[2,1024,16]{1,2,0:T(8,128)}, u32[]{:S(2)}) copy-start(f32[2,1024,16]{1,2,0:T(8,128)} %param.24) | copy-start | bytes 393220
  22.7 22.0 %collective-permute-start.2 = (f32[2,16,1024]{2,1,0:T(8,128)S(1)}, f32[2,16,1024]{2,1,0:T(8,128)S(1)}, u32[]{:S(2)}, u32[]{:S(2)}) collective-permute-start(f32[2,16,1024]{2,1,0:T(8,128)S(1)} %ema_last.1), channel_id=1, source_target_pairs={{0,3},{4,7},{8,11},{12,15},{16,19},{20,23},{24,27},{28,31}} | collective-permute-start | bytes 393224 | tf_op jit(solution)/shard_map/ppermute | solution.py:246
  28.5 17.7 %collective-permute-start.1 = (f32[2,16,1024]{2,1,0:T(8,128)S(1)}, f32[2,16,1024]{2,1,0:T(8,128)S(1)}, u32[]{:S(2)}, u32[]{:S(2)}) collective-permute-start(f32[2,16,1024]{2,1,0:T(8,128)S(1)} %ema_last.1), channel_id=1, source_target_pairs={{0,2},{1,3},{4,6},{5,7},{8,10},{9,11},{12,14},{13,15},{16,18},{17,... | collective-permute-start | bytes 393224 | tf_op jit(solution)/shard_map/ppermute | solution.py:246
  29.8 16.4 %collective-permute-start = (f32[2,16,1024]{2,1,0:T(8,128)S(1)}, f32[2,16,1024]{2,1,0:T(8,128)}, u32[]{:S(2)}, u32[]{:S(2)}) collective-permute-start(f32[2,16,1024]{2,1,0:T(8,128)S(1)} %ema_last.1), channel_id=1, source_target_pairs={{0,1},{1,2},{2,3},{4,5},{5,6},{6,7},{8,9},{9,10},{10,11},{12,13},{... | collective-permute-start | bytes 393224 | tf_op jit(solution)/shard_map/ppermute | solution.py:246
  33.0 54.5 %collective-permute-start.6 = (bf16[2,512,1024]{2,1,0:T(8,128)(2,1)S(1)}, bf16[2,512,1024]{2,1,0:T(8,128)(2,1)}, u32[]{:S(2)}, u32[]{:S(2)}) collective-permute-start(bf16[2,512,1024]{2,1,0:T(8,128)(2,1)S(1)} %fusion.42.feed_ref), channel_id=1, source_target_pairs={{0,1},{1,2},{2,3},{4,5},{5,6},{6,7},{8,9},{9,10},{10,11},{12,13},{... | collective-permute-start | bytes 6291464 | tf_op jit(solution)/shard_map/ppermute | solution.py:246
  35.6 109.0 %collective-permute-start.5 = (bf16[2,512,1024]{2,1,0:T(8,128)(2,1)S(1)}, bf16[2,512,1024]{2,1,0:T(8,128)(2,1)}, u32[]{:S(2)}, u32[]{:S(2)}) collective-permute-start(bf16[2,512,1024]{2,1,0:T(8,128)(2,1)S(1)} %fusion.42.feed_ref), channel_id=1, source_target_pairs={{0,2},{1,3},{4,6},{5,7},{8,10},{9,11},{12,14},{13,15},{16,18},{17,... | collective-permute-start | bytes 6291464 | tf_op jit(solution)/shard_map/ppermute | solution.py:246
  38.3 733.3 %all-reduce.5.cloned.1.call-start = ((), (), s32[]{:S(2)}) async-start(), calls=%async_computation.15 | async-start | bytes 262144 | tf_op jit(solution)/shard_map/psum | solution.py:426
  38.4 27.9 %copy-start.25 = (f32[16,1024]{1,0:T(8,128)}, f32[16,1024]{1,0:T(8,128)S(1)}, u32[]{:S(2)}) copy-start(f32[16,1024]{1,0:T(8,128)S(1)} %fusion.73) | copy-start | bytes 196612
  66.3 78.3 %copy-start.14 = (f32[2,512,1024]{2,1,0:T(8,128)}, f32[2,512,1024]{2,1,0:T(8,128)S(1)}, u32[]{:S(2)}) copy-start(f32[2,512,1024]{2,1,0:T(8,128)S(1)} %get-tuple-element.50) | copy-start | bytes 12582916
  169.5 75.8 %copy-start.21 = (bf16[1024,128]{1,0:T(8,128)(2,1)}, bf16[1024,128]{1,0:T(8,128)(2,1)S(1)}, u32[]{:S(2)}) copy-start(bf16[1024,128]{1,0:T(8,128)(2,1)S(1)} %get-tuple-element.46) | copy-start | bytes 786436
  169.5 75.8 %copy-start.31 = (bf16[1024,128]{1,0:T(8,128)(2,1)}, bf16[1024,128]{1,0:T(8,128)(2,1)S(1)}, u32[]{:S(2)}) copy-start(bf16[1024,128]{1,0:T(8,128)(2,1)S(1)} %get-tuple-element.45) | copy-start | bytes 786436
  169.5 69.2 %collective-permute-start.4 = (bf16[2,512,128]{2,1,0:T(8,128)(2,1)S(1)}, bf16[2,512,128]{2,1,0:T(8,128)(2,1)}, u32[]{:S(2)}, u32[]{:S(2)}) collective-permute-start(bf16[2,512,128]{2,1,0:T(8,128)(2,1)S(1)} %bitcast.222), channel_id=1, source_target_pairs={{0,1},{1,2},{2,3},{4,5},{5,6},{6,7},{8,9},{9,10},{10,11},{12,13},{... | collective-permute-start | bytes 786440 | tf_op jit(solution)/shard_map/ppermute | solution.py:246
  171.5 67.2 %collective-permute-start.3 = (bf16[2,512,128]{2,1,0:T(8,128)(2,1)S(1)}, bf16[2,512,128]{2,1,0:T(8,128)(2,1)}, u32[]{:S(2)}, u32[]{:S(2)}) collective-permute-start(bf16[2,512,128]{2,1,0:T(8,128)(2,1)S(1)} %bitcast.223), channel_id=1, source_target_pairs={{0,2},{1,3},{4,6},{5,7},{8,10},{9,11},{12,14},{13,15},{16,18},{17,... | collective-permute-start | bytes 786440 | tf_op jit(solution)/shard_map/ppermute | solution.py:246
  213.3 25.4 %copy-start.52 = (s32[2,1536]{1,0:T(2,128)S(1)}, s32[2,1536]{1,0:T(2,128)}, u32[]{:S(2)}) copy-start(s32[2,1536]{1,0:T(2,128)} %pad_dynamic-slice_fusion.1) | copy-start | bytes 36868
  213.3 25.4 %copy-start.63 = (s32[2,512]{1,0:T(2,128)S(1)}, s32[2,512]{1,0:T(2,128)}, u32[]{:S(2)}) copy-start(s32[2,512]{1,0:T(2,128)} %pad_dynamic-slice_fusion) | copy-start | bytes 12292
  290.7 64.9 %copy-start.50 = (f32[1,1024]{1,0:T(1,128)S(1)}, f32[1,1024]{1,0:T(1,128)}, u32[]{:S(2)}) copy-start(f32[1,1024]{1,0:T(1,128)} %get-tuple-element.57) | copy-start | bytes 12292
  290.7 178.9 %copy-start.46 = (f32[1024]{0:T(1024)}, f32[1024]{0:T(1024)S(1)}, u32[]{:S(2)}) copy-start(f32[1024]{0:T(1024)S(1)} %broadcast_multiply_fusion) | copy-start | bytes 12292
  293.3 176.4 %copy-start.48 = (f32[1024]{0:T(1024)}, f32[1024]{0:T(1024)S(1)}, u32[]{:S(2)}) copy-start(f32[1024]{0:T(1024)S(1)} %fusion.63) | copy-start | bytes 12292
  514.9 10.4 collective-permute-start.7
  516.2 11.2 collective-permute-start.8
  548.6 23.6 %copy-start.3 = (f32[2,16,1024]{2,1,0:T(8,128)S(1)}, f32[2,16,1024]{2,1,0:T(8,128)}, u32[]{:S(2)}) copy-start(f32[2,16,1024]{2,1,0:T(8,128)} %copy-done.2) | copy-start | bytes 393220
  558.8 9.8 collective-permute-start.13
  560.1 9.7 collective-permute-start.12
  561.4 10.7 collective-permute-start.11
  613.8 327.6 %reduce-scatter.10.cloned.1.call-start = ((), (), s32[]{:S(2)}) async-start(), calls=%async_computation.12 | async-start | bytes 4325376 | tf_op jit(solution)/shard_map/reduce_scatter | solution.py:254
  623.5 418.0 %reduce-scatter.8.cloned.1.call-start = ((), (), s32[]{:S(2)}) async-start(), calls=%async_computation.11 | async-start | bytes 4325376 | tf_op jit(solution)/shard_map/reduce_scatter | solution.py:254
  624.1 37.7 %slice-start.2 = ((s8[6291456]{0:T(1024)(128)(4,1)}), s8[2097152]{0:T(1024)(128)(4,1)S(1)}, s32[]{:S(2)}) async-start(s8[6291456]{0:T(1024)(128)(4,1)} %bitcast.213), calls=%async_computation.18 | async-start | bytes 4194304
  677.3 500.1 %reduce-scatter.6.cloned.1.call-start = ((), (), s32[]{:S(2)}) async-start(), calls=%async_computation.10 | async-start | bytes 8921088 | tf_op jit(solution)/shard_map/reduce_scatter | solution.py:254
  693.7 668.3 %reduce-scatter.12.cloned.1.call-start = ((), (), s32[]{:S(2)}) async-start(), calls=%async_computation.13 | async-start | bytes 8650752 | tf_op jit(solution)/shard_map/reduce_scatter | solution.py:254
  710.1 838.8 %reduce-scatter.14.cloned.1.call-start = ((), (), s32[]{:S(2)}) async-start(), calls=%async_computation.14 | async-start | bytes 8650752 | tf_op jit(solution)/shard_map/reduce_scatter | solution.py:254
  753.6 95.6 %collective-permute-start.9 = (bf16[2,512,1024]{2,1,0:T(8,128)(2,1)}, bf16[2,512,1024]{2,1,0:T(8,128)(2,1)}, u32[]{:S(2)}, u32[]{:S(2)}) collective-permute-start(bf16[2,512,1024]{2,1,0:T(8,128)(2,1)} %get-tuple-element.47), channel_id=1, source_target_pairs={{1,0},{2,1},{3,2},{5,4},{6,5},{7,6},{9,8},{10,9},{11,10},{13,12},{... | collective-permute-start | bytes 6291464 | tf_op jit(solution)/shard_map/ppermute | solution.py:246
  755.1 94.1 %copy-start.1 = (bf16[2,512,1024]{2,1,0:T(8,128)(2,1)S(1)}, bf16[2,512,1024]{2,1,0:T(8,128)(2,1)}, u32[]{:S(2)}) copy-start(bf16[2,512,1024]{2,1,0:T(8,128)(2,1)} %copy-done) | copy-start | bytes 6291460
  755.1 94.1 %copy-start.35 = (f32[2,512]{1,0:T(2,128)S(1)}, f32[2,512]{1,0:T(2,128)}, u32[]{:S(2)}) copy-start(f32[2,512]{1,0:T(2,128)} %copy-done.34) | copy-start | bytes 12292
  755.1 94.1 %copy-start.37 = (f32[1,1024]{1,0:T(1,128)S(1)}, f32[1,1024]{1,0:T(1,128)}, u32[]{:S(2)}) copy-start(f32[1,1024]{1,0:T(1,128)} %copy-done.36) | copy-start | bytes 12292
  755.1 94.1 %copy-start.43 = (f32[1,1024]{1,0:T(1,128)S(1)}, f32[1,1024]{1,0:T(1,128)}, u32[]{:S(2)}) copy-start(f32[1,1024]{1,0:T(1,128)} %copy-done.42) | copy-start | bytes 12292
  755.1 94.1 %collective-permute-start.10 = (bf16[2,512,1024]{2,1,0:T(8,128)(2,1)}, bf16[2,512,1024]{2,1,0:T(8,128)(2,1)}, u32[]{:S(2)}, u32[]{:S(2)}) collective-permute-start(bf16[2,512,1024]{2,1,0:T(8,128)(2,1)} %get-tuple-element.48), channel_id=1, source_target_pairs={{2,0},{3,1},{6,4},{7,5},{10,8},{11,9},{14,12},{15,13},{18,16},{19,... | collective-permute-start | bytes 6291464 | tf_op jit(solution)/shard_map/ppermute | solution.py:246
  855.8 80.1 %copy-start.9 = (bf16[2,512,1024]{2,1,0:T(8,128)(2,1)S(1)}, bf16[2,512,1024]{2,1,0:T(8,128)(2,1)}, u32[]{:S(2)}) copy-start(bf16[2,512,1024]{2,1,0:T(8,128)(2,1)} %param.13) | copy-start | bytes 6291460
  (52 other events, 457.6 us)
Sparse Core Ops, SparseCore 0:
  10.9 121.8 all-gather.5
  135.7 77.5 all-gather.7
  216.2 60.5 all-gather.9
  279.6 75.9 all-gather.11
  358.3 76.1 all-gather.13
  614.0 123.1 all-reduce.4
  739.4 160.9 reduce-scatter.9
  902.7 138.8 reduce-scatter.7
  1047.4 129.8 reduce-scatter.5
  1179.5 182.5 reduce-scatter.11
  1364.3 184.4 reduce-scatter.13

commit v2 on v1

v2 whole, which is shorter than its diff:
```python
import functools
import jax
import jax.numpy as jnp
from jax import lax
from jax.experimental import pallas as pl
from jax.experimental.pallas import tpu as pltpu
from jax.sharding import PartitionSpec as P

Z = 128
V = 2048
REACH = 1024
NEG_FILL = -1000000000.0
BOTH = ("dp", "seq")
MESH = pl.DeviceIdType.MESH
LANES = 128
EMA_STEP = 16
FORWARD_WIDTH = 512
BACKWARD_WIDTH = 256


def lanes_at(base, group):
    return pl.ds(pl.multiple_of(base + group * LANES, LANES), LANES)


def row_of(ref, step, group):
    return ref[group, pl.ds(step, 8, stride=0), :]


def widen(source, row, base, wide):
    for group in range(wide.shape[0]):
        wide[group] = source[row, :, lanes_at(base, group)].astype(jnp.float32)


def halves_of(ref, base, groups, row=None):
    spots = [(slice(h * 8, h * 8 + 8), lanes_at(base, g)) for g in range(groups) for h in range(2)]
    return [ref[spot] if row is None else ref[(row,) + spot] for spot in spots]


def put_halves(ref, base, values, row):
    for at, value in enumerate(values):
        g, h = divmod(at, 2)
        ref[row, h * 8 : h * 8 + 8, lanes_at(base, g)] = value


def add_halves(ref, first, base, values):
    for at, value in enumerate(values):
        g, h = divmod(at, 2)
        spot = (slice(first + h * 8, first + h * 8 + 8), lanes_at(base, g))
        ref[spot] = ref[spot] + value


def fold_rows(part, group):
    halves = []
    for half in range(EMA_STEP // 8):
        base = group * EMA_STEP * 8 + half * 64
        total = part[pl.ds(base, 8, stride=8), :]
        for sub in range(1, 8):
            total = total + part[pl.ds(base + sub, 8, stride=8), :]
        halves.append(total)
    return jnp.concatenate(halves, axis=0).astype(jnp.bfloat16)


def unit_of(index, width, chans):
    across = chans // width
    return lax.div(index, across), pl.multiple_of(lax.rem(index, across) * width, width)


def ema_last(reverse, row, base, feed, keep, decay, last, wide):
    length, groups = feed.shape[1], wide.shape[0]
    widen(feed, row, base, wide)
    decays = halves_of(decay, base, groups)

    def body(index, states):
        states = list(states)
        block = (length // EMA_STEP - 1 - index) if reverse else index
        first = pl.multiple_of(block * EMA_STEP, EMA_STEP)
        for offset in range(EMA_STEP):
            step = first + (EMA_STEP - 1 - offset if reverse else offset)
            kept = row_of(keep, step, row)
            for at in range(2 * groups):
                fed = row_of(wide, step, at // 2)
                if reverse:
                    states[at] = (kept * decays[at]) * (states[at] + fed)
                else:
                    states[at] = (kept * decays[at]) * states[at] + fed
        return tuple(states)

    zero = jnp.zeros((8, LANES), jnp.float32)
    put_halves(last, base, lax.fori_loop(0, length // EMA_STEP, body, (zero,) * (2 * groups)), row)


def ema_forward(row, base, feed, keep, decay, gain, start, out, wide, part):
    length, groups = feed.shape[1], wide.shape[0]
    widen(feed, row, base, wide)
    decays, gains = halves_of(decay, base, groups), halves_of(gain, base, groups)

    def body(index, states):
        states = list(states)
        first = pl.multiple_of(index * EMA_STEP, EMA_STEP)
        for offset in range(EMA_STEP):
            kept = row_of(keep, first + offset, row)
            for g in range(groups):
                fed = row_of(wide, first + offset, g)
                both = []
                for at in (2 * g, 2 * g + 1):
                    states[at] = (kept * decays[at]) * states[at] + fed
                    both.append(gains[at] * states[at])
                spot = g * EMA_STEP * 8 + offset * 8
                part[spot : spot + 8, :] = both[0] + both[1]
        for g in range(groups):
            out[row, pl.ds(first, EMA_STEP), lanes_at(base, g)] = fold_rows(part, g)
        return tuple(states)

    lax.fori_loop(0, length // EMA_STEP, body, tuple(halves_of(start, base, groups, row)))


def ema_backward(row, base, feed, grad, keep, decay, gain, start, end, back, sums, wide, wide_grad, part, held):
    length, groups = feed.shape[1], wide.shape[0]
    widen(feed, row, base, wide)
    widen(grad, row, base, wide_grad)
    decays, gains = halves_of(decay, base, groups), halves_of(gain, base, groups)
    blocks = length // EMA_STEP

    def forward(index, states):
        states = list(states)
        first = pl.multiple_of(index * EMA_STEP, EMA_STEP)
        for offset in range(EMA_STEP):
            kept = row_of(keep, first + offset, row)
            for at in range(2 * groups):
                g, h = divmod(at, 2)
                held[pl.ds((first + offset) * 16 + h * 8, 8), g * LANES : (g + 1) * LANES] = kept * states[at]
                states[at] = (kept * decays[at]) * states[at] + row_of(wide, first + offset, g)
        return tuple(states)

    lax.fori_loop(0, blocks, forward, tuple(halves_of(start, base, groups, row)))

    def backward(index, carried):
        pulls, gain_sums, decay_sums = (list(c) for c in carried)
        first = pl.multiple_of((blocks - 1 - index) * EMA_STEP, EMA_STEP)
        for offset in reversed(range(EMA_STEP)):
            step = first + offset
            kept = row_of(keep, step, row)
            for g in range(groups):
                pulled, fed = row_of(wide_grad, step, g), row_of(wide, step, g)
                both = []
                for h in range(2):
                    at = 2 * g + h
                    local = pulls[at] + pulled
                    both.append(gains[at] * local)
                    gain_sums[at] = gain_sums[at] + local * fed
                    before = held[pl.ds(step * 16 + h * 8, 8), g * LANES : (g + 1) * LANES]
                    decay_sums[at] = decay_sums[at] + local * before
                    pulls[at] = (kept * decays[at]) * local
                spot = g * EMA_STEP * 8 + offset * 8
                part[spot : spot + 8, :] = both[0] + both[1]
        for g in range(groups):
            back[row, pl.ds(first, EMA_STEP), lanes_at(base, g)] = fold_rows(part, g)
        return (tuple(pulls), tuple(gain_sums), tuple(decay_sums))

    zeros = (jnp.zeros((8, LANES), jnp.float32),) * (2 * groups)
    _, gain_sums, decay_sums = lax.fori_loop(
        0, blocks, backward, (tuple(halves_of(end, base, groups, row)), zeros, zeros)
    )
    add_halves(sums, 0, base, gain_sums)
    add_halves(sums, 16, base, decay_sums)


def layer_norm(values):
    center = values - jnp.mean(values, axis=-1, keepdims=True)
    spread = jnp.mean(center * center, axis=-1, keepdims=True)
    return center * lax.rsqrt(spread + 1e-05)


def scaled_norm(values, gain):
    return layer_norm(values) * gain


def silu_slope(values):
    squash = jax.nn.sigmoid(values)
    return squash * (1.0 + values * (1.0 - squash))


def product(left, right):
    return jnp.dot(left, right, preferred_element_type=jnp.float32)


def against(left, right):
    return lax.dot_general(left, right, (((1,), (1,)), ((), ())), preferred_element_type=jnp.float32)


def transposed(left, right):
    return lax.dot_general(left, right, (((0,), (0,)), ((), ())), preferred_element_type=jnp.float32)


def low(values):
    return values.astype(jnp.bfloat16)


def shift_seq(values, by):
    count = lax.axis_size("seq")
    pairs = [(i, i + by) for i in range(count) if 0 <= i + by < count]
    return lax.ppermute(values, "seq", pairs)


def side_of(count):
    side = 1
    while side * side < count:
        side *= 2
    return side


def shape_of():
    depth = lax.axis_size("dp") // 2
    seqs = lax.axis_size("seq")
    down = side_of(seqs)
    return depth, 2, down, seqs // down


def place_of():
    depth, cores, down, across = shape_of()
    dp, seq = lax.axis_index("dp"), lax.axis_index("seq")
    return lax.div(dp, cores), lax.rem(dp, cores), lax.div(seq, across), lax.rem(seq, across)


def peer_of(sizes, spot, axis, by):
    spot = list(spot)
    spot[axis] = lax.rem(spot[axis] + by, sizes[axis])
    return {"dp": spot[0] * sizes[1] + spot[1], "seq": spot[2] * sizes[3] + spot[3]}


def along(count, by):
    return {"dp": lax.axis_index("dp"), "seq": lax.rem(lax.axis_index("seq") + by, count)}


def greet(sizes, spot):
    barrier = pltpu.get_barrier_semaphore()
    seqs = sizes[2] * sizes[3]
    peers = [peer_of(sizes, spot, axis, by) for axis in (0, 1) for by in range(1, sizes[axis])]
    peers += [along(seqs, by) for by in range(1, seqs)]
    for peer in peers:
        pl.semaphore_signal(barrier, inc=1, device_id=peer, device_id_type=MESH)
    pl.semaphore_wait(barrier, len(peers))


def piece_shape(rows, columns):
    return (rows, columns) if rows % 16 == 0 else (rows * columns // LANES, LANES)


def share(total, parts, at):
    return total * at // parts, total * (at + 1) // parts


def spread_edge(seqs, edge, arrived, send, recv, forward):
    return [
        pltpu.make_async_remote_copy(
            src_ref=edge,
            dst_ref=arrived.at[by - 1],
            send_sem=send.at[by - 1],
            recv_sem=recv.at[by - 1],
            device_id=along(seqs, by if forward else seqs - by),
            device_id_type=MESH,
        )
        for by in range(1, seqs)
    ]


def join_edges(arrived, reach, power, entry):
    rows, _, chans = entry.shape

    def body(row, carry):
        for group in range(chans // LANES):
            spot = slice(group * LANES, (group + 1) * LANES)
            total = None
            for at in range(arrived.shape[0]):
                term = reach[at, row] * power[at, :, spot] * arrived[at, row, :, spot]
                total = term if total is None else total + term
            entry[row, :, spot] = total
        return carry

    lax.fori_loop(0, rows, body, 0)


class Halo:
    def __init__(self, count, seqs, feed, window, zero, send, recv, local, hand_send):
        place = lax.axis_index("seq")
        relay = seqs == 4 and count == 2
        self.items = []

        def copy(source, by, towards, sent):
            return pltpu.make_async_remote_copy(
                src_ref=source,
                dst_ref=window.at[:, count - by],
                send_sem=sent,
                recv_sem=recv.at[by - 1],
                device_id=along(seqs, towards),
                device_id_type=MESH,
            )

        for by in range(1, count + 1):
            gives = place + by < seqs
            if relay and by == 1:
                gives = jnp.logical_and(gives, place != 1)
            blank = pltpu.make_async_copy(zero, window.at[:, count - by], local.at[by - 1])
            self.items.append((gives, place >= by, copy(feed, by, by, send.at[by - 1]), blank))
        self.hands = (place == 3, copy(window.at[:, 0], 1, 3, hand_send.at[0])) if relay else None

    def start(self):
        for gives, takes, remote, blank in self.items:
            pl.when(gives)(remote.start)
            pl.when(jnp.logical_not(takes))(blank.start)

    def hand_on(self):
        if self.hands:
            at_hand, hand = self.hands

            @pl.when(at_hand)
            def _():
                self.items[1][2].wait_recv()
                hand.start()

    def wait(self):
        for at, (gives, takes, remote, blank) in enumerate(self.items):
            waits = takes
            if self.hands and at == 1:
                waits = jnp.logical_and(takes, jnp.logical_not(self.hands[0]))
            pl.when(waits)(remote.wait_recv)
            pl.when(jnp.logical_not(takes))(blank.wait)
            pl.when(gives)(remote.wait_send)
        if self.hands:
            pl.when(self.hands[0])(self.hands[1].wait_send)


def gather_kernel(sizes, count, halo, *refs):
    shards, (feed, keep, decay, gain, reach, power) = refs[:count], refs[count : count + 6]
    wholes, (window, entry, out) = refs[count + 6 : 2 * count + 6], refs[2 * count + 6 : 2 * count + 9]
    (
        send_sem, recv_sem, local_sem, edge, arrived, edge_send, edge_recv,
        zero, halo_send, halo_recv, halo_local, hand_send, wide_feed, part,
    ) = refs[2 * count + 9 :]
    rows, length, chans = feed.shape
    width = wide_feed.shape[0] * LANES
    seqs = sizes[2] * sizes[3]
    depth, cores, down, across = sizes
    spot = place_of()
    z, c, a, b = spot
    half = depth // 2
    greet(sizes, spot)
    slots = {}

    def copy(w, kind, source, target, axis, by):
        slot = slots.setdefault(kind, len(slots))
        return pltpu.make_async_remote_copy(
            src_ref=source,
            dst_ref=target,
            send_sem=send_sem.at[w, slot],
            recv_sem=recv_sem.at[w, slot],
            device_id=peer_of(sizes, spot, axis, by),
            device_id_type=MESH,
        )

    def block(w, a_by=0, b_by=0, part=None):
        at = pl.ds(0, depth) if part is None else part
        return wholes[w].at[at, c, lax.rem(a - a_by + down, down), lax.rem(b - b_by + across, across)]

    front, back = pl.ds(0, half), pl.ds(half, depth - half)
    local, line, wide, tall, cross, twin = [], [], [], [], [], []
    for w in range(count):
        own = wholes[w].at[z, c, a, b]
        local.append(pltpu.make_async_copy(shards[w], own, local_sem.at[w]))
        line.append([copy(w, ("z", k), shards[w], own, 0, k) for k in range(1, depth)])
        wide.append([copy(w, ("x", k), block(w), block(w), 3, k) for k in range(1, across)])
        tall.append([copy(w, ("y", l), block(w), block(w), 2, l) for l in range(1, down)])
        pairs = [(k, l) for k in range(1, across) for l in range(1, down)]
        cross.append(
            {
                (k, l): (
                    copy(w, ("f", k, l), block(w, 0, k, front), block(w, 0, k, front), 2, l),
                    copy(w, ("g", k, l), block(w, l, 0, back), block(w, l, 0, back), 3, k),
                )
                for k, l in pairs
            }
        )
        twin.append(
            {
                (l, k): copy(w, ("c", l, k), block(w, l, k), block(w, l, k), 1, 1)
                for l in range(down)
                for k in range(across)
            }
        )
    zero[...] = jnp.zeros_like(zero)
    around = Halo(halo, seqs, feed, window, zero, halo_send, halo_recv, halo_local, hand_send)
    own = pltpu.make_async_copy(feed, window.at[:, halo], local_sem.at[count])
    edges = spread_edge(seqs, edge, arrived, edge_send, edge_recv, True)
    for w in range(count):
        local[w].start()
    for item in line[0]:
        item.start()
    own.start()
    around.start()
    for w in range(1, min(2, count)):
        for item in line[w]:
            item.start()
    units = rows * (chans // width)

    def last_unit(index, carry):
        row, base = unit_of(index, width, chans)
        ema_last(False, row, base, feed, keep, decay, edge, wide_feed)
        return carry

    def forward_unit(index, carry):
        row, base = unit_of(index, width, chans)
        ema_forward(row, base, feed, keep, decay, gain, entry, out, wide_feed, part)
        return carry

    lax.fori_loop(0, units, last_unit, 0)
    for item in edges:
        item.start()
    for step in range(count + 2):
        if step < count:
            w = step
            local[w].wait()
            for item in line[w]:
                item.wait_recv()
            for item in wide[w] + tall[w]:
                item.start()
            twin[w][0, 0].start()
            if w + 2 < count:
                for item in line[w + 2]:
                    item.start()
        if 1 <= step <= count:
            w = step - 1
            for k in range(1, across):
                wide[w][k - 1].wait_recv()
                for l in range(1, down):
                    cross[w][k, l][0].start()
                twin[w][0, k].start()
            for l in range(1, down):
                tall[w][l - 1].wait_recv()
                for k in range(1, across):
                    cross[w][k, l][1].start()
                twin[w][l, 0].start()
        if step >= 2:
            w = step - 2
            for (k, l), both in cross[w].items():
                both[0].wait_recv()
                both[1].wait_recv()
                twin[w][l, k].start()
        if step == 0:
            for item in edges:
                item.wait()
            join_edges(arrived, reach, power, entry)
        if step == 1:
            around.hand_on()
        lax.fori_loop(*share(units, count + 2, step), forward_unit, 0)
    for w in range(count):
        for item in twin[w].values():
            item.wait()
        for item in line[w] + wide[w] + tall[w]:
            item.wait_send()
        for both in cross[w].values():
            both[0].wait_send()
            both[1].wait_send()
    own.wait()
    around.wait()


def vmem(count):
    return [pl.BlockSpec(memory_space=pltpu.VMEM)] * count


def anywhere(count):
    return [pl.BlockSpec(memory_space=pl.ANY)] * count


def gather_weights(shards, feed, keep, decay, gain, reach, power, halo):
    sizes = shape_of()
    depth, cores, down, across = sizes
    seqs = down * across
    count = len(shards)
    pieces = [piece_shape(*shard.shape) for shard in shards]
    slots = (depth - 1) + (across - 1) + (down - 1) + 2 * (across - 1) * (down - 1) + across * down
    rows, length, chans = feed.shape
    state = (rows, 16, chans)
    width = min(FORWARD_WIDTH, chans)
    results = pl.pallas_call(
        functools.partial(gather_kernel, sizes, count, halo),
        out_shape=[jax.ShapeDtypeStruct(sizes + piece, jnp.bfloat16) for piece in pieces]
        + [
            jax.ShapeDtypeStruct((rows, halo + 1, length, chans), jnp.bfloat16),
            jax.ShapeDtypeStruct(state, jnp.float32),
            jax.ShapeDtypeStruct(feed.shape, jnp.bfloat16),
        ],
        in_specs=anywhere(count) + vmem(6),
        out_specs=anywhere(count + 1) + vmem(2),
        scratch_shapes=[
            pltpu.SemaphoreType.DMA((count, slots)),
            pltpu.SemaphoreType.DMA((count, slots)),
            pltpu.SemaphoreType.DMA((count + 1,)),
            pltpu.VMEM(state, jnp.float32),
            pltpu.VMEM((seqs - 1,) + state, jnp.float32),
            pltpu.SemaphoreType.DMA((seqs - 1,)),
            pltpu.SemaphoreType.DMA((seqs - 1,)),
            pltpu.VMEM(feed.shape, jnp.bfloat16),
            pltpu.SemaphoreType.DMA((halo,)),
            pltpu.SemaphoreType.DMA((halo,)),
            pltpu.SemaphoreType.DMA((halo,)),
            pltpu.SemaphoreType.DMA((1,)),
            pltpu.VMEM((width // LANES, length, LANES), jnp.float32),
            pltpu.VMEM((width // LANES * EMA_STEP * 8, LANES), jnp.float32),
        ],
        compiler_params=pltpu.CompilerParams(collective_id=0, has_side_effects=True, vmem_limit_bytes=48 * 2**20),
        name="gather_weights",
    )(*[shard.reshape(piece) for shard, piece in zip(shards, pieces)], feed, keep, decay, gain, reach, power)
    total = depth * cores * down * across
    wholes = [whole.reshape(total * shard.shape[0], shard.shape[1]) for whole, shard in zip(results, shards)]
    return wholes, *results[count:]


def add_rows(target, total, others):
    rows = total.shape[0]
    chunk = 16 if rows % 16 == 0 else rows

    def body(index, carry):
        at = pl.ds(pl.multiple_of(index * chunk, chunk), chunk)
        result = total[at, :].astype(jnp.float32)
        for other in others:
            result = result + other[at, :].astype(jnp.float32)
        target[at, :] = result.astype(target.dtype)
        return carry

    lax.fori_loop(0, rows // chunk, body, 0)


def scatter_kernel(sizes, count, *refs):
    grads, small = refs[:count], refs[count]
    feed, grad, keep, decay, gain, start, reach, power = refs[count + 1 : count + 9]
    refs = refs[count + 9 :]
    outs, (small_out, back_out) = refs[:count], refs[count : count + 2]
    rest = refs[count + 2 :]
    rest, (
        edge, arrived, end, edge_send, edge_recv, wide, wide_grad, part, kept_states,
    ) = rest[:-9], rest[-9:]
    rows, length, chans = feed.shape
    width = wide.shape[0] * LANES
    seqs = sizes[2] * sizes[3]
    names = ("arrive", "own", "first_a", "first_b", "second_a", "second_b", "third")
    held = {name: rest[at * count : (at + 1) * count] for at, name in enumerate(names)}
    small_parts, send_sem, recv_sem, own_sem, small_send, small_recv = rest[len(names) * count :]
    depth, cores, down, across = sizes
    spot = place_of()
    z, c, a, b = spot
    half = depth // 2
    front, back = pl.ds(0, half), pl.ds(half, depth - half)
    greet(sizes, spot)
    slots = {}

    def copy(w, kind, source, target, axis, by):
        slot = slots.setdefault(kind, len(slots))
        return pltpu.make_async_remote_copy(
            src_ref=source,
            dst_ref=target,
            send_sem=send_sem.at[w, slot],
            recv_sem=recv_sem.at[w, slot],
            device_id=peer_of(sizes, spot, axis, by),
            device_id_type=MESH,
        )

    def at_a(by):
        return lax.rem(a + by, down)

    def at_b(by):
        return lax.rem(b + by, across)

    twin, first, second, third = [], [], [], []
    for w in range(count):
        arrive = held["arrive"][w]
        twin.append(copy(w, "c", grads[w].at[:, 1 - c], arrive, 1, 1))
        first.append(
            [
                copy(w, ("a1", k), arrive.at[front, :, at_b(k)], held["first_a"][w].at[k - 1], 3, k)
                for k in range(1, across)
            ]
            + [
                copy(w, ("b1", l), arrive.at[back, at_a(l)], held["first_b"][w].at[l - 1], 2, l)
                for l in range(1, down)
            ]
        )
        second.append(
            [
                copy(w, ("a2", l), arrive.at[front, at_a(l), b], held["second_a"][w].at[l - 1], 2, l)
                for l in range(1, down)
            ]
            + [
                copy(w, ("b2", k), arrive.at[back, a, at_b(k)], held["second_b"][w].at[k - 1], 3, k)
                for k in range(1, across)
            ]
        )
        third.append(
            [
                copy(w, ("z", k), arrive.at[lax.rem(z + k, depth), a, b], held["third"][w].at[k - 1], 0, k)
                for k in range(1, depth)
            ]
        )

    stages = [(axis, 1 << bit) for axis in (1, 2, 3, 0) for bit in range(sizes[axis].bit_length() - 1)]

    def small_copy(at):
        axis, bit = stages[at]
        mine = spot[axis]
        towards = jnp.where(lax.rem(mine // bit, 2) == 0, bit, sizes[axis] - bit)
        return pltpu.make_async_remote_copy(
            src_ref=small_out,
            dst_ref=small_parts.at[at],
            send_sem=small_send.at[at],
            recv_sem=small_recv.at[at],
            device_id=peer_of(sizes, spot, axis, towards),
            device_id_type=MESH,
        )

    def own_load(w, at):
        return pltpu.make_async_copy(grads[w].at[at, c], held["own"][w].at[lax.rem(at, 2)], own_sem.at[w, lax.rem(at, 2)])

    def add_own(w):
        own_load(w, 0).start()

        def body(at, carry):
            @pl.when(at + 1 < depth)
            def _():
                own_load(w, at + 1).start()

            own_load(w, at).wait()
            for down_at in range(down):
                for across_at in range(across):
                    spot_ref = held["arrive"][w].at[at, down_at, across_at]
                    add_rows(spot_ref, spot_ref, [held["own"][w].at[lax.rem(at, 2), down_at, across_at]])
            return carry

        lax.fori_loop(0, depth, body, 0)

    small_out[...] = small[...]
    edges = spread_edge(seqs, edge, arrived, edge_send, edge_recv, False)
    units = rows * (chans // width)

    def last_unit(index, carry):
        row, base = unit_of(index, width, chans)
        ema_last(True, row, base, grad, keep, decay, edge, wide)
        return carry

    def backward_unit(index, carry):
        row, base = unit_of(index, width, chans)
        ema_backward(
            row, base, feed, grad, keep, decay, gain, start, end, back_out, small_out, wide, wide_grad, part, kept_states
        )
        return carry

    for w in range(min(2, count)):
        twin[w].start()
    lax.fori_loop(0, units, last_unit, 0)
    for item in edges:
        item.start()
    busy = count - 1
    for step in range(max(count + 3, busy + len(stages))):
        if step < count:
            w = step
            twin[w].wait_recv()
            if w + 2 < count:
                twin[w + 2].start()
            add_own(w)
            for item in first[w]:
                item.start()
        if 1 <= step <= count:
            w = step - 1
            arrive = held["arrive"][w]
            for item in first[w]:
                item.wait_recv()
            for at in range(half):
                for l in range(down):
                    spot_ref = arrive.at[at, l, b]
                    add_rows(spot_ref, spot_ref, [held["first_a"][w].at[k, at, l] for k in range(across - 1)])
            for at in range(half, depth):
                for k in range(across):
                    spot_ref = arrive.at[at, a, k]
                    add_rows(spot_ref, spot_ref, [held["first_b"][w].at[l, at - half, k] for l in range(down - 1)])
            for item in second[w]:
                item.start()
        if 2 <= step <= count + 1:
            w = step - 2
            arrive = held["arrive"][w]
            for item in second[w]:
                item.wait_recv()
            for at in range(half):
                spot_ref = arrive.at[at, a, b]
                add_rows(spot_ref, spot_ref, [held["second_a"][w].at[l, at] for l in range(down - 1)])
            for at in range(half, depth):
                spot_ref = arrive.at[at, a, b]
                add_rows(spot_ref, spot_ref, [held["second_b"][w].at[k, at - half] for k in range(across - 1)])
            for item in third[w]:
                item.start()
        if 3 <= step <= count + 2:
            w = step - 3
            for item in third[w]:
                item.wait_recv()
            add_rows(outs[w], held["arrive"][w].at[z, a, b], [held["third"][w].at[k] for k in range(depth - 1)])
        if step == 0:
            for item in edges:
                item.wait()
            join_edges(arrived, reach, power, end)
        if step < busy:
            lax.fori_loop(*share(units, busy, step), backward_unit, 0)
        stage = step - busy
        if stage == -1:
            small_copy(0).start()
        if 0 <= stage < len(stages):
            small_copy(stage).wait()
            small_out[...] = small_out[...] + small_parts[stage]
            if stage + 1 < len(stages):
                small_copy(stage + 1).start()
    for w in range(count):
        for item in [twin[w]] + first[w] + second[w] + third[w]:
            item.wait_send()


def scatter_grads(grads, small, feed, grad, keep, decay, gain, start, reach, power):
    sizes = shape_of()
    depth, cores, down, across = sizes
    total = depth * cores * down * across
    count = len(grads)
    half = depth // 2
    pieces = [piece_shape(g.shape[0] // total, g.shape[1]) for g in grads]
    leads = (
        (depth, down, across),
        (2, down, across),
        (across - 1, half, down),
        (down - 1, depth - half, across),
        (down - 1, half),
        (across - 1, depth - half),
        (depth - 1,),
    )
    slots = 1 + 2 * (across - 1 + down - 1) + depth - 1
    stages = sum(size.bit_length() - 1 for size in sizes)
    rows, length, chans = feed.shape
    state = (rows, 16, chans)
    width = min(BACKWARD_WIDTH, chans)
    seqs = down * across
    results = pl.pallas_call(
        functools.partial(scatter_kernel, sizes, count),
        out_shape=[jax.ShapeDtypeStruct(piece, jnp.float32) for piece in pieces]
        + [
            jax.ShapeDtypeStruct(small.shape, jnp.float32),
            jax.ShapeDtypeStruct(feed.shape, jnp.bfloat16),
        ],
        in_specs=anywhere(count) + vmem(9),
        out_specs=vmem(count + 2),
        scratch_shapes=[pltpu.VMEM(lead + piece, jnp.bfloat16) for lead in leads for piece in pieces]
        + [
            pltpu.VMEM((stages,) + small.shape, jnp.float32),
            pltpu.SemaphoreType.DMA((count, slots)),
            pltpu.SemaphoreType.DMA((count, slots)),
            pltpu.SemaphoreType.DMA((count, 2)),
            pltpu.SemaphoreType.DMA((stages,)),
            pltpu.SemaphoreType.DMA((stages,)),
            pltpu.VMEM(state, jnp.float32),
            pltpu.VMEM((seqs - 1,) + state, jnp.float32),
            pltpu.VMEM(state, jnp.float32),
            pltpu.SemaphoreType.DMA((seqs - 1,)),
            pltpu.SemaphoreType.DMA((seqs - 1,)),
            pltpu.VMEM((width // LANES, length, LANES), jnp.float32),
            pltpu.VMEM((width // LANES, length, LANES), jnp.float32),
            pltpu.VMEM((width // LANES * EMA_STEP * 8, LANES), jnp.float32),
            pltpu.VMEM((length * 16, width), jnp.float32),
        ],
        compiler_params=pltpu.CompilerParams(collective_id=1, has_side_effects=True, vmem_limit_bytes=62 * 2**20),
        name="scatter_grads",
    )(
        *[g.reshape(sizes + piece) for g, piece in zip(grads, pieces)],
        small, feed, grad, keep, decay, gain, start, reach, power,
    )
    sums = [result.reshape(g.shape[0] // total, g.shape[1]) for result, g in zip(results[:count], grads)]
    return sums, *results[count:]


def passed_on(alive, forward):
    count = lax.axis_size("seq")
    place = lax.axis_index("seq")
    through = jnp.ones((alive.shape[0], 1, 1), jnp.float32)
    factors = []
    for away in range(1, count):
        exists = place >= away if forward else place + away < count
        factors.append(jnp.broadcast_to(jnp.where(exists, through, 0.0), (alive.shape[0], 16, LANES)))
        at = jnp.clip(place - away if forward else place + away, 0, count - 1)
        through = through * lax.dynamic_slice_in_dim(alive, at, 1, 1)[:, :, None]
    return jnp.stack(factors)


def on_device(
    layer_input,
    cotangent,
    doc_ids,
    resets,
    mix_weight,
    value_weight,
    head_weight,
    expand_weight,
    shrink_weight,
    chan_vectors,
    ema_logits,
    ema_beta_eta,
    z_affine,
):
    seq_count = lax.axis_size("seq")
    seq_place = lax.axis_index("seq")
    rows, places, width = layer_input.shape
    tokens = rows * places
    scale = Z ** (-0.5)
    halo = min(-(-(REACH - 1) // places), seq_count - 1)
    window = (halo + 1) * places

    inputs32 = layer_input.astype(jnp.float32)
    center = inputs32 - jnp.mean(inputs32, axis=-1, keepdims=True)
    unit = lax.rsqrt(jnp.mean(center * center, axis=-1, keepdims=True) + 1e-05)
    plain = center * unit
    normed = plain * chan_vectors[0]
    normed_low = low(normed)

    rate = jax.nn.sigmoid(ema_logits[0])
    damping = jax.nn.sigmoid(ema_logits[1])
    decay = (1.0 - rate * damping).T
    weight_in = rate * ema_beta_eta[0]
    weight_out = ema_beta_eta[1]
    gain = (weight_in * weight_out).T
    decay_all = decay
    reach = 1
    while reach < places:
        decay_all = decay_all * decay_all
        reach *= 2
    powers = [jnp.ones_like(decay)]
    while len(powers) < seq_count - 1:
        powers.append(powers[-1] * decay_all)
    power = jnp.stack(powers)
    keep_row = 1.0 - resets.astype(jnp.float32)
    keep_own = lax.dynamic_slice_in_dim(keep_row, seq_place * places, places, 1)
    keep = jnp.broadcast_to(keep_own[:, None, :, None], (rows, 1, places, LANES)).reshape(rows, places, LANES)
    alive = jnp.min(keep_row.reshape(rows, seq_count, places), axis=2)

    (value_full, mix_full, head_full), normed_window, start, ema_low = gather_weights(
        (value_weight, mix_weight, head_weight),
        normed_low,
        keep,
        decay,
        gain,
        passed_on(alive, True),
        power,
        halo,
    )
    normed_window = normed_window.reshape(rows * window, width)
    value_full, mix_full, head_full, expand_late, shrink_late = lax.optimization_barrier(
        (value_full, mix_full, head_full, expand_weight, shrink_weight)
    )
    expand_full = lax.all_gather(expand_late, BOTH, axis=0, tiled=True)
    shrink_full = lax.all_gather(shrink_late, BOTH, axis=0, tiled=True)

    premix = (ema_low.astype(jnp.float32) + chan_vectors[2] * normed).reshape(tokens, width)
    mixed_low = low(jax.nn.silu(premix))
    value_pre = product(normed_window, value_full)
    values_low = low(jax.nn.silu(value_pre)).reshape(rows, window, V)
    projected = product(mixed_low, mix_full)
    shared_pre = projected[:, :Z]
    reset_pre = projected[:, Z : Z + V]
    head_base = projected[:, Z + V : Z + V + width]
    update_pre = projected[:, Z + V + width :]
    shared = jax.nn.silu(shared_pre)
    queries_low = low(shared * z_affine[0] + z_affine[1]).reshape(rows, places, Z)
    keys_low = low(shared * z_affine[2]).reshape(rows, places, Z)
    key_window = jnp.concatenate([shift_seq(keys_low, by) for by in range(halo, 0, -1)] + [keys_low], axis=1)
    reset_gate = jax.nn.silu(reset_pre)
    update_gate = jax.nn.sigmoid(update_pre)

    padded_docs = jnp.pad(doc_ids, ((0, 0), (halo * places, 0)), constant_values=-1)
    key_docs = lax.dynamic_slice_in_dim(padded_docs, seq_place * places, window, 1)
    query_docs = key_docs[:, halo * places :]
    causal = jnp.arange(window)[None, :] <= jnp.arange(places)[:, None] + halo * places
    allowed = causal[None] & (query_docs[:, :, None] == key_docs[:, None, :])
    scores = jnp.einsum("rid,rjd->rij", queries_low, key_window, preferred_element_type=jnp.float32) * scale
    scores = jnp.where(allowed, scores, NEG_FILL)
    peak = jnp.max(scores, axis=-1, keepdims=True)
    expo = jnp.exp(scores - peak)
    total = jnp.sum(expo, axis=-1, keepdims=True)
    probs = expo / total
    probs_low = low(probs)
    attended = jnp.einsum(
        "rij,rjv->riv", probs_low, values_low, preferred_element_type=jnp.float32
    ).reshape(tokens, V)
    gated_low = low(reset_gate * attended)
    head_pre = head_base + product(gated_low, head_full)
    candidate = jax.nn.silu(head_pre)
    residual_in = inputs32.reshape(tokens, width)
    first = residual_in + update_gate * (candidate - residual_in)
    second, second_pull = jax.vjp(scaled_norm, first, chan_vectors[1])
    second_low = low(second)
    expand_pre = product(second_low, expand_full)
    hidden_low = low(jax.nn.silu(expand_pre))
    output = low(first + product(hidden_low, shrink_full)).reshape(rows, places, width)

    cot_low = cotangent.reshape(tokens, width)
    shrink_part = low(transposed(hidden_low, cot_low))
    d_expand = low(against(cot_low, shrink_full) * silu_slope(expand_pre))
    expand_part = low(transposed(second_low, d_expand))
    d_first_norm, d_gain_two = second_pull(against(d_expand, expand_full))
    d_first = cot_low.astype(jnp.float32) + d_first_norm
    d_update = d_first * (candidate - residual_in) * update_gate * (1.0 - update_gate)
    d_direct = d_first * (1.0 - update_gate)
    d_head = d_first * update_gate * silu_slope(head_pre)
    d_head_low = low(d_head)
    head_part = low(transposed(gated_low, d_head_low))
    d_gated = against(d_head_low, head_full)
    d_reset = d_gated * attended * silu_slope(reset_pre)
    d_attended = low(d_gated * reset_gate).reshape(rows, places, V)
    d_probs = jnp.einsum("riv,rjv->rij", d_attended, values_low, preferred_element_type=jnp.float32)
    balance = jnp.sum(probs * d_probs, axis=-1, keepdims=True)
    d_scores = low(probs * (d_probs - balance))
    d_queries = scale * jnp.einsum("rij,rjd->rid", d_scores, key_window, preferred_element_type=jnp.float32)
    key_term = scale * jnp.einsum("rij,rid->rjd", d_scores, queries_low, preferred_element_type=jnp.float32)
    d_keys = key_term[:, halo * places :]
    for by in range(1, halo + 1):
        begin = (halo - by) * places
        d_keys = d_keys + shift_seq(low(key_term[:, begin : begin + places]), -by).astype(jnp.float32)
    d_keys32 = low(d_keys).astype(jnp.float32).reshape(tokens, Z)
    d_values = jnp.einsum("rij,riv->rjv", probs_low, d_attended, preferred_element_type=jnp.float32)
    d_value_pre = low(d_values.reshape(rows * window, V) * silu_slope(value_pre))
    value_part = low(transposed(normed_window, d_value_pre))
    value_term = against(d_value_pre, value_full).reshape(rows, halo + 1, places, width)
    terms = low(value_term[:, :halo])
    d_normed_value = value_term[:, halo]
    for by in range(1, halo + 1):
        d_normed_value = d_normed_value + shift_seq(terms[:, halo - by], -by).astype(jnp.float32)
    d_query_flat = d_queries.reshape(tokens, Z)
    d_shared = d_query_flat * z_affine[0] + d_keys32 * z_affine[2]
    affine_part = jnp.stack(
        [
            jnp.sum(d_query_flat * shared, axis=0),
            jnp.sum(d_query_flat, axis=0),
            jnp.sum(d_keys32 * shared, axis=0),
        ]
    )
    d_projected = low(
        jnp.concatenate([d_shared * silu_slope(shared_pre), d_reset, d_head, d_update], axis=1)
    )
    mix_part = low(transposed(mixed_low, d_projected))
    d_premix = against(d_projected, mix_full) * silu_slope(premix)
    omega_part = jnp.sum(d_premix * normed.reshape(tokens, width), axis=0)
    d_premix = d_premix.reshape(rows, places, width)
    d_ema = low(d_premix)
    known = d_premix * chan_vectors[2] + d_normed_value
    d_gain_one = jnp.sum(known * plain, axis=(0, 1))
    small_part = jnp.concatenate(
        [
            jnp.zeros((32, width), jnp.float32),
            jnp.stack([d_gain_one, d_gain_two, omega_part]),
            jnp.pad(affine_part.reshape(1, 3 * Z), ((0, 4), (0, width - 3 * Z))),
        ],
        axis=0,
    )
    (shrink_grad, expand_grad, head_grad, value_grad, mix_grad), small_sum, d_feed = scatter_grads(
        (shrink_part, expand_part, head_part, value_part, mix_part),
        small_part,
        normed_low,
        d_ema,
        keep,
        decay,
        gain,
        start,
        passed_on(alive, False),
        power,
    )
    d_normed = known + d_feed.astype(jnp.float32)
    pulled = d_normed * chan_vectors[0]
    pulled = pulled - jnp.mean(pulled, axis=-1, keepdims=True) - plain * jnp.mean(pulled * plain, axis=-1, keepdims=True)
    x_grad = d_direct.reshape(rows, places, width) + pulled * unit
    gain_sum = small_sum[:16]
    decay_sum = small_sum[16:32]
    chan_grad = small_sum[32:35].at[0].add(jnp.sum(gain * gain_sum, axis=0) / chan_vectors[0])
    affine_grad = small_sum[35, : 3 * Z].reshape(3, Z)
    d_gain = gain_sum.T
    d_decay = (decay_sum * gain).T
    d_weight_in = d_gain * weight_out
    coef_grad = jnp.stack([d_weight_in * rate, d_gain * weight_in])
    d_rate = d_weight_in * ema_beta_eta[0] - d_decay * damping
    d_damping = -d_decay * rate
    logits_grad = jnp.stack([d_rate * rate * (1.0 - rate), d_damping * damping * (1.0 - damping)])
    return (
        output,
        x_grad,
        mix_grad,
        value_grad,
        head_grad,
        expand_grad,
        shrink_grad,
        chan_grad,
        logits_grad,
        coef_grad,
        affine_grad,
    )


def solution(mesh):
    placed = (
        P("dp", "seq", None),
        P("dp", "seq", None),
        P("dp", None),
        P("dp", None),
        P(BOTH, None),
        P(BOTH, None),
        P(BOTH, None),
        P(BOTH, None),
        P(BOTH, None),
        P(),
        P(),
        P(),
        P(),
    )
    return jax.shard_map(
        on_device,
        mesh=mesh,
        in_specs=placed,
        out_specs=(
            P("dp", "seq", None),
            P("dp", "seq", None),
            P(BOTH, None),
            P(BOTH, None),
            P(BOTH, None),
            P(BOTH, None),
            P(BOTH, None),
            P(),
            P(),
            P(),
            P(),
        ),
        check_vma=False,
    )
```

time: 1570 us -> 859 us (0.55)
  waiting for transfers between devices: 939 us -> 41.8 us
  Pallas kernels: 69.2 us -> 381 us
  blocking collectives: 77.8 us -> 0 us
  other arithmetic: 97.5 us -> 78.5 us
    reduce_scatter x5 -> x0, waiting for transfers between devices: 601 us -> none  [scatter_grad(): lax.psum_scatter(low(grad), BOTH, scatter_dimension=0, tiled=True)]
    pallas_call x4 -> x2, Pallas kernels: 69.2 us -> 381 us  [the longest x1 224 us: scatter_grads(): pl.pallas_call(functools.partial(scatter_kernel, sizes, count), out_shape...]
    ppermute x14 -> x6, waiting for transfers between devices: 170 us -> 0.02 us  [shift_seq(): return lax.ppermute(values, 'seq', pairs)]
    all_gather x5 -> x2, waiting for transfers between devices: 166 us -> 41.8 us  [the longest x1 41.8 us: on_device(): shrink_full = lax.all_gather(shrink_late, BOTH, axis=0, tiled=True)]
    psum x1 -> x0, blocking collectives: 77.8 us -> none  [on_device(): lax.psum((jnp.stack([d_gain_one, d_gain_two, omega_part]), jnp.sum(gain_p...]
    ppermute x14 -> x6, starting transfers between devices: 32.2 us -> 19 us  [shift_seq(): return lax.ppermute(values, 'seq', pairs)]
    convert_element_type x9 -> x7, other arithmetic: 46.3 us -> 35.9 us  [low(): return values.astype(jnp.bfloat16)]
  transfers between devices with their start and end apart: 25 -> 8, of which waited for: 17 -> 1; matrix products, arithmetic and copies ran while one was open for 19% -> 21% of each run, Pallas kernels for 1% -> 0%
where the time goes in v2:
time: 859 us; the launch traced here: 850 us
  Pallas kernels  381 us (44%)
  matrix products  284 us (33%)
  other arithmetic  78.5 us (9%)
  waiting for transfers between devices  41.8 us (5%)
  local copies, waits for them, and re-layouts  29.7 us (3%)
  starting transfers between devices  19.1 us (2%)
  between operations  15.7 us (2%)
    pallas_call x1, Pallas kernels, scatter_grads(): pl.pallas_call(functools.partial(scatter_kernel, sizes, count), out_shape...  224 us
    pallas_call x1, Pallas kernels, gather_weights(): pl.pallas_call(functools.partial(gather_kernel, sizes, count, halo), out_...  157 us
    dot_general x5, matrix products, against(): lax.dot_general(left, right, (((1,), (1,)), ((), ())), preferred_element_...  84.2 us
    dot_general x5, matrix products, product(): return jnp.dot(left, right, preferred_element_type=jnp.float32)  83.1 us
    dot_general x5, matrix products, transposed(): lax.dot_general(left, right, (((0,), (0,)), ((), ())), preferred_element_...  68 us
    all_gather x1, waiting for transfers between devices, on_device(): shrink_full = lax.all_gather(shrink_late, BOTH, axis=0, tiled=True)  41.8 us
    convert_element_type x7, other arithmetic, low(): return values.astype(jnp.bfloat16)  35.9 us
    unnamed x162, local copies, waits for them, and re-layouts  19.3 us
  transfers between devices with their start and end apart: 8, of which 1 were waited for; matrix products, arithmetic and copies ran while one was open for 21% of the time, Pallas kernels for 0%

profile of v2, /device:TPU:0, one launch (start us, length us, event | category | flops | bytes accessed | tf_op | source)
XLA Modules:
  0.0 850.4 jit_solution(388253867756470938)
XLA Ops:
  8.2 1.9 convert_reduce_fusion
  10.2 2.3 fusion.33
  12.9 2.7 fusion.27
  16.4 157.1 %gather_weights.1 = (bf16[4,2,2,2,32,2048]{5,4,3,2,1,0:T(8,128)(2,1)}, bf16[4,2,2,2,32,4224]{5,4,3,2,1,0:T(8,128)(2,1)}, bf16[4,2,2,2,64,1024]{5,4,3,2,1,0:T(8,1...) custom-call(bf16[32,2048]{1,0:T(8,128)(2,1)S(1)} %copy-done.8, ...), custom_call_target="tpu_custom_call" | custom-call | tf_op jit(solution)/shard_map/gather_weights/pallas_call | solution.py:485
  173.5 1.3 copy-done
  175.7 2.7 multiply_add_fusion
  178.3 2.0 copy-done.18
  181.5 13.3 %fusion.90 = f32[1024,4224]{1,0:T(8,128)S(1)} fusion(bf16[1024,1024]{1,0:T(8,128)(2,1)S(1)} %fusion.18, bf16[1024,4224]{1,0:T(8,128)(2,1)} %bitcast.296), kind=kOutput, calls=%fused_computation.196 | convolution fusion | flops 8858370048 | bytes 28049408 | tf_op jit(solution)/shard_map/dot_general | solution.py:184
  194.9 5.9 copy-done.20
  201.0 12.6 %collective-permute-start = (bf16[2,512,128]{2,1,0:T(8,128)(2,1)S(1)}, bf16[2,512,128]{2,1,0:T(8,128)(2,1)S(1)}, u32[]{:S(2)}, u32[]{:S(2)}) collective-permute-start(bf16[2,512,128]{2,1,0:T(8,128)(2,1)S(1)} %bitcast.271), channel_id=1, source_target_pairs={{0,2},{1,3},{4,6},{5,7},{8,10},{9,11},{12,14},{13,15},{16,18},{17,... | collective-permute-start | bytes 786440 | tf_op jit(solution)/shard_map/ppermute | solution.py:202
  213.6 1.3 collective-permute-start.1
  215.5 26.4 %multiply_convert_fusion = (bf16[3072,2048]{1,0:T(8,128)(2,1)}, f32[3072,2048]{1,0:T(8,128)}) fusion(bf16[3072,1024]{1,0:T(8,128)(2,1)} %bitcast.300, bf16[1024,2048]{1,0:T(8,128)(2,1)} %bitcast.302), kind=kOutput, calls=%fused_computation.3 | convolution fusion | flops 12916359168 | bytes 48234496 | tf_op jit(solution)/shard_map/dot_general | solution.py:184
  242.8 4.5 fusion.87
  247.9 14.2 %fusion.41 = f32[2,512,2048]{2,1,0:T(8,128)} fusion(bf16[2,1536,2048]{2,1,0:T(8,128)(2,1)} %bitcast.306, f32[2,512]{1,0:T(2,128)S(1)} %get-tuple-element.103, s32[2,1536]{1,0:T(2,128)S(1)} %pad_dynamic-slice_fusion.1, s32[2,512]{1,0:T(2,128)S(1)} %pad_dynamic-slice_fusion, pred[512,1536]{1,0:T(8,128)(4,1)S(1)} %iota_compare_fusion, ...), kind=kOutput, calls=%fused_computation.90 | convolution fusion | flops 6858476032 | bytes 22827008 | tf_op jit(solution)/shard_map/rij,rjv->riv/dot_general | solution.py:890
  262.1 7.9 fusion.3
  270.2 11.4 %fusion.83 = (f32[1024]{0:T(1024)S(1)}, f32[1024,1024]{1,0:T(8,128)S(1)}, f32[1024,1024]{1,0:T(8,128)}) fusion(f32[1024,4224]{1,0:T(8,128)} %copy-done.20, bf16[2,512,1024]{2,1,0:T(8,128)(2,1)S(1)} %copy-done.11, bf16[1024,2048]{1,0:T(8,128)(2,1)S(1)} %fusion.3, bf16[2048,1024]{1,0:T(8,128)(2,1)S(1)} %bitcast.305), kind=kOutput, calls=%fused_computation.189 | convolution fusion | flops 4308597760 | bytes 27267072 | tf_op jit(solution)/shard_map/dot_general | solution.py:184
  281.6 2.0 copy-done.15
  284.2 19.7 %multiply_convert_fusion.1 = (bf16[1024,4096]{1,0:T(8,128)(2,1)}, f32[1024,4096]{1,0:T(8,128)}) fusion(bf16[1024,4096]{1,0:T(8,128)(2,1)} %all-gather.3.cloned.1.call-done, f32[1024,1024]{1,0:T(8,128)} %copy-done.15, f32[1024]{0:T(1024)S(1)} %bitcast.283, f32[1024]{0:T(1024)S(1)} %fusion.69, f32[1024]{0:T(1024)S(1)} %broadcast_multiply_fusion), kind=kOutput, calls=%fused_computation.7 | convolution fusion | flops 8615100416 | bytes 37761024 | tf_op jit(solution)/shard_map/dot_general | solution.py:184
  304.0 41.8 %all-gather.5.cloned.1.call-done = bf16[4096,1024]{1,0:T(8,128)(2,1)} async-done(((bf16[128,1024]{1,0:T(8,128)(2,1)}), bf16[4096,1024]{1,0:T(8,128)(2,1)}) %all-gather.5.cloned.1.call-update) | async-done | bytes 8388624 | tf_op jit(solution)/shard_map/all_gather | solution.py:860
  345.7 19.7 %fusion.2 = bf16[1024,4096]{1,0:T(8,128)(2,1)} fusion(f32[1024,4096]{1,0:T(8,128)} %get-tuple-element.107, bf16[4096,1024]{1,0:T(8,128)(2,1)} %all-gather.5.cloned.1.call-done, bf16[1024,1024]{1,0:T(8,128)(2,1)} %bitcast.265), kind=kOutput, calls=%fused_computation.6 | convolution fusion | flops 8627683328 | bytes 35651584 | tf_op jit(solution)/shard_map/dot_general | solution.py:188
  365.4 15.1 %multiply_reduce_fusion.1 = (f32[1024]{0:T(1024)}, f32[1024]{0:T(1024)S(1)}, f32[1024,1024]{1,0:T(8,128)S(1)}) fusion(f32[1024,1024]{1,0:T(8,128)S(1)} %copy-done.16, f32[1024]{0:T(1024)S(1)} %fusion.69, f32[1024]{0:T(1024)S(1)} %broadcast_multiply_fusion, f32[1024]{0:T(1024)S(1)} %bitcast.284, bf16[1024,4096]{1,0:T(8,128)(2,1)} %fusion.2, ...), kind=kOutput, calls=%fused_computation.65 | convolution fusion | flops 8597272576 | bytes 25186304 | tf_op jit(solution)/shard_map/dot_general | solution.py:188
  380.5 1.8 fusion.82
  383.4 8.2 multiply_convert_fusion.4
  391.6 15.6 %fusion.5 = (bf16[1024,2048]{1,0:T(8,128)(2,1)}, bf16[1024,2048]{1,0:T(8,128)(2,1)}) fusion(f32[2,512,2048]{2,1,0:T(8,128)} %fusion.41, f32[1024,4224]{1,0:T(8,128)} %copy-done.20, bf16[1024,1024]{1,0:T(8,128)(2,1)} %get-tuple-element.78, bf16[2048,1024]{1,0:T(8,128)(2,1)} %bitcast.304), kind=kOutput, calls=%fused_computation.15 | convolution fusion | flops 4322230272 | bytes 31457280 | tf_op jit(solution)/shard_map/dot_general | solution.py:188
  407.2 6.3 convolution_convert_fusion.4
  413.6 15.4 %convolution_convert_fusion.1 = bf16[1024,4096]{1,0:T(8,128)(2,1)} fusion(bf16[1024,4096]{1,0:T(8,128)(2,1)} %fusion.2, f32[1024,1024]{1,0:T(8,128)S(1)} %copy-done.16, f32[1024]{0:T(1024)S(1)} %bitcast.286, f32[1024]{0:T(1024)S(1)} %fusion.69, f32[1024]{0:T(1024)S(1)} %broadcast_multiply_fusion), kind=kOutput, calls=%fused_computation.19 | convolution fusion | flops 8598323200 | bytes 20983808 | tf_op jit(solution)/shard_map/dot_general | solution.py:192
  429.0 15.1 %fusion.39 = f32[2,1536,2048]{2,1,0:T(8,128)} fusion(bf16[2,512,2048]{2,1,0:T(8,128)(2,1)} %bitcast.308, f32[2,512]{1,0:T(2,128)S(1)} %copy-done.64, s32[2,1536]{1,0:T(2,128)S(1)} %copy-done.57, s32[2,512]{1,0:T(2,128)S(1)} %copy-done.66, pred[512,1536]{1,0:T(8,128)(4,1)} %copy-done.35, bf16[2,512,128]{2,1,0:T(8,128)(2,1)S(1)} %bitcast.269, ...), kind=kOutput, calls=%fused_computation.88 | convolution fusion | flops 6858476032 | bytes 31215616 | tf_op jit(solution)/shard_map/rij,riv->rjv/dot_general | solution.py:928
  444.1 19.2 %fusion.1 = bf16[3072,2048]{1,0:T(8,128)(2,1)S(1)} fusion(f32[2,1536,2048]{2,1,0:T(8,128)} %fusion.39, f32[3072,2048]{1,0:T(8,128)} %get-tuple-element.102), kind=kLoop, calls=%fused_computation.2 | loop fusion | flops 56623104 | bytes 62914560 | tf_op jit(solution)/shard_map/convert_element_type | solution.py:196
  463.4 16.0 %fusion.91 = f32[3072,1024]{1,0:T(8,128)} fusion(bf16[3072,2048]{1,0:T(8,128)(2,1)S(1)} %fusion.1, bf16[1024,2048]{1,0:T(8,128)(2,1)S(1)} %bitcast.303), kind=kOutput, calls=%fused_computation.197 | convolution fusion | flops 12884901888 | bytes 29360128 | tf_op jit(solution)/shard_map/dot_general | solution.py:188
  479.4 16.2 %convolution_convert_fusion.3 = bf16[1024,2048]{1,0:T(8,128)(2,1)} fusion(bf16[3072,1024]{1,0:T(8,128)(2,1)} %bitcast.301, bf16[3072,2048]{1,0:T(8,128)(2,1)S(1)} %fusion.1), kind=kOutput, calls=%fused_computation.76 | convolution fusion | flops 12886999040 | bytes 23068672 | tf_op jit(solution)/shard_map/dot_general | solution.py:192
  495.6 12.8 %multiply_reduce_fusion = (f32[2,512]{1,0:T(2,128)S(1)}, f32[2,512,1536]{2,1,0:T(8,128)}) fusion(f32[2,512,1536]{2,1,0:T(8,128)S(1)} %bitcast.260, f32[2,512]{1,0:T(2,128)S(1)} %copy-done.64, bf16[2,512,2048]{2,1,0:T(8,128)(2,1)} %bitcast.309, bf16[2,1536,2048]{2,1,0:T(8,128)(2,1)} %bitcast.307), kind=kOutput, calls=%fused_computation.22 | convolution fusion | flops 6447168512 | bytes 29368320 | tf_op jit(solution)/shard_map/riv,rjv->rij/dot_general | solution.py:918
  508.4 3.4 multiply_convert_fusion.3
  511.8 1.3 fusion.88
  513.2 1.3 collective-permute-start.2
  514.5 1.3 collective-permute-start.3
  515.8 6.4 slice_bitcast_fusion.2
  524.8 15.0 %convolution_convert_fusion.2 = bf16[4096,1024]{1,0:T(8,128)(2,1)} fusion(bf16[1024,4096]{1,0:T(8,128)(2,1)} %get-tuple-element.106, bf16[1024,1024]{1,0:T(8,128)(2,1)S(1)} %bitcast.266), kind=kOutput, calls=%fused_computation.20 | convolution fusion | flops 8594128896 | bytes 18874368 | tf_op jit(solution)/shard_map/dot_general | solution.py:192
  539.8 12.2 %add_convert_fusion = bf16[1024,1024]{1,0:T(8,128)(2,1)} fusion(f32[1024,1024]{1,0:T(8,128)S(1)} %copy-done.17, bf16[1024,4096]{1,0:T(8,128)(2,1)} %get-tuple-element.106, bf16[4096,1024]{1,0:T(8,128)(2,1)S(1)} %bitcast.299), kind=kOutput, calls=%fused_computation.70 | convolution fusion | flops 8592031744 | bytes 23068672 | tf_op jit(solution)/shard_map/dot_general | solution.py:184
  553.2 1.4 fusion.53
  554.6 17.8 %fusion.14 = (f32[1024]{0:T(1024)S(1)}, f32[1024,1024]{1,0:T(8,128)}) fusion(f32[2,512,1024]{2,1,0:T(8,128)} %get-tuple-element.87, f32[2,512,1024]{2,1,0:T(8,128)} %copy-done.18, bf16[1024,4224]{1,0:T(8,128)(2,1)} %bitcast.297, bf16[1024,1024]{1,0:T(8,128)(2,1)S(1)} %copy-done.29, bf16[1024,1024]{1,0:T(8,128)(2,1)} %get-tuple-element.78, ...), kind=kOutput, calls=%fused_computation.37 | convolution fusion | flops 8903457792 | bytes 29888512 | tf_op jit(solution)/shard_map/dot_general | solution.py:188
  572.5 4.0 bitcast_convert_fusion.refs_7_
  576.5 15.2 %convolution_convert_fusion = bf16[1024,4224]{1,0:T(8,128)(2,1)} fusion(bf16[1024,1024]{1,0:T(8,128)(2,1)S(1)} %copy-done.26, bf16[1024,1024]{1,0:T(8,128)(2,1)} %get-tuple-element.77, bf16[1024,1024]{1,0:T(8,128)(2,1)} %get-tuple-element.78, bf16[1024,2048]{1,0:T(8,128)(2,1)} %get-tuple-element.79, bf16[1024,128]{1,0:T(8,128)(2,1)S(1)} %get-tuple-element.82), kind=kOutput, calls=%fused_computation.9 | convolution fusion | flops 8897298432 | bytes 19398656 | tf_op jit(solution)/shard_map/dot_general | solution.py:192
  591.7 5.8 fusion.28
  597.5 1.3 concatenate.14.refs_5_
  598.8 224.2 %scatter_grads.1 = (f32[128,1024]{1,0:T(8,128)}, f32[32,4096]{1,0:T(8,128)}, f32[64,1024]{1,0:T(8,128)}, f32[32,2048]{1,0:T(8,128)}, f32[32,4224]{1,0:T(8,128)},...) custom-call(bf16[4,2,2,2,128,1024]{5,4,3,2,1,0:T(8,128)(2,1)} %bitcast.258, ...), custom_call_target="tpu_custom_call" | custom-call | tf_op jit(solution)/shard_map/scatter_grads/pallas_call | solution.py:745
  825.6 1.3 slice_reduce_fusion
  827.8 4.3 fusion.43
  833.7 4.8 fusion.32
  (220 shorter events, 21.2 us)
Async XLA Ops:
  7.2 277.0 %all-gather.3.cloned.1.call-start = ((), (), s32[]{:S(2)}) async-start(), calls=%async_computation | async-start | bytes 8650752 | tf_op jit(solution)/shard_map/all_gather | solution.py:859
  10.2 165.5 %copy-start.45 = (f32[2,512]{1,0:T(2,128)}, f32[2,512]{1,0:T(2,128)S(1)}, u32[]{:S(2)}) copy-start(f32[2,512]{1,0:T(2,128)S(1)} %broadcast_multiply_fusion.3) | copy-start | bytes 12292
  12.5 163.1 %copy-start.47 = (f32[2,512]{1,0:T(2,128)}, f32[2,512]{1,0:T(2,128)S(1)}, u32[]{:S(2)}) copy-start(f32[2,512]{1,0:T(2,128)S(1)} %add_rsqrt_fusion) | copy-start | bytes 12292
  12.5 163.1 %copy-start.49 = (f32[1,1024]{1,0:T(1,128)}, f32[1,1024]{1,0:T(1,128)S(1)}, u32[]{:S(2)}) copy-start(f32[1,1024]{1,0:T(1,128)S(1)} %get-tuple-element.96) | copy-start | bytes 12292
  12.5 163.1 %copy-start.52 = (f32[1,1024]{1,0:T(1,128)}, f32[1,1024]{1,0:T(1,128)S(1)}, u32[]{:S(2)}) copy-start(f32[1,1024]{1,0:T(1,128)S(1)} %get-tuple-element.97) | copy-start | bytes 12292
  15.6 160.0 %copy-start.67 = (f32[3,128]{1,0:T(4,128)S(1)}, f32[3,128]{1,0:T(4,128)}, u32[]{:S(2)}) copy-start(f32[3,128]{1,0:T(4,128)} %param.27) | copy-start | bytes 4612
  16.1 159.4 %copy-start.2 = (f32[3,16,1024]{2,1,0:T(8,128)}, f32[3,16,1024]{2,1,0:T(8,128)S(1)}, u32[]{:S(2)}) copy-start(f32[3,16,1024]{2,1,0:T(8,128)S(1)} %pad_maximum_fusion.4.refs_8_.refs_13_) | copy-start | bytes 589828
  16.3 157.2 %copy-start.1 = (f32[2,512,128]{2,1,0:T(8,128)}, f32[2,512,128]{2,1,0:T(8,128)S(1)}, u32[]{:S(2)}) copy-start(f32[2,512,128]{2,1,0:T(8,128)S(1)} %reshape.287.refs_4_.refs_8_) | copy-start | bytes 1572868
  175.5 170.2 %all-gather.5.cloned.1.call-start = ((), (), s32[]{:S(2)}) async-start(), calls=%async_computation.1 | async-start | bytes 8650752 | tf_op jit(solution)/shard_map/all_gather | solution.py:860
  175.6 19.3 %copy-start.58 = (f32[128]{0:T(128)}, f32[128]{0:T(128)S(1)}, u32[]{:S(2)}) copy-start(f32[128]{0:T(128)S(1)} %get-tuple-element.98) | copy-start | bytes 1540
  175.6 19.3 %copy-start.60 = (f32[128]{0:T(128)}, f32[128]{0:T(128)S(1)}, u32[]{:S(2)}) copy-start(f32[128]{0:T(128)S(1)} %get-tuple-element.99) | copy-start | bytes 1540
  181.5 13.4 %copy-start.25 = (bf16[1024,1024]{1,0:T(8,128)(2,1)}, bf16[1024,1024]{1,0:T(8,128)(2,1)S(1)}, u32[]{:S(2)}) copy-start(bf16[1024,1024]{1,0:T(8,128)(2,1)S(1)} %fusion.18) | copy-start | bytes 6291460
  181.5 33.4 %copy-start.51 = (s32[2,2048]{1,0:T(2,128)S(1)}, s32[2,2048]{1,0:T(2,128)}, u32[]{:S(2)}) copy-start(s32[2,2048]{1,0:T(2,128)} %param.17) | copy-start | bytes 49156
  201.0 46.3 %copy-start.31 = (bf16[1024,128]{1,0:T(8,128)(2,1)}, bf16[1024,128]{1,0:T(8,128)(2,1)S(1)}, u32[]{:S(2)}) copy-start(bf16[1024,128]{1,0:T(8,128)(2,1)S(1)} %get-tuple-element.84) | copy-start | bytes 786436
  201.0 46.3 %copy-start.41 = (bf16[1024,128]{1,0:T(8,128)(2,1)}, bf16[1024,128]{1,0:T(8,128)(2,1)S(1)}, u32[]{:S(2)}) copy-start(bf16[1024,128]{1,0:T(8,128)(2,1)S(1)} %get-tuple-element.83) | copy-start | bytes 786436
  201.0 41.8 %collective-permute-start = (bf16[2,512,128]{2,1,0:T(8,128)(2,1)S(1)}, bf16[2,512,128]{2,1,0:T(8,128)(2,1)S(1)}, u32[]{:S(2)}, u32[]{:S(2)}) collective-permute-start(bf16[2,512,128]{2,1,0:T(8,128)(2,1)S(1)} %bitcast.271), channel_id=1, source_target_pairs={{0,2},{1,3},{4,6},{5,7},{8,10},{9,11},{12,14},{13,15},{16,18},{17,... | collective-permute-start | bytes 786440 | tf_op jit(solution)/shard_map/ppermute | solution.py:202
  213.6 29.2 %collective-permute-start.1 = (bf16[2,512,128]{2,1,0:T(8,128)(2,1)S(1)}, bf16[2,512,128]{2,1,0:T(8,128)(2,1)S(1)}, u32[]{:S(2)}, u32[]{:S(2)}) collective-permute-start(bf16[2,512,128]{2,1,0:T(8,128)(2,1)S(1)} %bitcast.272), channel_id=1, source_target_pairs={{0,1},{1,2},{2,3},{4,5},{5,6},{6,7},{8,9},{9,10},{10,11},{12,13},{... | collective-permute-start | bytes 786440 | tf_op jit(solution)/shard_map/ppermute | solution.py:202
  215.0 32.3 %copy-start.56 = (s32[2,1536]{1,0:T(2,128)}, s32[2,1536]{1,0:T(2,128)S(1)}, u32[]{:S(2)}) copy-start(s32[2,1536]{1,0:T(2,128)S(1)} %pad_dynamic-slice_fusion.1) | copy-start | bytes 36868
  215.5 31.8 %copy-start.35 = (pred[512,1536]{1,0:T(8,128)(4,1)}, pred[512,1536]{1,0:T(8,128)(4,1)S(1)}, u32[]{:S(2)}) copy-start(pred[512,1536]{1,0:T(8,128)(4,1)S(1)} %iota_compare_fusion) | copy-start | bytes 2359300
  345.7 19.7 %copy-start.16 = (f32[1024,1024]{1,0:T(8,128)S(1)}, f32[1024,1024]{1,0:T(8,128)}, u32[]{:S(2)}) copy-start(f32[1024,1024]{1,0:T(8,128)} %copy-done.15) | copy-start | bytes 12582916
  391.6 15.6 %copy-start.23 = (bf16[1024,2048]{1,0:T(8,128)(2,1)S(1)}, bf16[1024,2048]{1,0:T(8,128)(2,1)}, u32[]{:S(2)}) copy-start(bf16[1024,2048]{1,0:T(8,128)(2,1)} %copy-done.22) | copy-start | bytes 12582916
  391.6 15.6 %copy-start.30 = (bf16[1024,1024]{1,0:T(8,128)(2,1)S(1)}, bf16[1024,1024]{1,0:T(8,128)(2,1)}, u32[]{:S(2)}) copy-start(bf16[1024,1024]{1,0:T(8,128)(2,1)} %get-tuple-element.78) | copy-start | bytes 6291460
  413.5 15.4 %copy-start.32 = (bf16[1024,128]{1,0:T(8,128)(2,1)S(1)}, bf16[1024,128]{1,0:T(8,128)(2,1)}, u32[]{:S(2)}) copy-start(bf16[1024,128]{1,0:T(8,128)(2,1)} %copy-done.31) | copy-start | bytes 786436
  413.5 15.4 %copy-start.42 = (bf16[1024,128]{1,0:T(8,128)(2,1)S(1)}, bf16[1024,128]{1,0:T(8,128)(2,1)}, u32[]{:S(2)}) copy-start(bf16[1024,128]{1,0:T(8,128)(2,1)} %copy-done.41) | copy-start | bytes 786436
  413.5 15.4 %copy-start.57 = (s32[2,1536]{1,0:T(2,128)S(1)}, s32[2,1536]{1,0:T(2,128)}, u32[]{:S(2)}) copy-start(s32[2,1536]{1,0:T(2,128)} %copy-done.56) | copy-start | bytes 36868
  413.5 15.4 %copy-start.64 = (f32[2,512]{1,0:T(2,128)S(1)}, f32[2,512]{1,0:T(2,128)}, u32[]{:S(2)}) copy-start(f32[2,512]{1,0:T(2,128)} %copy-done.63) | copy-start | bytes 12292
  413.5 15.4 %copy-start.66 = (s32[2,512]{1,0:T(2,128)S(1)}, s32[2,512]{1,0:T(2,128)}, u32[]{:S(2)}) copy-start(s32[2,512]{1,0:T(2,128)} %copy-done.65) | copy-start | bytes 12292
  413.6 15.4 %copy-start.71 = (bf16[2,512,128]{2,1,0:T(8,128)(2,1)S(1)}, bf16[2,512,128]{2,1,0:T(8,128)(2,1)}, u32[]{:S(2)}) copy-start(bf16[2,512,128]{2,1,0:T(8,128)(2,1)} %copy-done.70) | copy-start | bytes 786436
  413.6 15.4 %copy-start.73 = (bf16[2,512,128]{2,1,0:T(8,128)(2,1)S(1)}, bf16[2,512,128]{2,1,0:T(8,128)(2,1)}, u32[]{:S(2)}) copy-start(bf16[2,512,128]{2,1,0:T(8,128)(2,1)} %copy-done.72) | copy-start | bytes 786436
  444.1 19.2 %copy-start.68 = (bf16[4,2,2,2,32,2048]{5,4,3,2,1,0:T(8,128)(2,1)S(1)}, bf16[4,2,2,2,32,2048]{5,4,3,2,1,0:T(8,128)(2,1)}, u32[]{:S(2)}) copy-start(bf16[4,2,2,2,32,2048]{5,4,3,2,1,0:T(8,128)(2,1)} %get-tuple-element.42) | copy-start | bytes 12582916
  444.1 51.5 %slice-start = ((s8[6291456]{0:T(1024)(128)(4,1)}), s8[4194304]{0:T(1024)(128)(4,1)S(1)}, s32[]{:S(2)}) async-start(s8[6291456]{0:T(1024)(128)(4,1)} %bitcast.259), calls=%async_computation.2 | async-start | bytes 8388608
  463.4 32.2 %slice-start.1 = ((s8[6291456]{0:T(1024)(128)(4,1)}), s8[2097152]{0:T(1024)(128)(4,1)S(1)}, s32[]{:S(2)}) async-start(s8[6291456]{0:T(1024)(128)(4,1)} %bitcast.259), calls=%async_computation.3 | async-start | bytes 4194304
  513.2 39.9 %collective-permute-start.2 = (bf16[2,512,128]{2,1,0:T(8,128)(2,1)S(1)}, bf16[2,512,128]{2,1,0:T(8,128)(2,1)S(1)}, u32[]{:S(2)}, u32[]{:S(2)}) collective-permute-start(bf16[2,512,128]{2,1,0:T(8,128)(2,1)S(1)} %get-tuple-element.89), channel_id=1, source_target_pairs={{1,0},{2,1},{3,2},{5,4},{6,5},{7,6},{9,8},{10,9},{11,10},{13,12},{... | collective-permute-start | bytes 786440 | tf_op jit(solution)/shard_map/ppermute | solution.py:202
  514.5 38.6 %collective-permute-start.3 = (bf16[2,512,128]{2,1,0:T(8,128)(2,1)S(1)}, bf16[2,512,128]{2,1,0:T(8,128)(2,1)S(1)}, u32[]{:S(2)}, u32[]{:S(2)}) collective-permute-start(bf16[2,512,128]{2,1,0:T(8,128)(2,1)S(1)} %get-tuple-element.90), channel_id=1, source_target_pairs={{2,0},{3,1},{6,4},{7,5},{10,8},{11,9},{14,12},{15,13},{18,16},{19,... | collective-permute-start | bytes 786440 | tf_op jit(solution)/shard_map/ppermute | solution.py:202
  515.8 24.0 %slice-start.2 = ((s8[8388608]{0:T(1024)(128)(4,1)}), s8[4194304]{0:T(1024)(128)(4,1)S(1)}, s32[]{:S(2)}) async-start(s8[8388608]{0:T(1024)(128)(4,1)} %bitcast.298), calls=%async_computation.4 | async-start | bytes 8388608
  522.2 69.5 %collective-permute-start.4 = (bf16[2,512,1024]{2,1,0:T(8,128)(2,1)}, bf16[2,512,1024]{2,1,0:T(8,128)(2,1)}, u32[]{:S(2)}, u32[]{:S(2)}) collective-permute-start(bf16[2,512,1024]{2,1,0:T(8,128)(2,1)} %get-tuple-element.85), channel_id=1, source_target_pairs={{1,0},{2,1},{3,2},{5,4},{6,5},{7,6},{9,8},{10,9},{11,10},{13,12},{... | collective-permute-start | bytes 6291464 | tf_op jit(solution)/shard_map/ppermute | solution.py:202
  523.5 68.2 %collective-permute-start.5 = (bf16[2,512,1024]{2,1,0:T(8,128)(2,1)}, bf16[2,512,1024]{2,1,0:T(8,128)(2,1)}, u32[]{:S(2)}, u32[]{:S(2)}) collective-permute-start(bf16[2,512,1024]{2,1,0:T(8,128)(2,1)} %get-tuple-element.86), channel_id=1, source_target_pairs={{2,0},{3,1},{6,4},{7,5},{10,8},{11,9},{14,12},{15,13},{18,16},{19,... | collective-permute-start | bytes 6291464 | tf_op jit(solution)/shard_map/ppermute | solution.py:202
  524.8 15.0 %copy-start.17 = (f32[1024,1024]{1,0:T(8,128)S(1)}, f32[1024,1024]{1,0:T(8,128)}, u32[]{:S(2)}) copy-start(f32[1024,1024]{1,0:T(8,128)} %copy-done.15) | copy-start | bytes 12582916
  524.8 15.0 %slice-start.3 = ((s8[8388608]{0:T(1024)(128)(4,1)}), s8[4194304]{0:T(1024)(128)(4,1)S(1)}, s32[]{:S(2)}) async-start(s8[8388608]{0:T(1024)(128)(4,1)} %bitcast.298), calls=%async_computation.5 | async-start | bytes 8388608
  576.5 15.2 %copy-start.12 = (bf16[2,512,1024]{2,1,0:T(8,128)(2,1)S(1)}, bf16[2,512,1024]{2,1,0:T(8,128)(2,1)}, u32[]{:S(2)}) copy-start(bf16[2,512,1024]{2,1,0:T(8,128)(2,1)} %param.15) | copy-start | bytes 6291460
  576.5 15.2 %copy-start.19 = (f32[1024,1024]{1,0:T(8,128)S(1)}, f32[1024,1024]{1,0:T(8,128)}, u32[]{:S(2)}) copy-start(f32[1024,1024]{1,0:T(8,128)} %get-tuple-element.114) | copy-start | bytes 12582916
  576.5 15.2 %copy-start.46 = (f32[2,512]{1,0:T(2,128)S(1)}, f32[2,512]{1,0:T(2,128)}, u32[]{:S(2)}) copy-start(f32[2,512]{1,0:T(2,128)} %copy-done.45) | copy-start | bytes 12292
  576.5 15.2 %copy-start.48 = (f32[2,512]{1,0:T(2,128)S(1)}, f32[2,512]{1,0:T(2,128)}, u32[]{:S(2)}) copy-start(f32[2,512]{1,0:T(2,128)} %copy-done.47) | copy-start | bytes 12292
  576.5 15.2 %copy-start.53 = (f32[1,1024]{1,0:T(1,128)S(1)}, f32[1,1024]{1,0:T(1,128)}, u32[]{:S(2)}) copy-start(f32[1,1024]{1,0:T(1,128)} %copy-done.52) | copy-start | bytes 12292
  598.8 224.2 %copy-start.4 = (f32[16,1024]{1,0:T(8,128)S(1)}, f32[16,1024]{1,0:T(8,128)}, u32[]{:S(2)}) copy-start(f32[16,1024]{1,0:T(8,128)} %copy-done.3) | copy-start | bytes 196612
  598.8 224.2 %copy-start.34 = (f32[2,1024,16]{1,2,0:T(8,128)S(1)}, f32[2,1024,16]{1,2,0:T(8,128)}, u32[]{:S(2)}) copy-start(f32[2,1024,16]{1,2,0:T(8,128)} %param.25) | copy-start | bytes 393220
  598.8 224.3 %copy-start.40 = (f32[2,1024,16]{1,2,0:T(8,128)S(1)}, f32[2,1024,16]{1,2,0:T(8,128)}, u32[]{:S(2)}) copy-start(f32[2,1024,16]{1,2,0:T(8,128)} %param.26) | copy-start | bytes 393220
  598.8 229.0 %copy-start.50 = (f32[1,1024]{1,0:T(1,128)S(1)}, f32[1,1024]{1,0:T(1,128)}, u32[]{:S(2)}) copy-start(f32[1,1024]{1,0:T(1,128)} %copy-done.49) | copy-start | bytes 12292
  (38 other events, 178.3 us)
Sparse Core Ops, SparseCore 0:
  175.6 90.9 all-gather.2
  269.5 76.1 all-gather.4

commit v3 on v2

--- a/solution.py
+++ b/solution.py
@@ -792,6 +792,158 @@
     return jnp.stack(factors)
 
 
+QUERY_BLOCK = 256
+KEY_BLOCK = 512
+VALUE_BLOCK = 1024
+
+
+def attend_kernel(halo_span, query, key, value, key_docs, query_docs, out, probs):
+    size, span = probs.shape
+    first = pl.program_id(1) * size
+    keys = pl.ds(pl.multiple_of(first, LANES), span)
+    scores = against(query[0], key[0, keys, :]) * Z ** (-0.5)
+    query_at = lax.broadcasted_iota(jnp.int32, (size, span), 0) + halo_span
+    key_at = lax.broadcasted_iota(jnp.int32, (size, span), 1)
+    allowed = (key_at <= query_at) & (key_docs[0, :, keys] == query_docs[0])
+    scores = jnp.where(allowed, scores, NEG_FILL)
+    expo = jnp.exp(scores - jnp.max(scores, axis=1, keepdims=True))
+    probs[...] = low(expo / jnp.sum(expo, axis=1, keepdims=True))
+
+    def body(at, carry):
+        columns = pl.ds(pl.multiple_of(at * VALUE_BLOCK, VALUE_BLOCK), VALUE_BLOCK)
+        out[0, :, columns] = product(probs[...], value[0, keys, columns])
+        return carry
+
+    lax.fori_loop(0, out.shape[2] // VALUE_BLOCK, body, 0)
+
+
+def attend(query, key, value, docs_row, docs_column, halo):
+    rows, places, _ = query.shape
+    window, wide = value.shape[1:]
+    size = min(QUERY_BLOCK, places)
+    span = halo * places + size
+    return pl.pallas_call(
+        functools.partial(attend_kernel, halo * places),
+        out_shape=jax.ShapeDtypeStruct((rows, places, wide), jnp.float32),
+        grid=(rows, places // size),
+        in_specs=[
+            pl.BlockSpec((1, size, Z), lambda r, i: (r, i, 0)),
+            pl.BlockSpec((1, window, Z), lambda r, i: (r, 0, 0)),
+            pl.BlockSpec((1, window, wide), lambda r, i: (r, 0, 0)),
+            pl.BlockSpec((1, 1, window), lambda r, i: (r, 0, 0)),
+            pl.BlockSpec((1, size, 1), lambda r, i: (r, i, 0)),
+        ],
+        out_specs=pl.BlockSpec((1, size, wide), lambda r, i: (r, i, 0)),
+        scratch_shapes=[pltpu.VMEM((size, span), jnp.bfloat16)],
+        compiler_params=pltpu.CompilerParams(vmem_limit_bytes=40 * 2**20),
+        cost_estimate=pl.CostEstimate(
+            flops=2 * rows * places * span * (wide + Z),
+            bytes_accessed=rows * (window * wide * 2 + places * wide * 4),
+            transcendentals=rows * places * span,
+        ),
+        name="attend",
+    )(query, key, value, docs_row, docs_column[:, halo * places :])
+
+
+def attend_back_kernel(
+    halo_span, query, key, value, slope, pulled, key_docs, query_docs, d_query, d_key, d_value, chances, pulls, balance
+):
+    window, places = chances.shape
+    step = d_value.shape[1]
+    chunk = pl.program_id(1)
+
+    @pl.when(chunk == 0)
+    def _():
+        peak = jnp.full((1, places), NEG_FILL, jnp.float32)
+
+        def score(at, peak):
+            keys = pl.ds(pl.multiple_of(at * step, step), step)
+            scores = against(key[0, keys, :], query[0]) * Z ** (-0.5)
+            key_at = lax.broadcasted_iota(jnp.int32, (step, places), 0) + at * step
+            query_at = lax.broadcasted_iota(jnp.int32, (step, places), 1) + halo_span
+            allowed = (key_at <= query_at) & (key_docs[0, keys, :] == query_docs[0])
+            scores = jnp.where(allowed, scores, NEG_FILL)
+            chances[keys, :] = scores
+            return jnp.maximum(peak, jnp.max(scores, axis=0, keepdims=True))
+
+        peak = lax.fori_loop(0, window // step, score, peak)
+
+        def weigh(at, total):
+            keys = pl.ds(pl.multiple_of(at * step, step), step)
+            expo = jnp.exp(chances[keys, :] - peak)
+            chances[keys, :] = expo
+            return total + jnp.sum(expo, axis=0, keepdims=True)
+
+        total = lax.fori_loop(0, window // step, weigh, jnp.zeros((1, places), jnp.float32))
+
+        def pull(at, held):
+            keys = pl.ds(pl.multiple_of(at * step, step), step)
+            probs = chances[keys, :] / total
+            chances[keys, :] = probs
+            local = against(value[0, keys, :], pulled[0])
+            pulls[keys, :] = local
+            return held + jnp.sum(probs * local, axis=0, keepdims=True)
+
+        balance[...] = lax.fori_loop(0, window // step, pull, jnp.zeros((1, places), jnp.float32))
+        d_query[...] = jnp.zeros_like(d_query)
+
+    keys = pl.ds(pl.multiple_of(chunk * step, step), step)
+    probs = chances[keys, :]
+    d_scores = low(probs * (pulls[keys, :] - balance[...]))
+    d_key[0] = product(d_scores, query[0]) * Z ** (-0.5)
+    d_query[0] = d_query[0] + transposed(d_scores, key[0, keys, :]) * Z ** (-0.5)
+    probs_low = low(probs)
+
+    def body(at, carry):
+        columns = pl.ds(pl.multiple_of(at * VALUE_BLOCK, VALUE_BLOCK), VALUE_BLOCK)
+        local = product(probs_low, pulled[0, :, columns])
+        d_value[0, :, columns] = low(local * slope[0, :, columns].astype(jnp.float32))
+        return carry
+
+    lax.fori_loop(0, d_value.shape[2] // VALUE_BLOCK, body, 0)
+
+
+def attend_back(query, key, value, slope, pulled, docs_row, docs_column, halo):
+    rows, places, _ = query.shape
+    window, wide = value.shape[1:]
+    step = min(KEY_BLOCK, places)
+    return pl.pallas_call(
+        functools.partial(attend_back_kernel, halo * places),
+        out_shape=[
+            jax.ShapeDtypeStruct((rows, places, Z), jnp.float32),
+            jax.ShapeDtypeStruct((rows, window, Z), jnp.float32),
+            jax.ShapeDtypeStruct((rows, window, wide), jnp.bfloat16),
+        ],
+        grid=(rows, window // step),
+        in_specs=[
+            pl.BlockSpec((1, places, Z), lambda r, i: (r, 0, 0)),
+            pl.BlockSpec((1, window, Z), lambda r, i: (r, 0, 0)),
+            pl.BlockSpec((1, window, wide), lambda r, i: (r, 0, 0)),
+            pl.BlockSpec((1, step, wide), lambda r, i: (r, i, 0)),
+            pl.BlockSpec((1, places, wide), lambda r, i: (r, 0, 0)),
+            pl.BlockSpec((1, window, 1), lambda r, i: (r, 0, 0)),
+            pl.BlockSpec((1, 1, places), lambda r, i: (r, 0, 0)),
+        ],
+        out_specs=[
+            pl.BlockSpec((1, places, Z), lambda r, i: (r, 0, 0)),
+            pl.BlockSpec((1, step, Z), lambda r, i: (r, i, 0)),
+            pl.BlockSpec((1, step, wide), lambda r, i: (r, i, 0)),
+        ],
+        scratch_shapes=[
+            pltpu.VMEM((window, places), jnp.float32),
+            pltpu.VMEM((window, places), jnp.float32),
+            pltpu.VMEM((1, places), jnp.float32),
+        ],
+        compiler_params=pltpu.CompilerParams(vmem_limit_bytes=48 * 2**20),
+        cost_estimate=pl.CostEstimate(
+            flops=4 * rows * places * window * (wide + Z),
+            bytes_accessed=rows * (window * wide * 6 + places * wide * 2),
+            transcendentals=rows * places * window,
+        ),
+        name="attend_back",
+    )(query, key, value, slope, pulled, docs_column, docs_row[:, :, halo * places :])
+
+
 def on_device(
     layer_input,
     cotangent,
@@ -811,7 +963,6 @@
     seq_place = lax.axis_index("seq")
     rows, places, width = layer_input.shape
     tokens = rows * places
-    scale = Z ** (-0.5)
     halo = min(-(-(REACH - 1) // places), seq_count - 1)
     window = (halo + 1) * places
 
@@ -842,8 +993,8 @@
     keep = jnp.broadcast_to(keep_own[:, None, :, None], (rows, 1, places, LANES)).reshape(rows, places, LANES)
     alive = jnp.min(keep_row.reshape(rows, seq_count, places), axis=2)
 
-    (value_full, mix_full, head_full), normed_window, start, ema_low = gather_weights(
-        (value_weight, mix_weight, head_weight),
+    (value_full, mix_full, head_full, expand_full), normed_window, start, ema_low = gather_weights(
+        (value_weight, mix_weight, head_weight, expand_weight),
         normed_low,
         keep,
         decay,
@@ -853,16 +1004,16 @@
         halo,
     )
     normed_window = normed_window.reshape(rows * window, width)
-    value_full, mix_full, head_full, expand_late, shrink_late = lax.optimization_barrier(
-        (value_full, mix_full, head_full, expand_weight, shrink_weight)
-    )
-    expand_full = lax.all_gather(expand_late, BOTH, axis=0, tiled=True)
+    value_full, mix_full, head_full, expand_full, shrink_late = lax.optimization_barrier(
+        (value_full, mix_full, head_full, expand_full, shrink_weight)
+    )
     shrink_full = lax.all_gather(shrink_late, BOTH, axis=0, tiled=True)
 
     premix = (ema_low.astype(jnp.float32) + chan_vectors[2] * normed).reshape(tokens, width)
     mixed_low = low(jax.nn.silu(premix))
     value_pre = product(normed_window, value_full)
     values_low = low(jax.nn.silu(value_pre)).reshape(rows, window, V)
+    value_slope = low(silu_slope(value_pre)).reshape(rows, window, V)
     projected = product(mixed_low, mix_full)
     shared_pre = projected[:, :Z]
     reset_pre = projected[:, Z : Z + V]
@@ -877,19 +1028,8 @@
 
     padded_docs = jnp.pad(doc_ids, ((0, 0), (halo * places, 0)), constant_values=-1)
     key_docs = lax.dynamic_slice_in_dim(padded_docs, seq_place * places, window, 1)
-    query_docs = key_docs[:, halo * places :]
-    causal = jnp.arange(window)[None, :] <= jnp.arange(places)[:, None] + halo * places
-    allowed = causal[None] & (query_docs[:, :, None] == key_docs[:, None, :])
-    scores = jnp.einsum("rid,rjd->rij", queries_low, key_window, preferred_element_type=jnp.float32) * scale
-    scores = jnp.where(allowed, scores, NEG_FILL)
-    peak = jnp.max(scores, axis=-1, keepdims=True)
-    expo = jnp.exp(scores - peak)
-    total = jnp.sum(expo, axis=-1, keepdims=True)
-    probs = expo / total
-    probs_low = low(probs)
-    attended = jnp.einsum(
-        "rij,rjv->riv", probs_low, values_low, preferred_element_type=jnp.float32
-    ).reshape(tokens, V)
+    docs_row, docs_column = key_docs[:, None, :], key_docs[:, :, None]
+    attended = attend(queries_low, key_window, values_low, docs_row, docs_column, halo).reshape(tokens, V)
     gated_low = low(reset_gate * attended)
     head_pre = head_base + product(gated_low, head_full)
     candidate = jax.nn.silu(head_pre)
@@ -898,12 +1038,13 @@
     second, second_pull = jax.vjp(scaled_norm, first, chan_vectors[1])
     second_low = low(second)
     expand_pre = product(second_low, expand_full)
-    hidden_low = low(jax.nn.silu(expand_pre))
+    expand_slope = silu_slope(expand_pre)
+    hidden_low, expand_slope = lax.optimization_barrier((low(jax.nn.silu(expand_pre)), expand_slope))
     output = low(first + product(hidden_low, shrink_full)).reshape(rows, places, width)
 
     cot_low = cotangent.reshape(tokens, width)
     shrink_part = low(transposed(hidden_low, cot_low))
-    d_expand = low(against(cot_low, shrink_full) * silu_slope(expand_pre))
+    d_expand = low(against(cot_low, shrink_full) * expand_slope)
     expand_part = low(transposed(second_low, d_expand))
     d_first_norm, d_gain_two = second_pull(against(d_expand, expand_full))
     d_first = cot_low.astype(jnp.float32) + d_first_norm
@@ -915,18 +1056,15 @@
     d_gated = against(d_head_low, head_full)
     d_reset = d_gated * attended * silu_slope(reset_pre)
     d_attended = low(d_gated * reset_gate).reshape(rows, places, V)
-    d_probs = jnp.einsum("riv,rjv->rij", d_attended, values_low, preferred_element_type=jnp.float32)
-    balance = jnp.sum(probs * d_probs, axis=-1, keepdims=True)
-    d_scores = low(probs * (d_probs - balance))
-    d_queries = scale * jnp.einsum("rij,rjd->rid", d_scores, key_window, preferred_element_type=jnp.float32)
-    key_term = scale * jnp.einsum("rij,rid->rjd", d_scores, queries_low, preferred_element_type=jnp.float32)
+    d_queries, key_term, d_value_pre = attend_back(
+        queries_low, key_window, values_low, value_slope, d_attended, docs_row, docs_column, halo
+    )
+    d_value_pre = d_value_pre.reshape(rows * window, V)
     d_keys = key_term[:, halo * places :]
     for by in range(1, halo + 1):
         begin = (halo - by) * places
         d_keys = d_keys + shift_seq(low(key_term[:, begin : begin + places]), -by).astype(jnp.float32)
     d_keys32 = low(d_keys).astype(jnp.float32).reshape(tokens, Z)
-    d_values = jnp.einsum("rij,riv->rjv", probs_low, d_attended, preferred_element_type=jnp.float32)
-    d_value_pre = low(d_values.reshape(rows * window, V) * silu_slope(value_pre))
     value_part = low(transposed(normed_window, d_value_pre))
     value_term = against(d_value_pre, value_full).reshape(rows, halo + 1, places, width)
     terms = low(value_term[:, :halo])

time: 859 us -> 808 us (0.941)
  Pallas kernels: 381 us -> 452 us
  waiting for transfers between devices: 41.8 us -> 0.03 us
  matrix products: 284 us -> 243 us
  other arithmetic: 78.5 us -> 56.7 us
  local copies, waits for them, and re-layouts: 29.7 us -> 17.9 us
    pallas_call x0 -> x2, Pallas kernels: none -> 45.5 us  [the longest x1 32.5 us: attend_back(): pl.pallas_call(functools.partial(attend_back_kernel, halo * places), out_...]
    dot_general x5 -> x0, matrix products: 44.5 us -> none  [the longest x1 15.1 us: on_device(): jnp.einsum('rij,riv->rjv', probs_low, d_attended, preferred_element_type=...]
    all_gather x1, waiting for transfers between devices: 41.8 us -> 0.01 us  [on_device(): shrink_full = lax.all_gather(shrink_late, BOTH, axis=0, tiled=True)]
    pallas_call x1, Pallas kernels: 157 us -> 194 us  [gather_weights(): pl.pallas_call(functools.partial(gather_kernel, sizes, count, halo), out_...]
    convert_element_type x7 -> x5, other arithmetic: 35.9 us -> 15.3 us  [low(): return values.astype(jnp.bfloat16)]
    pallas_call x1, Pallas kernels: 224 us -> 212 us  [scatter_grads(): pl.pallas_call(functools.partial(scatter_kernel, sizes, count), out_shape...]
    unnamed x162 -> x148, local copies, waits for them, and re-layouts: 19.3 us -> 10.8 us
  transfers between devices with their start and end apart: 8 -> 7, of which waited for: 1 -> 0; matrix products, arithmetic and copies ran while one was open for 21% -> 23% of each run, Pallas kernels for 0% -> 2%
where the time goes in v3:
time: 808 us; the launch traced here: 800 us
  Pallas kernels  452 us (56%)
  matrix products  243 us (30%)
  other arithmetic  56.7 us (7%)
  local copies, waits for them, and re-layouts  17.9 us (2%)
  between operations  15.6 us (2%)
  starting transfers between devices  15.2 us (2%)
    pallas_call x1, Pallas kernels, scatter_grads(): pl.pallas_call(functools.partial(scatter_kernel, sizes, count), out_shape...  212 us
    pallas_call x1, Pallas kernels, gather_weights(): pl.pallas_call(functools.partial(gather_kernel, sizes, count, halo), out_...  194 us
    dot_general x5, matrix products, product(): return jnp.dot(left, right, preferred_element_type=jnp.float32)  87.5 us
    dot_general x5, matrix products, against(): lax.dot_general(left, right, (((1,), (1,)), ((), ())), preferred_element_...  84.1 us
    dot_general x5, matrix products, transposed(): lax.dot_general(left, right, (((0,), (0,)), ((), ())), preferred_element_...  71.4 us
    pallas_call x1, Pallas kernels, attend_back(): pl.pallas_call(functools.partial(attend_back_kernel, halo * places), out_...  32.5 us
  transfers between devices with their start and end apart: 7, of which 0 were waited for; matrix products, arithmetic and copies ran while one was open for 23% of the time, Pallas kernels for 2%

profile of v3, /device:TPU:0, one launch (start us, length us, event | category | flops | bytes accessed | tf_op | source)
XLA Modules:
  0.0 800.3 jit_solution(7149267063945031290)
XLA Ops:
  7.3 0.9 convert_subtract_fusion.1
  8.2 1.9 convert_reduce_fusion
  10.2 2.3 fusion.33
  12.9 2.7 fusion.27
  16.4 194.2 %gather_weights.1 = (bf16[4,2,2,2,32,2048]{5,4,3,2,1,0:T(8,128)(2,1)}, bf16[4,2,2,2,32,4224]{5,4,3,2,1,0:T(8,128)(2,1)}, bf16[4,2,2,2,64,1024]{5,4,3,2,1,0:T(8,1...) custom-call(bf16[32,2048]{1,0:T(8,128)(2,1)S(1)} %copy-done.16, ...), custom_call_target="tpu_custom_call" | custom-call | tf_op jit(solution)/shard_map/gather_weights/pallas_call | solution.py:485
  210.7 1.1 multiply_add_fusion
  211.8 1.1 fusion.18
  212.9 1.3 copy-done.65
  214.2 2.2 copy-done.66
  216.5 12.2 %fusion.73 = f32[1024,4224]{1,0:T(8,128)} fusion(bf16[1024,1024]{1,0:T(8,128)(2,1)S(1)} %fusion.18, bf16[1024,4224]{1,0:T(8,128)(2,1)S(1)} %bitcast.286), kind=kOutput, calls=%fused_computation.170 | convolution fusion | flops 8858370048 | bytes 28049408 | tf_op jit(solution)/shard_map/dot_general | solution.py:184
  228.7 1.3 multiply_convert_fusion.7
  230.0 8.3 %collective-permute-start = (bf16[2,512,128]{2,1,0:T(8,128)(2,1)S(1)}, bf16[2,512,128]{2,1,0:T(8,128)(2,1)S(1)}, u32[]{:S(2)}, u32[]{:S(2)}) collective-permute-start(bf16[2,512,128]{2,1,0:T(8,128)(2,1)S(1)} %bitcast.263), channel_id=1, source_target_pairs={{0,2},{1,3},{4,6},{5,7},{8,10},{9,11},{12,14},{13,15},{16,18},{17,... | collective-permute-start | bytes 786440 | tf_op jit(solution)/shard_map/ppermute | solution.py:202
  238.3 1.5 collective-permute-start.1
  239.9 28.6 %multiply_convert_fusion = (bf16[3072,2048]{1,0:T(8,128)(2,1)}, bf16[3072,2048]{1,0:T(8,128)(2,1)}) fusion(bf16[3072,1024]{1,0:T(8,128)(2,1)} %bitcast.291, bf16[1024,2048]{1,0:T(8,128)(2,1)} %bitcast.293), kind=kOutput, calls=%fused_computation | convolution fusion | flops 12947816448 | bytes 35651584 | tf_op jit(solution)/shard_map/dot_general | solution.py:184
  270.0 13.0 %attend.1 = f32[2,512,2048]{2,1,0:T(8,128)S(1)} custom-call(bf16[2,512,128]{2,1,0:T(8,128)(2,1)S(1)} %bitcast.251, bf16[2,1536,128]{2,1,0:T(8,128)(2,1)S(1)} %pad_maximum_fusion.3.key, bf16[2,1536,2048]{2,1,0:T(8,128)(2,1)} %bitcast.254, s32[2,1,1536]{2,1,0:T(1,128)S(1)} %broadcast_in_dim.20.key_docs, s32[2,512,1]{2,1,0:T(8,128)S(1)} %slice.139.query_docs), custom_call_target="tpu_custom_call" | custom-call | flops 5704253440 | bytes 20971520 | tf_op jit(solution)/shard_map/attend/pallas_call | solution.py:825
  283.1 8.9 %fusion.3 = bf16[1024,2048]{1,0:T(8,128)(2,1)S(1)} fusion(f32[2,512,2048]{2,1,0:T(8,128)S(1)} %attend.1, f32[1024,4224]{1,0:T(8,128)} %fusion.73), kind=kLoop, calls=%fused_computation.14 | loop fusion | flops 12582912 | bytes 20971520 | tf_op jit(solution)/shard_map/convert_element_type | solution.py:196
  292.0 12.6 %fusion.68 = (f32[1024]{0:T(1024)S(1)}, f32[1024,1024]{1,0:T(8,128)S(1)}, f32[1024,1024]{1,0:T(8,128)}) fusion(f32[1024,4224]{1,0:T(8,128)} %fusion.73, bf16[2,512,1024]{2,1,0:T(8,128)(2,1)S(1)} %copy-done.19, bf16[1024,2048]{1,0:T(8,128)(2,1)S(1)} %fusion.3, bf16[2048,1024]{1,0:T(8,128)(2,1)} %bitcast.295), kind=kOutput, calls=%fused_computation.165 | convolution fusion | flops 4308597760 | bytes 27267072 | tf_op jit(solution)/shard_map/dot_general | solution.py:184
  305.2 21.7 %add_multiply_fusion = (f32[1024,4096]{1,0:T(8,128)}, bf16[1024,4096]{1,0:T(8,128)(2,1)}) fusion(bf16[1024,4096]{1,0:T(8,128)(2,1)} %bitcast.289, f32[1024,1024]{1,0:T(8,128)S(1)} %get-tuple-element.86, f32[1024]{0:T(1024)S(1)} %bitcast.272, f32[1024]{0:T(1024)S(1)} %fusion.56, f32[1024]{0:T(1024)S(1)} %broadcast_multiply_fusion), kind=kOutput, calls=%fused_computation.5 | convolution fusion | flops 8631877632 | bytes 37761024 | tf_op jit(solution)/shard_map/dot_general | solution.py:184
  326.9 14.8 %convolution_convert_fusion.2 = bf16[4096,1024]{1,0:T(8,128)(2,1)} fusion(bf16[1024,4096]{1,0:T(8,128)(2,1)} %get-tuple-element.57, bf16[1024,1024]{1,0:T(8,128)(2,1)S(1)} %bitcast.262), kind=kOutput, calls=%fused_computation.21 | convolution fusion | flops 8594128896 | bytes 18874368 | tf_op jit(solution)/shard_map/dot_general | solution.py:192
  341.8 17.3 %fusion = bf16[1024,4096]{1,0:T(8,128)(2,1)} fusion(f32[1024,4096]{1,0:T(8,128)} %get-tuple-element.59, bf16[4096,1024]{1,0:T(8,128)(2,1)} %all-gather.2.cloned.1.call-done, bf16[1024,1024]{1,0:T(8,128)(2,1)} %bitcast.261), kind=kOutput, calls=%fused_computation.4 | convolution fusion | flops 8598323200 | bytes 35651584 | tf_op jit(solution)/shard_map/dot_general | solution.py:188
  359.1 16.6 %multiply_reduce_fusion = (f32[1024]{0:T(1024)}, f32[1024]{0:T(1024)S(1)}, f32[1024,1024]{1,0:T(8,128)}) fusion(f32[1024,1024]{1,0:T(8,128)S(1)} %copy-done.25, f32[1024]{0:T(1024)S(1)} %fusion.56, f32[1024]{0:T(1024)S(1)} %broadcast_multiply_fusion, f32[1024]{0:T(1024)S(1)} %bitcast.273, bf16[1024,4096]{1,0:T(8,128)(2,1)} %fusion, ...), kind=kOutput, calls=%fused_computation.62 | convolution fusion | flops 8597272576 | bytes 25186304 | tf_op jit(solution)/shard_map/dot_general | solution.py:188
  375.7 15.2 %convolution_convert_fusion.1 = bf16[1024,4096]{1,0:T(8,128)(2,1)} fusion(bf16[1024,4096]{1,0:T(8,128)(2,1)} %fusion, f32[1024,1024]{1,0:T(8,128)S(1)} %copy-done.25, f32[1024]{0:T(1024)S(1)} %bitcast.274, f32[1024]{0:T(1024)S(1)} %fusion.56, f32[1024]{0:T(1024)S(1)} %broadcast_multiply_fusion), kind=kOutput, calls=%fused_computation.20 | convolution fusion | flops 8598323200 | bytes 20983808 | tf_op jit(solution)/shard_map/dot_general | solution.py:192
  391.0 1.8 fusion.67
  392.8 1.0 copy-done.34
  394.4 8.9 %multiply_convert_fusion.4 = (bf16[1024,1024]{1,0:T(8,128)(2,1)}, bf16[1024,1024]{1,0:T(8,128)(2,1)}, f32[1024,1024]{1,0:T(8,128)}) fusion(bf16[2,512,1024]{2,1,0:T(8,128)(2,1)S(1)} %copy-done.20, f32[1024,1024]{1,0:T(8,128)S(1)} %copy-done.34, f32[1024,1024]{1,0:T(8,128)S(1)} %get-tuple-element.84, f32[1024]{0:T(1024)S(1)} %negate_multiply_fusion, ...), kind=kLoop, calls=%fused_computation.63 | loop fusion | flops 26214400 | bytes 25169920 | tf_op jit(solution)/shard_map/convert.5
  403.3 13.2 %fusion.5 = (bf16[1024,2048]{1,0:T(8,128)(2,1)}, bf16[1024,2048]{1,0:T(8,128)(2,1)}) fusion(f32[2,512,2048]{2,1,0:T(8,128)S(1)} %bitcast.250, f32[1024,4224]{1,0:T(8,128)} %fusion.73, bf16[1024,1024]{1,0:T(8,128)(2,1)} %get-tuple-element.90, bf16[2048,1024]{1,0:T(8,128)(2,1)} %bitcast.296), kind=kOutput, calls=%fused_computation.16 | convolution fusion | flops 4322230272 | bytes 31457280 | tf_op jit(solution)/shard_map/dot_general | solution.py:188
  416.6 32.5 %attend_back.1 = (f32[2,512,128]{2,1,0:T(8,128)S(1)}, f32[2,1536,128]{2,1,0:T(8,128)S(1)}, bf16[2,1536,2048]{2,1,0:T(8,128)(2,1)}) custom-call(bf16[2,512,128]{2,1,0:T(8,128)(2,1)S(1)} %bitcast.252, bf16[2,1536,128]{2,1,0:T(8,128)(2,1)S(1)} %copy-done.4, bf16[2,1536,2048]{2,1,0:T(8,128)(2,1)} %bitcast.255, bf16[2,1536,2048]{2,1,0:T(8,128)(2,1)} %bitcast.297, ...), custom_call_target="tpu_custom_call" | custom-call | flops 13690208256 | bytes 41943040 | tf_op jit(solution)/shard_map/attend_back/pallas_call | solution.py:910
  449.2 1.3 collective-permute-start.2
  450.5 1.3 collective-permute-start.3
  451.8 19.2 %fusion.72 = (bf16[2,3,512,1024]{3,2,0,1:T(8,128)(2,1)S(1)}, f32[2,3,512,1024]{3,2,0,1:T(8,128)}) fusion(bf16[1024,2048]{1,0:T(8,128)(2,1)} %bitcast.294, bf16[2,3,512,2048]{3,2,1,0:T(8,128)(2,1)} %bitcast.298), kind=kOutput, calls=%fused_computation.168 | convolution fusion | flops 12888047616 | bytes 35651584 | tf_op jit(solution)/shard_map/dot_general | solution.py:188
  471.0 2.6 slice_bitcast_fusion.2
  473.6 1.4 collective-permute-start.4
  475.0 1.3 collective-permute-start.5
  476.3 19.9 %convolution_convert_fusion.3 = bf16[1024,2048]{1,0:T(8,128)(2,1)} fusion(bf16[3072,1024]{1,0:T(8,128)(2,1)} %bitcast.292, bf16[3072,2048]{1,0:T(8,128)(2,1)} %bitcast.299), kind=kOutput, calls=%fused_computation.73 | convolution fusion | flops 12886999040 | bytes 23068672 | tf_op jit(solution)/shard_map/dot_general | solution.py:192
  496.2 12.3 %add_convert_fusion = bf16[1024,1024]{1,0:T(8,128)(2,1)} fusion(f32[1024,1024]{1,0:T(8,128)S(1)} %copy-done.27, bf16[1024,4096]{1,0:T(8,128)(2,1)} %get-tuple-element.57, bf16[4096,1024]{1,0:T(8,128)(2,1)S(1)} %bitcast.288), kind=kOutput, calls=%fused_computation.67 | convolution fusion | flops 8592031744 | bytes 23068672 | tf_op jit(solution)/shard_map/dot_general | solution.py:184
  508.6 6.3 convolution_convert_fusion.4
  515.2 1.4 fusion.40
  516.7 17.7 %fusion.13 = (f32[1024]{0:T(1024)S(1)}, f32[1024,1024]{1,0:T(8,128)}) fusion(f32[2,512,1024]{2,1,0:T(8,128)} %get-tuple-element.103, f32[2,512,1024]{2,1,0:T(8,128)} %copy-done.28, bf16[1024,4224]{1,0:T(8,128)(2,1)} %bitcast.285, bf16[1024,1024]{1,0:T(8,128)(2,1)} %get-tuple-element.89, bf16[1024,1024]{1,0:T(8,128)(2,1)} %get-tuple-element.90, ...), kind=kOutput, calls=%fused_computation.33 | convolution fusion | flops 8903457792 | bytes 29888512 | tf_op jit(solution)/shard_map/dot_general | solution.py:188
  534.4 4.0 bitcast_convert_fusion.refs_7_
  538.4 15.2 %convolution_convert_fusion = bf16[1024,4224]{1,0:T(8,128)(2,1)} fusion(bf16[1024,1024]{1,0:T(8,128)(2,1)S(1)} %copy-done.36, bf16[1024,1024]{1,0:T(8,128)(2,1)} %get-tuple-element.89, bf16[1024,1024]{1,0:T(8,128)(2,1)} %get-tuple-element.90, bf16[1024,2048]{1,0:T(8,128)(2,1)} %get-tuple-element.91, bf16[1024,128]{1,0:T(8,128)(2,1)S(1)} %get-tuple-element.96), kind=kOutput, calls=%fused_computation.10 | convolution fusion | flops 8897298432 | bytes 19398656 | tf_op jit(solution)/shard_map/dot_general | solution.py:192
  553.7 5.8 fusion.28
  559.4 1.3 concatenate.14.refs_5_
  560.8 212.2 %scatter_grads.1 = (f32[128,1024]{1,0:T(8,128)}, f32[32,4096]{1,0:T(8,128)}, f32[64,1024]{1,0:T(8,128)}, f32[32,2048]{1,0:T(8,128)}, f32[32,4224]{1,0:T(8,128)},...) custom-call(bf16[4,2,2,2,128,1024]{5,4,3,2,1,0:T(8,128)(2,1)} %bitcast.257, ...), custom_call_target="tpu_custom_call" | custom-call | tf_op jit(solution)/shard_map/scatter_grads/pallas_call | solution.py:745
  773.0 0.9 fusion.54
  775.6 1.3 slice_reduce_fusion
  777.8 4.3 fusion.34
  782.1 0.9 copy-done.23
  783.7 4.8 fusion.32
  (202 shorter events, 12.1 us)
Async XLA Ops:
  7.2 334.5 %all-gather.2.cloned.1.call-start = ((), (), s32[]{:S(2)}) async-start(), calls=%async_computation | async-start | bytes 8650752 | tf_op jit(solution)/shard_map/all_gather | solution.py:1010
  10.2 200.5 %copy-start.49 = (f32[2,512]{1,0:T(2,128)}, f32[2,512]{1,0:T(2,128)S(1)}, u32[]{:S(2)}) copy-start(f32[2,512]{1,0:T(2,128)S(1)} %broadcast_multiply_fusion.3) | copy-start | bytes 12292
  12.5 198.2 %copy-start.51 = (f32[2,512]{1,0:T(2,128)}, f32[2,512]{1,0:T(2,128)S(1)}, u32[]{:S(2)}) copy-start(f32[2,512]{1,0:T(2,128)S(1)} %add_rsqrt_fusion) | copy-start | bytes 12292
  12.5 198.1 %copy-start.53 = (f32[1,1024]{1,0:T(1,128)}, f32[1,1024]{1,0:T(1,128)S(1)}, u32[]{:S(2)}) copy-start(f32[1,1024]{1,0:T(1,128)S(1)} %get-tuple-element.112) | copy-start | bytes 12292
  12.5 198.1 %copy-start.56 = (f32[1,1024]{1,0:T(1,128)}, f32[1,1024]{1,0:T(1,128)S(1)}, u32[]{:S(2)}) copy-start(f32[1,1024]{1,0:T(1,128)S(1)} %get-tuple-element.113) | copy-start | bytes 12292
  15.6 196.2 %copy-start.1 = (bf16[2,512,1024]{2,1,0:T(8,128)(2,1)}, bf16[2,512,1024]{2,1,0:T(8,128)(2,1)S(1)}, u32[]{:S(2)}) copy-start(bf16[2,512,1024]{2,1,0:T(8,128)(2,1)S(1)} %get-tuple-element.104.refs_4_.refs_6_) | copy-start | bytes 6291460
  16.1 195.7 %copy-start.7 = (f32[3,16,1024]{2,1,0:T(8,128)}, f32[3,16,1024]{2,1,0:T(8,128)S(1)}, u32[]{:S(2)}) copy-start(f32[3,16,1024]{2,1,0:T(8,128)S(1)} %pad_maximum_fusion.4.refs_9_.refs_13_) | copy-start | bytes 589828
  16.3 195.5 %copy-start.2 = (f32[2,512,128]{2,1,0:T(8,128)}, f32[2,512,128]{2,1,0:T(8,128)S(1)}, u32[]{:S(2)}) copy-start(f32[2,512,128]{2,1,0:T(8,128)S(1)} %reshape.264.refs_5_.refs_8_) | copy-start | bytes 1572868
  211.8 16.9 %copy-start.28 = (f32[2,512,1024]{2,1,0:T(8,128)}, f32[2,512,1024]{2,1,0:T(8,128)S(1)}, u32[]{:S(2)}) copy-start(f32[2,512,1024]{2,1,0:T(8,128)S(1)} %multiply_add_fusion) | copy-start | bytes 12582916
  214.2 14.5 %copy-start.35 = (bf16[1024,1024]{1,0:T(8,128)(2,1)}, bf16[1024,1024]{1,0:T(8,128)(2,1)S(1)}, u32[]{:S(2)}) copy-start(bf16[1024,1024]{1,0:T(8,128)(2,1)S(1)} %fusion.18) | copy-start | bytes 6291460
  216.4 12.2 %copy-start.60 = (f32[128]{0:T(128)}, f32[128]{0:T(128)S(1)}, u32[]{:S(2)}) copy-start(f32[128]{0:T(128)S(1)} %get-tuple-element.114) | copy-start | bytes 1540
  216.4 12.2 %copy-start.62 = (f32[128]{0:T(128)}, f32[128]{0:T(128)S(1)}, u32[]{:S(2)}) copy-start(f32[128]{0:T(128)S(1)} %get-tuple-element.115) | copy-start | bytes 1540
  216.5 23.4 %copy-start.55 = (s32[2,2048]{1,0:T(2,128)S(1)}, s32[2,2048]{1,0:T(2,128)}, u32[]{:S(2)}) copy-start(s32[2,2048]{1,0:T(2,128)} %param.17) | copy-start | bytes 49156
  230.0 40.0 %copy-start.10 = (bf16[1024,128]{1,0:T(8,128)(2,1)}, bf16[1024,128]{1,0:T(8,128)(2,1)S(1)}, u32[]{:S(2)}) copy-start(bf16[1024,128]{1,0:T(8,128)(2,1)S(1)} %get-tuple-element.98) | copy-start | bytes 786436
  230.0 40.0 %collective-permute-start = (bf16[2,512,128]{2,1,0:T(8,128)(2,1)S(1)}, bf16[2,512,128]{2,1,0:T(8,128)(2,1)S(1)}, u32[]{:S(2)}, u32[]{:S(2)}) collective-permute-start(bf16[2,512,128]{2,1,0:T(8,128)(2,1)S(1)} %bitcast.263), channel_id=1, source_target_pairs={{0,2},{1,3},{4,6},{5,7},{8,10},{9,11},{12,14},{13,15},{16,18},{17,... | collective-permute-start | bytes 786440 | tf_op jit(solution)/shard_map/ppermute | solution.py:202
  238.3 31.6 %collective-permute-start.1 = (bf16[2,512,128]{2,1,0:T(8,128)(2,1)S(1)}, bf16[2,512,128]{2,1,0:T(8,128)(2,1)S(1)}, u32[]{:S(2)}, u32[]{:S(2)}) collective-permute-start(bf16[2,512,128]{2,1,0:T(8,128)(2,1)S(1)} %bitcast.264), channel_id=1, source_target_pairs={{0,1},{1,2},{2,3},{4,5},{5,6},{6,7},{8,9},{9,10},{10,11},{12,13},{... | collective-permute-start | bytes 786440 | tf_op jit(solution)/shard_map/ppermute | solution.py:202
  270.0 13.0 %copy-start.3 = (bf16[2,1536,128]{2,1,0:T(8,128)(2,1)}, bf16[2,1536,128]{2,1,0:T(8,128)(2,1)S(1)}, u32[]{:S(2)}) copy-start(bf16[2,1536,128]{2,1,0:T(8,128)(2,1)S(1)} %pad_maximum_fusion.3.key) | copy-start | bytes 2359300
  283.0 8.9 %copy-start = (f32[2,512,2048]{2,1,0:T(8,128)}, f32[2,512,2048]{2,1,0:T(8,128)S(1)}, u32[]{:S(2)}) copy-start(f32[2,512,2048]{2,1,0:T(8,128)S(1)} %attend.1) | copy-start | bytes 25165828
  283.0 8.9 %copy-start.19 = (bf16[2,512,1024]{2,1,0:T(8,128)(2,1)S(1)}, bf16[2,512,1024]{2,1,0:T(8,128)(2,1)}, u32[]{:S(2)}) copy-start(bf16[2,512,1024]{2,1,0:T(8,128)(2,1)} %param.15) | copy-start | bytes 6291460
  292.0 12.7 %copy-start.31 = (bf16[1024,2048]{1,0:T(8,128)(2,1)}, bf16[1024,2048]{1,0:T(8,128)(2,1)S(1)}, u32[]{:S(2)}) copy-start(bf16[1024,2048]{1,0:T(8,128)(2,1)S(1)} %fusion.3) | copy-start | bytes 12582916
  304.6 22.3 %copy-start.24 = (f32[1024,1024]{1,0:T(8,128)}, f32[1024,1024]{1,0:T(8,128)S(1)}, u32[]{:S(2)}) copy-start(f32[1024,1024]{1,0:T(8,128)S(1)} %get-tuple-element.86) | copy-start | bytes 12582916
  305.2 21.7 %copy-start.37 = (bf16[2,512,1024]{2,1,0:T(8,128)(2,1)S(1)}, bf16[2,512,1024]{2,1,0:T(8,128)(2,1)}, u32[]{:S(2)}) copy-start(bf16[2,512,1024]{2,1,0:T(8,128)(2,1)} %param.16) | copy-start | bytes 6291460
  341.8 17.3 %copy-start.25 = (f32[1024,1024]{1,0:T(8,128)S(1)}, f32[1024,1024]{1,0:T(8,128)}, u32[]{:S(2)}) copy-start(f32[1024,1024]{1,0:T(8,128)} %copy-done.24) | copy-start | bytes 12582916
  375.7 15.2 %copy-start.26 = (f32[1024,1024]{1,0:T(8,128)S(1)}, f32[1024,1024]{1,0:T(8,128)}, u32[]{:S(2)}) copy-start(f32[1024,1024]{1,0:T(8,128)} %copy-done.24) | copy-start | bytes 12582916
  375.7 15.2 %copy-start.33 = (f32[1024,1024]{1,0:T(8,128)S(1)}, f32[1024,1024]{1,0:T(8,128)}, u32[]{:S(2)}) copy-start(f32[1024,1024]{1,0:T(8,128)} %get-tuple-element.118) | copy-start | bytes 12582916
  391.0 12.3 %slice-start = ((s8[8388608]{0:T(1024)(128)(4,1)}), s8[4194304]{0:T(1024)(128)(4,1)S(1)}, s32[]{:S(2)}) async-start(s8[8388608]{0:T(1024)(128)(4,1)} %bitcast.249), calls=%async_computation.1 | async-start | bytes 8388608
  394.4 8.9 %slice-start.1 = ((s8[8388608]{0:T(1024)(128)(4,1)}), s8[4194304]{0:T(1024)(128)(4,1)S(1)}, s32[]{:S(2)}) async-start(s8[8388608]{0:T(1024)(128)(4,1)} %bitcast.249), calls=%async_computation.2 | async-start | bytes 8388608
  403.3 13.3 %copy-start.4 = (bf16[2,1536,128]{2,1,0:T(8,128)(2,1)S(1)}, bf16[2,1536,128]{2,1,0:T(8,128)(2,1)}, u32[]{:S(2)}) copy-start(bf16[2,1536,128]{2,1,0:T(8,128)(2,1)} %copy-done.3) | copy-start | bytes 2359300
  403.3 13.2 %copy-start.11 = (bf16[1024,128]{1,0:T(8,128)(2,1)S(1)}, bf16[1024,128]{1,0:T(8,128)(2,1)}, u32[]{:S(2)}) copy-start(bf16[1024,128]{1,0:T(8,128)(2,1)} %copy-done.10) | copy-start | bytes 786436
  449.0 22.0 %copy-start.5 = (f32[2,512,128]{2,1,0:T(8,128)}, f32[2,512,128]{2,1,0:T(8,128)S(1)}, u32[]{:S(2)}) copy-start(f32[2,512,128]{2,1,0:T(8,128)S(1)} %get-tuple-element.60) | copy-start | bytes 1572868
  449.2 65.9 %collective-permute-start.2 = (bf16[2,512,128]{2,1,0:T(8,128)(2,1)S(1)}, bf16[2,512,128]{2,1,0:T(8,128)(2,1)S(1)}, u32[]{:S(2)}, u32[]{:S(2)}) collective-permute-start(bf16[2,512,128]{2,1,0:T(8,128)(2,1)S(1)} %get-tuple-element.105), channel_id=1, source_target_pairs={{1,0},{2,1},{3,2},{5,4},{6,5},{7,6},{9,8},{10,9},{11,10},{13,12},{... | collective-permute-start | bytes 786440 | tf_op jit(solution)/shard_map/ppermute | solution.py:202
  450.5 64.6 %collective-permute-start.3 = (bf16[2,512,128]{2,1,0:T(8,128)(2,1)S(1)}, bf16[2,512,128]{2,1,0:T(8,128)(2,1)S(1)}, u32[]{:S(2)}, u32[]{:S(2)}) collective-permute-start(bf16[2,512,128]{2,1,0:T(8,128)(2,1)S(1)} %get-tuple-element.106), channel_id=1, source_target_pairs={{2,0},{3,1},{6,4},{7,5},{10,8},{11,9},{14,12},{15,13},{18,16},{19,... | collective-permute-start | bytes 786440 | tf_op jit(solution)/shard_map/ppermute | solution.py:202
  471.0 25.2 %slice-start.2 = ((s8[8388608]{0:T(1024)(128)(4,1)}), s8[4194304]{0:T(1024)(128)(4,1)S(1)}, s32[]{:S(2)}) async-start(s8[8388608]{0:T(1024)(128)(4,1)} %bitcast.287), calls=%async_computation.3 | async-start | bytes 8388608
  473.6 80.0 %collective-permute-start.4 = (bf16[2,512,1024]{2,1,0:T(8,128)(2,1)}, bf16[2,512,1024]{2,1,0:T(8,128)(2,1)}, u32[]{:S(2)}, u32[]{:S(2)}) collective-permute-start(bf16[2,512,1024]{2,1,0:T(8,128)(2,1)} %get-tuple-element.101), channel_id=1, source_target_pairs={{1,0},{2,1},{3,2},{5,4},{6,5},{7,6},{9,8},{10,9},{11,10},{13,12},{... | collective-permute-start | bytes 6291464 | tf_op jit(solution)/shard_map/ppermute | solution.py:202
  475.0 78.6 %collective-permute-start.5 = (bf16[2,512,1024]{2,1,0:T(8,128)(2,1)}, bf16[2,512,1024]{2,1,0:T(8,128)(2,1)}, u32[]{:S(2)}, u32[]{:S(2)}) collective-permute-start(bf16[2,512,1024]{2,1,0:T(8,128)(2,1)} %get-tuple-element.102), channel_id=1, source_target_pairs={{2,0},{3,1},{6,4},{7,5},{10,8},{11,9},{14,12},{15,13},{18,16},{19,... | collective-permute-start | bytes 6291464 | tf_op jit(solution)/shard_map/ppermute | solution.py:202
  476.3 19.9 %copy-start.27 = (f32[1024,1024]{1,0:T(8,128)S(1)}, f32[1024,1024]{1,0:T(8,128)}, u32[]{:S(2)}) copy-start(f32[1024,1024]{1,0:T(8,128)} %copy-done.24) | copy-start | bytes 12582916
  476.3 19.9 %slice-start.3 = ((s8[8388608]{0:T(1024)(128)(4,1)}), s8[4194304]{0:T(1024)(128)(4,1)S(1)}, s32[]{:S(2)}) async-start(s8[8388608]{0:T(1024)(128)(4,1)} %bitcast.287), calls=%async_computation.4 | async-start | bytes 8388608
  496.2 12.3 %copy-start.32 = (bf16[1024,2048]{1,0:T(8,128)(2,1)S(1)}, bf16[1024,2048]{1,0:T(8,128)(2,1)}, u32[]{:S(2)}) copy-start(bf16[1024,2048]{1,0:T(8,128)(2,1)} %copy-done.31) | copy-start | bytes 12582916
  496.2 12.3 %copy-start.39 = (bf16[1024,1024]{1,0:T(8,128)(2,1)S(1)}, bf16[1024,1024]{1,0:T(8,128)(2,1)}, u32[]{:S(2)}) copy-start(bf16[1024,1024]{1,0:T(8,128)(2,1)} %get-tuple-element.90) | copy-start | bytes 6291460
  538.4 15.2 %copy-start.21 = (bf16[2,512,1024]{2,1,0:T(8,128)(2,1)S(1)}, bf16[2,512,1024]{2,1,0:T(8,128)(2,1)}, u32[]{:S(2)}) copy-start(bf16[2,512,1024]{2,1,0:T(8,128)(2,1)} %param.15) | copy-start | bytes 6291460
  538.4 15.2 %copy-start.29 = (f32[1024,1024]{1,0:T(8,128)S(1)}, f32[1024,1024]{1,0:T(8,128)}, u32[]{:S(2)}) copy-start(f32[1024,1024]{1,0:T(8,128)} %get-tuple-element.122) | copy-start | bytes 12582916
  538.4 15.2 %copy-start.50 = (f32[2,512]{1,0:T(2,128)S(1)}, f32[2,512]{1,0:T(2,128)}, u32[]{:S(2)}) copy-start(f32[2,512]{1,0:T(2,128)} %copy-done.49) | copy-start | bytes 12292
  538.4 15.2 %copy-start.52 = (f32[2,512]{1,0:T(2,128)S(1)}, f32[2,512]{1,0:T(2,128)}, u32[]{:S(2)}) copy-start(f32[2,512]{1,0:T(2,128)} %copy-done.51) | copy-start | bytes 12292
  538.4 15.2 %copy-start.57 = (f32[1,1024]{1,0:T(1,128)S(1)}, f32[1,1024]{1,0:T(1,128)}, u32[]{:S(2)}) copy-start(f32[1,1024]{1,0:T(1,128)} %copy-done.56) | copy-start | bytes 12292
  560.7 212.2 %copy-start.9 = (f32[16,1024]{1,0:T(8,128)S(1)}, f32[16,1024]{1,0:T(8,128)}, u32[]{:S(2)}) copy-start(f32[16,1024]{1,0:T(8,128)} %copy-done.8) | copy-start | bytes 196612
  560.7 212.2 %copy-start.41 = (f32[2,1024,16]{1,2,0:T(8,128)S(1)}, f32[2,1024,16]{1,2,0:T(8,128)}, u32[]{:S(2)}) copy-start(f32[2,1024,16]{1,2,0:T(8,128)} %param.25) | copy-start | bytes 393220
  560.7 212.3 %copy-start.46 = (f32[2,1024,16]{1,2,0:T(8,128)S(1)}, f32[2,1024,16]{1,2,0:T(8,128)}, u32[]{:S(2)}) copy-start(f32[2,1024,16]{1,2,0:T(8,128)} %param.26) | copy-start | bytes 393220
  560.7 217.0 %copy-start.54 = (f32[1,1024]{1,0:T(1,128)S(1)}, f32[1,1024]{1,0:T(1,128)}, u32[]{:S(2)}) copy-start(f32[1,1024]{1,0:T(1,128)} %copy-done.53) | copy-start | bytes 12292
  (30 other events, 145.5 us)
Sparse Core Ops, SparseCore 0:
  240.0 76.6 all-gather.1

commit v4 on v3

--- a/solution.py
+++ b/solution.py
@@ -16,6 +16,7 @@
 EMA_STEP = 16
 FORWARD_WIDTH = 512
 BACKWARD_WIDTH = 256
+HOST_TILE = 512
 
 
 def lanes_at(base, group):
@@ -330,9 +331,13 @@
             pl.when(self.hands[0])(self.hands[1].wait_send)
 
 
-def gather_kernel(sizes, count, halo, *refs):
+def gather_kernel(sizes, count, halo, hosts, *refs):
     shards, (feed, keep, decay, gain, reach, power) = refs[:count], refs[count : count + 6]
     wholes, (window, entry, out) = refs[count + 6 : 2 * count + 6], refs[2 * count + 6 : 2 * count + 9]
+    if hosts:
+        values, slopes = refs[2 * count + 9 : 2 * count + 11]
+        weight, block_in, value_tile, slope_tile, weight_sem, in_sem, out_sem = refs[-7:]
+        refs = refs[: 2 * count + 9] + refs[2 * count + 11 : -7]
     (
         send_sem, recv_sem, local_sem, edge, arrived, edge_send, edge_recv,
         zero, halo_send, halo_recv, halo_local, hand_send, wide_feed, part,
@@ -410,6 +415,52 @@
     def forward_unit(index, carry):
         row, base = unit_of(index, width, chans)
         ema_forward(row, base, feed, keep, decay, gain, entry, out, wide_feed, part)
+        return carry
+
+    def block_place(index):
+        return lax.rem(index, rows), halo - lax.div(index, rows)
+
+    def load_block(index):
+        slot = lax.rem(index, 2)
+        return pltpu.make_async_copy(window.at[block_place(index)], block_in.at[slot], in_sem.at[slot])
+
+    def store_tiles(index):
+        slot = lax.rem(index, 2)
+        row, back_by = block_place(lax.div(index, tiles))
+        columns = pl.ds(pl.multiple_of(lax.rem(index, tiles) * HOST_TILE, HOST_TILE), HOST_TILE)
+        return [
+            pltpu.make_async_copy(tile.at[slot], whole.at[row, back_by, :, columns], out_sem.at[at, slot])
+            for at, (tile, whole) in enumerate(((value_tile, values), (slope_tile, slopes)))
+        ]
+
+    blocks = rows * (halo + 1)
+    tiles = wholes[0].shape[-1] // HOST_TILE
+
+    def value_unit(index, carry):
+        block, slot = lax.div(index, tiles), lax.rem(index, 2)
+
+        @pl.when(lax.rem(index, tiles) == 0)
+        def _():
+            load_block(block).wait()
+
+            @pl.when(block + 1 < blocks)
+            def _():
+                load_block(block + 1).start()
+
+        columns = pl.ds(pl.multiple_of(lax.rem(index, tiles) * HOST_TILE, HOST_TILE), HOST_TILE)
+        part_weight = weight[:, :, :, :, :, columns].reshape(chans, HOST_TILE)
+        before = product(block_in[lax.rem(block, 2)], part_weight)
+        squash = jax.nn.sigmoid(before)
+
+        @pl.when(index >= 2)
+        def _():
+            for item in store_tiles(index - 2):
+                item.wait()
+
+        value_tile[slot] = low(before * squash)
+        slope_tile[slot] = low(squash * (1.0 + before * (1.0 - squash)))
+        for item in store_tiles(index):
+            item.start()
         return carry
 
     lax.fori_loop(0, units, last_unit, 0)
@@ -452,16 +503,34 @@
         if step == 1:
             around.hand_on()
         lax.fori_loop(*share(units, count + 2, step), forward_unit, 0)
+        if hosts and step == 2:
+            for item in twin[0].values():
+                item.wait_recv()
+            full = pltpu.make_async_copy(wholes[0], weight, weight_sem.at[0])
+            full.start()
+            own.wait()
+            around.wait()
+            load_block(0).start()
+            full.wait()
+        if hosts and step >= 2:
+            lax.fori_loop(*share(blocks * tiles, count, step - 2), value_unit, 0)
+    if hosts:
+        for index in (blocks * tiles - 2, blocks * tiles - 1):
+            for item in store_tiles(index):
+                item.wait()
     for w in range(count):
         for item in twin[w].values():
-            item.wait()
+            item.wait_send()
+            if w or not hosts:
+                item.wait_recv()
         for item in line[w] + wide[w] + tall[w]:
             item.wait_send()
         for both in cross[w].values():
             both[0].wait_send()
             both[1].wait_send()
-    own.wait()
-    around.wait()
+    if not hosts:
+        own.wait()
+        around.wait()
 
 
 def vmem(count):
@@ -482,16 +551,31 @@
     rows, length, chans = feed.shape
     state = (rows, 16, chans)
     width = min(FORWARD_WIDTH, chans)
+    hosts = pieces[0] == shards[0].shape
+    made, extra = [], []
+    if hosts:
+        wide = shards[0].shape[1]
+        made = [jax.ShapeDtypeStruct((rows, halo + 1, length, wide), jnp.bfloat16)] * 2
+        extra = [
+            pltpu.VMEM(sizes + pieces[0], jnp.bfloat16),
+            pltpu.VMEM((2, length, chans), jnp.bfloat16),
+            pltpu.VMEM((2, length, HOST_TILE), jnp.bfloat16),
+            pltpu.VMEM((2, length, HOST_TILE), jnp.bfloat16),
+            pltpu.SemaphoreType.DMA((1,)),
+            pltpu.SemaphoreType.DMA((2,)),
+            pltpu.SemaphoreType.DMA((2, 2)),
+        ]
     results = pl.pallas_call(
-        functools.partial(gather_kernel, sizes, count, halo),
+        functools.partial(gather_kernel, sizes, count, halo, hosts),
         out_shape=[jax.ShapeDtypeStruct(sizes + piece, jnp.bfloat16) for piece in pieces]
         + [
             jax.ShapeDtypeStruct((rows, halo + 1, length, chans), jnp.bfloat16),
             jax.ShapeDtypeStruct(state, jnp.float32),
             jax.ShapeDtypeStruct(feed.shape, jnp.bfloat16),
-        ],
+        ]
+        + made,
         in_specs=anywhere(count) + vmem(6),
-        out_specs=anywhere(count + 1) + vmem(2),
+        out_specs=anywhere(count + 1) + vmem(2) + anywhere(len(made)),
         scratch_shapes=[
             pltpu.SemaphoreType.DMA((count, slots)),
             pltpu.SemaphoreType.DMA((count, slots)),
@@ -507,6 +591,7 @@
             pltpu.SemaphoreType.DMA((1,)),
             pltpu.VMEM((width // LANES, length, LANES), jnp.float32),
             pltpu.VMEM((width // LANES * EMA_STEP * 8, LANES), jnp.float32),
+            *extra,
         ],
         compiler_params=pltpu.CompilerParams(collective_id=0, has_side_effects=True, vmem_limit_bytes=48 * 2**20),
         name="gather_weights",
@@ -993,7 +1078,7 @@
     keep = jnp.broadcast_to(keep_own[:, None, :, None], (rows, 1, places, LANES)).reshape(rows, places, LANES)
     alive = jnp.min(keep_row.reshape(rows, seq_count, places), axis=2)
 
-    (value_full, mix_full, head_full, expand_full), normed_window, start, ema_low = gather_weights(
+    (value_full, mix_full, head_full, expand_full), normed_window, start, ema_low, *made = gather_weights(
         (value_weight, mix_weight, head_weight, expand_weight),
         normed_low,
         keep,
@@ -1011,18 +1096,22 @@
 
     premix = (ema_low.astype(jnp.float32) + chan_vectors[2] * normed).reshape(tokens, width)
     mixed_low = low(jax.nn.silu(premix))
-    value_pre = product(normed_window, value_full)
-    values_low = low(jax.nn.silu(value_pre)).reshape(rows, window, V)
-    value_slope = low(silu_slope(value_pre)).reshape(rows, window, V)
+    if made:
+        values_low, value_slope = (item.reshape(rows, window, V) for item in made)
+    else:
+        value_pre = product(normed_window, value_full)
+        values_low = low(jax.nn.silu(value_pre)).reshape(rows, window, V)
+        value_slope = low(silu_slope(value_pre)).reshape(rows, window, V)
+    shared_pre = product(mixed_low, mix_full[:, :Z])
+    shared = jax.nn.silu(shared_pre)
+    queries_low = low(shared * z_affine[0] + z_affine[1]).reshape(rows, places, Z)
+    keys_low = low(shared * z_affine[2]).reshape(rows, places, Z)
+    keys_low, mixed_low = lax.optimization_barrier((keys_low, mixed_low))
+    key_window = jnp.concatenate([shift_seq(keys_low, by) for by in range(halo, 0, -1)] + [keys_low], axis=1)
     projected = product(mixed_low, mix_full)
-    shared_pre = projected[:, :Z]
     reset_pre = projected[:, Z : Z + V]
     head_base = projected[:, Z + V : Z + V + width]
     update_pre = projected[:, Z + V + width :]
-    shared = jax.nn.silu(shared_pre)
-    queries_low = low(shared * z_affine[0] + z_affine[1]).reshape(rows, places, Z)
-    keys_low = low(shared * z_affine[2]).reshape(rows, places, Z)
-    key_window = jnp.concatenate([shift_seq(keys_low, by) for by in range(halo, 0, -1)] + [keys_low], axis=1)
     reset_gate = jax.nn.silu(reset_pre)
     update_gate = jax.nn.sigmoid(update_pre)
 

time: 808 us -> 791 us (0.979)
  matrix products: 243 us -> 222 us
    dot_general x5, matrix products: 87.5 us -> 66.6 us  [product(): return jnp.dot(left, right, preferred_element_type=jnp.float32)]
where the time goes in v4:
time: 791 us; the launch traced here: 782 us
  Pallas kernels  455 us (58%)
  matrix products  222 us (28%)
  other arithmetic  54.7 us (7%)
  local copies, waits for them, and re-layouts  17.2 us (2%)
  starting transfers between devices  17 us (2%)
  between operations  15.7 us (2%)
    pallas_call x1, Pallas kernels, scatter_grads(): pl.pallas_call(functools.partial(scatter_kernel, sizes, count), out_shape...  208 us
    pallas_call x1, Pallas kernels, gather_weights(): pl.pallas_call(functools.partial(gather_kernel, sizes, count, halo, hosts...  201 us
    dot_general x5, matrix products, against(): lax.dot_general(left, right, (((1,), (1,)), ((), ())), preferred_element_...  84.1 us
    dot_general x5, matrix products, transposed(): lax.dot_general(left, right, (((0,), (0,)), ((), ())), preferred_element_...  71.6 us
    dot_general x5, matrix products, product(): return jnp.dot(left, right, preferred_element_type=jnp.float32)  66.6 us
    pallas_call x1, Pallas kernels, attend_back(): pl.pallas_call(functools.partial(attend_back_kernel, halo * places), out_...  32.9 us
    ppermute x6, starting transfers between devices, shift_seq(): return lax.ppermute(values, 'seq', pairs)  16.9 us
  transfers between devices with their start and end apart: 7, of which 0 were waited for; matrix products, arithmetic and copies ran while one was open for 23% of the time, Pallas kernels for 2%

profile of v4, /device:TPU:0, one launch (start us, length us, event | category | flops | bytes accessed | tf_op | source)
XLA Modules:
  0.0 782.3 jit_solution(10976068340119206830)
XLA Ops:
  7.3 0.9 convert_subtract_fusion.1
  8.2 1.9 convert_reduce_fusion
  10.2 2.3 fusion.33
  12.9 2.7 fusion.27
  16.4 201.4 %gather_weights.1 = (bf16[4,2,2,2,32,2048]{5,4,3,2,1,0:T(8,128)(2,1)}, bf16[4,2,2,2,32,4224]{5,4,3,2,1,0:T(8,128)(2,1)}, bf16[4,2,2,2,64,1024]{5,4,3,2,1,0:T(8,1...) custom-call(bf16[32,2048]{1,0:T(8,128)(2,1)S(1)} %copy-done.16, ...), custom_call_target="tpu_custom_call" | custom-call | tf_op jit(solution)/shard_map/gather_weights/pallas_call | solution.py:568
  217.8 1.3 copy-done.1
  219.9 2.7 multiply_add_fusion
  222.6 1.1 fusion.18
  223.7 2.7 add_convert_fusion.2
  226.4 10.1 %collective-permute-start = (bf16[2,512,128]{2,1,0:T(8,128)(2,1)S(1)}, bf16[2,512,128]{2,1,0:T(8,128)(2,1)S(1)}, u32[]{:S(2)}, u32[]{:S(2)}) collective-permute-start(bf16[2,512,128]{2,1,0:T(8,128)(2,1)S(1)} %bitcast.262), channel_id=1, source_target_pairs={{0,2},{1,3},{4,6},{5,7},{8,10},{9,11},{12,14},{13,15},{16,18},{17,... | collective-permute-start | bytes 786440 | tf_op jit(solution)/shard_map/ppermute | solution.py:203
  236.6 1.5 collective-permute-start.1
  238.1 16.8 %fusion.75 = f32[1024,4224]{1,0:T(8,128)} fusion(bf16[1024,1024]{1,0:T(8,128)(2,1)} %copy-done.35, bf16[1024,4224]{1,0:T(8,128)(2,1)} %bitcast.286), kind=kOutput, calls=%fused_computation.171 | convolution fusion | flops 8858370048 | bytes 28049408 | tf_op jit(solution)/shard_map/dot_general | solution.py:185
  256.5 13.0 %attend.1 = f32[2,512,2048]{2,1,0:T(8,128)S(1)} custom-call(bf16[2,512,128]{2,1,0:T(8,128)(2,1)S(1)} %bitcast.250, bf16[2,1536,128]{2,1,0:T(8,128)(2,1)S(1)} %constant_dynamic-update-slice_fusion.key, bf16[2,1536,2048]{2,1,0:T(8,128)(2,1)} %bitcast.253, s32[2,1,1536]{2,1,0:T(1,128)S(1)} %broadcast_in_dim.20.key_docs, s32[2,512,1]{2,1,0:T(8,128)S(1)} %slice.138.query_docs), custom_call_target="tpu_custom_call" | custom-call | flops 5704253440 | bytes 20971520 | tf_op jit(solution)/shard_map/attend/pallas_call | solution.py:910
  269.5 8.1 %fusion.3 = bf16[1024,2048]{1,0:T(8,128)(2,1)S(1)} fusion(f32[2,512,2048]{2,1,0:T(8,128)S(1)} %attend.1, f32[1024,4224]{1,0:T(8,128)} %fusion.75), kind=kLoop, calls=%fused_computation.11 | loop fusion | flops 12582912 | bytes 20971520 | tf_op jit(solution)/shard_map/convert_element_type | solution.py:197
  277.7 12.6 %fusion.70 = (f32[1024]{0:T(1024)S(1)}, f32[1024,1024]{1,0:T(8,128)S(1)}, f32[1024,1024]{1,0:T(8,128)}) fusion(f32[1024,4224]{1,0:T(8,128)} %fusion.75, bf16[2,512,1024]{2,1,0:T(8,128)(2,1)S(1)} %copy-done.19, bf16[1024,2048]{1,0:T(8,128)(2,1)S(1)} %fusion.3, bf16[2048,1024]{1,0:T(8,128)(2,1)} %bitcast.294), kind=kOutput, calls=%fused_computation.166 | convolution fusion | flops 4308597760 | bytes 27267072 | tf_op jit(solution)/shard_map/dot_general | solution.py:185
  290.9 22.3 %add_multiply_fusion = (f32[1024,4096]{1,0:T(8,128)}, bf16[1024,4096]{1,0:T(8,128)(2,1)}) fusion(bf16[1024,4096]{1,0:T(8,128)(2,1)} %bitcast.290, f32[1024,1024]{1,0:T(8,128)S(1)} %get-tuple-element.94, f32[1024]{0:T(1024)S(1)} %bitcast.271, f32[1024]{0:T(1024)S(1)} %fusion.58, f32[1024]{0:T(1024)S(1)} %broadcast_multiply_fusion), kind=kOutput, calls=%fused_computation.2 | convolution fusion | flops 8631877632 | bytes 37761024 | tf_op jit(solution)/shard_map/dot_general | solution.py:185
  313.1 14.6 %convolution_convert_fusion.2 = bf16[4096,1024]{1,0:T(8,128)(2,1)} fusion(bf16[1024,4096]{1,0:T(8,128)(2,1)} %get-tuple-element.62, bf16[1024,1024]{1,0:T(8,128)(2,1)S(1)} %bitcast.261), kind=kOutput, calls=%fused_computation.18 | convolution fusion | flops 8594128896 | bytes 18874368 | tf_op jit(solution)/shard_map/dot_general | solution.py:193
  327.8 17.7 %fusion = bf16[1024,4096]{1,0:T(8,128)(2,1)} fusion(f32[1024,4096]{1,0:T(8,128)} %get-tuple-element.64, bf16[4096,1024]{1,0:T(8,128)(2,1)} %all-gather.2.cloned.1.call-done, bf16[1024,1024]{1,0:T(8,128)(2,1)} %bitcast.260), kind=kOutput, calls=%fused_computation.1 | convolution fusion | flops 8598323200 | bytes 35651584 | tf_op jit(solution)/shard_map/dot_general | solution.py:189
  345.5 16.4 %multiply_reduce_fusion = (f32[1024]{0:T(1024)}, f32[1024]{0:T(1024)S(1)}, f32[1024,1024]{1,0:T(8,128)}) fusion(f32[1024,1024]{1,0:T(8,128)S(1)} %copy-done.25, f32[1024]{0:T(1024)S(1)} %fusion.58, f32[1024]{0:T(1024)S(1)} %broadcast_multiply_fusion, f32[1024]{0:T(1024)S(1)} %bitcast.272, bf16[1024,4096]{1,0:T(8,128)(2,1)} %fusion, ...), kind=kOutput, calls=%fused_computation.59 | convolution fusion | flops 8597272576 | bytes 25186304 | tf_op jit(solution)/shard_map/dot_general | solution.py:189
  361.8 15.3 %convolution_convert_fusion.1 = bf16[1024,4096]{1,0:T(8,128)(2,1)} fusion(bf16[1024,4096]{1,0:T(8,128)(2,1)} %fusion, f32[1024,1024]{1,0:T(8,128)S(1)} %copy-done.25, f32[1024]{0:T(1024)S(1)} %bitcast.273, f32[1024]{0:T(1024)S(1)} %fusion.58, f32[1024]{0:T(1024)S(1)} %broadcast_multiply_fusion), kind=kOutput, calls=%fused_computation.17 | convolution fusion | flops 8598323200 | bytes 20983808 | tf_op jit(solution)/shard_map/dot_general | solution.py:193
  377.2 1.8 fusion.69
  379.0 1.0 copy-done.34
  380.6 8.4 %multiply_convert_fusion.2 = (bf16[1024,1024]{1,0:T(8,128)(2,1)}, bf16[1024,1024]{1,0:T(8,128)(2,1)}, f32[1024,1024]{1,0:T(8,128)}) fusion(bf16[2,512,1024]{2,1,0:T(8,128)(2,1)S(1)} %copy-done.20, f32[1024,1024]{1,0:T(8,128)S(1)} %copy-done.34, f32[1024,1024]{1,0:T(8,128)S(1)} %get-tuple-element.92, f32[1024]{0:T(1024)S(1)} %negate_multiply_fusion, ...), kind=kLoop, calls=%fused_computation.60 | loop fusion | flops 26214400 | bytes 25169920 | tf_op jit(solution)/shard_map/convert.5
  389.0 13.2 %fusion.5 = (bf16[1024,2048]{1,0:T(8,128)(2,1)}, bf16[1024,2048]{1,0:T(8,128)(2,1)}) fusion(f32[2,512,2048]{2,1,0:T(8,128)S(1)} %bitcast.249, f32[1024,4224]{1,0:T(8,128)} %fusion.75, bf16[1024,1024]{1,0:T(8,128)(2,1)} %get-tuple-element.98, bf16[2048,1024]{1,0:T(8,128)(2,1)} %bitcast.295), kind=kOutput, calls=%fused_computation.13 | convolution fusion | flops 4322230272 | bytes 31457280 | tf_op jit(solution)/shard_map/dot_general | solution.py:189
  402.2 32.9 %attend_back.1 = (f32[2,512,128]{2,1,0:T(8,128)S(1)}, f32[2,1536,128]{2,1,0:T(8,128)S(1)}, bf16[2,1536,2048]{2,1,0:T(8,128)(2,1)}) custom-call(bf16[2,512,128]{2,1,0:T(8,128)(2,1)S(1)} %bitcast.251, bf16[2,1536,128]{2,1,0:T(8,128)(2,1)S(1)} %copy-done.9, bf16[2,1536,2048]{2,1,0:T(8,128)(2,1)} %bitcast.254, bf16[2,1536,2048]{2,1,0:T(8,128)(2,1)} %bitcast.284, ...), custom_call_target="tpu_custom_call" | custom-call | flops 13690208256 | bytes 41943040 | tf_op jit(solution)/shard_map/attend_back/pallas_call | solution.py:995
  435.9 1.3 collective-permute-start.2
  437.2 1.3 collective-permute-start.3
  438.5 19.2 %fusion.74 = (bf16[2,3,512,1024]{3,2,0,1:T(8,128)(2,1)S(1)}, f32[2,3,512,1024]{3,2,0,1:T(8,128)}) fusion(bf16[1024,2048]{1,0:T(8,128)(2,1)} %bitcast.293, bf16[2,3,512,2048]{3,2,1,0:T(8,128)(2,1)} %bitcast.296), kind=kOutput, calls=%fused_computation.169 | convolution fusion | flops 12888047616 | bytes 35651584 | tf_op jit(solution)/shard_map/dot_general | solution.py:189
  457.7 2.6 slice_bitcast_fusion.2
  460.2 1.4 collective-permute-start.4
  461.7 1.3 collective-permute-start.5
  463.0 19.9 %convolution_convert_fusion.3 = bf16[1024,2048]{1,0:T(8,128)(2,1)} fusion(bf16[3072,1024]{1,0:T(8,128)(2,1)} %bitcast.292, bf16[3072,2048]{1,0:T(8,128)(2,1)} %bitcast.297), kind=kOutput, calls=%fused_computation.70 | convolution fusion | flops 12886999040 | bytes 23068672 | tf_op jit(solution)/shard_map/dot_general | solution.py:193
  482.9 12.3 %add_convert_fusion = bf16[1024,1024]{1,0:T(8,128)(2,1)} fusion(f32[1024,1024]{1,0:T(8,128)S(1)} %copy-done.27, bf16[1024,4096]{1,0:T(8,128)(2,1)} %get-tuple-element.62, bf16[4096,1024]{1,0:T(8,128)(2,1)S(1)} %bitcast.289), kind=kOutput, calls=%fused_computation.64 | convolution fusion | flops 8592031744 | bytes 23068672 | tf_op jit(solution)/shard_map/dot_general | solution.py:185
  495.3 6.5 convolution_convert_fusion.4
  502.5 17.7 %fusion.13 = (f32[1024]{0:T(1024)S(1)}, f32[1024,1024]{1,0:T(8,128)}) fusion(f32[2,512,1024]{2,1,0:T(8,128)} %get-tuple-element.106, f32[2,512,1024]{2,1,0:T(8,128)} %copy-done.28, bf16[1024,4224]{1,0:T(8,128)(2,1)} %bitcast.287, bf16[1024,1024]{1,0:T(8,128)(2,1)} %get-tuple-element.97, bf16[1024,1024]{1,0:T(8,128)(2,1)} %get-tuple-element.98, ...), kind=kOutput, calls=%fused_computation.30 | convolution fusion | flops 8903457792 | bytes 29888512 | tf_op jit(solution)/shard_map/dot_general | solution.py:189
  520.2 4.0 bitcast_convert_fusion.refs_7_
  524.3 15.2 %convolution_convert_fusion = bf16[1024,4224]{1,0:T(8,128)(2,1)} fusion(bf16[1024,1024]{1,0:T(8,128)(2,1)S(1)} %copy-done.36, bf16[1024,1024]{1,0:T(8,128)(2,1)} %get-tuple-element.97, bf16[1024,1024]{1,0:T(8,128)(2,1)} %get-tuple-element.98, bf16[1024,2048]{1,0:T(8,128)(2,1)} %get-tuple-element.99, bf16[1024,128]{1,0:T(8,128)(2,1)S(1)} %get-tuple-element.108), kind=kOutput, calls=%fused_computation.7 | convolution fusion | flops 8897298432 | bytes 19398656 | tf_op jit(solution)/shard_map/dot_general | solution.py:193
  539.6 5.8 fusion.28
  545.4 1.3 concatenate.14.refs_5_
  546.7 208.2 %scatter_grads.1 = (f32[128,1024]{1,0:T(8,128)}, f32[32,4096]{1,0:T(8,128)}, f32[64,1024]{1,0:T(8,128)}, f32[32,2048]{1,0:T(8,128)}, f32[32,4224]{1,0:T(8,128)},...) custom-call(bf16[4,2,2,2,128,1024]{5,4,3,2,1,0:T(8,128)(2,1)} %bitcast.256, ...), custom_call_target="tpu_custom_call" | custom-call | tf_op jit(solution)/shard_map/scatter_grads/pallas_call | solution.py:830
  755.0 0.9 fusion.56
  755.9 0.9 multiply_reduce_fusion.3
  757.5 1.3 slice_reduce_fusion
  759.8 4.3 fusion.34
  764.1 0.9 copy-done.23
  765.7 4.8 fusion.32
  771.2 0.8 copy.60
  773.4 0.8 copy.63
  (203 shorter events, 11.4 us)
Async XLA Ops:
  7.2 320.6 %all-gather.2.cloned.1.call-start = ((), (), s32[]{:S(2)}) async-start(), calls=%async_computation | async-start | bytes 8650752 | tf_op jit(solution)/shard_map/all_gather | solution.py:1095
  10.2 209.7 %copy-start.50 = (f32[2,512]{1,0:T(2,128)}, f32[2,512]{1,0:T(2,128)S(1)}, u32[]{:S(2)}) copy-start(f32[2,512]{1,0:T(2,128)S(1)} %broadcast_multiply_fusion.3) | copy-start | bytes 12292
  12.5 207.4 %copy-start.52 = (f32[2,512]{1,0:T(2,128)}, f32[2,512]{1,0:T(2,128)S(1)}, u32[]{:S(2)}) copy-start(f32[2,512]{1,0:T(2,128)S(1)} %add_rsqrt_fusion) | copy-start | bytes 12292
  12.5 207.4 %copy-start.54 = (f32[1,1024]{1,0:T(1,128)}, f32[1,1024]{1,0:T(1,128)S(1)}, u32[]{:S(2)}) copy-start(f32[1,1024]{1,0:T(1,128)S(1)} %get-tuple-element.118) | copy-start | bytes 12292
  12.5 207.4 %copy-start.57 = (f32[1,1024]{1,0:T(1,128)}, f32[1,1024]{1,0:T(1,128)S(1)}, u32[]{:S(2)}) copy-start(f32[1,1024]{1,0:T(1,128)S(1)} %get-tuple-element.119) | copy-start | bytes 12292
  15.6 204.2 %copy-start.66 = (f32[3,128]{1,0:T(4,128)S(1)}, f32[3,128]{1,0:T(4,128)}, u32[]{:S(2)}) copy-start(f32[3,128]{1,0:T(4,128)} %param.27) | copy-start | bytes 4612
  16.1 203.7 %copy-start.5 = (f32[3,16,1024]{2,1,0:T(8,128)}, f32[3,16,1024]{2,1,0:T(8,128)S(1)}, u32[]{:S(2)}) copy-start(f32[3,16,1024]{2,1,0:T(8,128)S(1)} %pad_maximum_fusion.3.refs_9_.refs_13_) | copy-start | bytes 589828
  16.3 201.5 %copy-start.2 = (f32[2,512,128]{2,1,0:T(8,128)}, f32[2,512,128]{2,1,0:T(8,128)S(1)}, u32[]{:S(2)}) copy-start(f32[2,512,128]{2,1,0:T(8,128)S(1)} %reshape.264.refs_5_.refs_8_) | copy-start | bytes 1572868
  223.7 14.4 %copy-start.56 = (s32[2,2048]{1,0:T(2,128)S(1)}, s32[2,2048]{1,0:T(2,128)}, u32[]{:S(2)}) copy-start(s32[2,2048]{1,0:T(2,128)} %param.17) | copy-start | bytes 49156
  226.4 30.1 %copy-start.12 = (bf16[1024,128]{1,0:T(8,128)(2,1)}, bf16[1024,128]{1,0:T(8,128)(2,1)S(1)}, u32[]{:S(2)}) copy-start(bf16[1024,128]{1,0:T(8,128)(2,1)S(1)} %get-tuple-element.111) | copy-start | bytes 786436
  226.4 29.9 %collective-permute-start = (bf16[2,512,128]{2,1,0:T(8,128)(2,1)S(1)}, bf16[2,512,128]{2,1,0:T(8,128)(2,1)S(1)}, u32[]{:S(2)}, u32[]{:S(2)}) collective-permute-start(bf16[2,512,128]{2,1,0:T(8,128)(2,1)S(1)} %bitcast.262), channel_id=1, source_target_pairs={{0,2},{1,3},{4,6},{5,7},{8,10},{9,11},{12,14},{13,15},{16,18},{17,... | collective-permute-start | bytes 786440 | tf_op jit(solution)/shard_map/ppermute | solution.py:203
  236.6 19.8 %collective-permute-start.1 = (bf16[2,512,128]{2,1,0:T(8,128)(2,1)S(1)}, bf16[2,512,128]{2,1,0:T(8,128)(2,1)S(1)}, u32[]{:S(2)}, u32[]{:S(2)}) collective-permute-start(bf16[2,512,128]{2,1,0:T(8,128)(2,1)S(1)} %bitcast.263), channel_id=1, source_target_pairs={{0,1},{1,2},{2,3},{4,5},{5,6},{6,7},{8,9},{9,10},{10,11},{12,13},{... | collective-permute-start | bytes 786440 | tf_op jit(solution)/shard_map/ppermute | solution.py:203
  256.5 13.0 %copy-start.8 = (bf16[2,1536,128]{2,1,0:T(8,128)(2,1)}, bf16[2,1536,128]{2,1,0:T(8,128)(2,1)S(1)}, u32[]{:S(2)}) copy-start(bf16[2,1536,128]{2,1,0:T(8,128)(2,1)S(1)} %constant_dynamic-update-slice_fusion.key) | copy-start | bytes 2359300
  269.5 8.2 %copy-start = (f32[2,512,2048]{2,1,0:T(8,128)}, f32[2,512,2048]{2,1,0:T(8,128)S(1)}, u32[]{:S(2)}) copy-start(f32[2,512,2048]{2,1,0:T(8,128)S(1)} %attend.1) | copy-start | bytes 25165828
  269.5 8.2 %copy-start.19 = (bf16[2,512,1024]{2,1,0:T(8,128)(2,1)S(1)}, bf16[2,512,1024]{2,1,0:T(8,128)(2,1)}, u32[]{:S(2)}) copy-start(bf16[2,512,1024]{2,1,0:T(8,128)(2,1)} %param.15) | copy-start | bytes 6291460
  277.7 12.6 %copy-start.31 = (bf16[1024,2048]{1,0:T(8,128)(2,1)}, bf16[1024,2048]{1,0:T(8,128)(2,1)S(1)}, u32[]{:S(2)}) copy-start(bf16[1024,2048]{1,0:T(8,128)(2,1)S(1)} %fusion.3) | copy-start | bytes 12582916
  290.3 22.8 %copy-start.24 = (f32[1024,1024]{1,0:T(8,128)}, f32[1024,1024]{1,0:T(8,128)S(1)}, u32[]{:S(2)}) copy-start(f32[1024,1024]{1,0:T(8,128)S(1)} %get-tuple-element.94) | copy-start | bytes 12582916
  290.9 22.3 %copy-start.37 = (bf16[2,512,1024]{2,1,0:T(8,128)(2,1)S(1)}, bf16[2,512,1024]{2,1,0:T(8,128)(2,1)}, u32[]{:S(2)}) copy-start(bf16[2,512,1024]{2,1,0:T(8,128)(2,1)} %param.16) | copy-start | bytes 6291460
  327.8 17.7 %copy-start.25 = (f32[1024,1024]{1,0:T(8,128)S(1)}, f32[1024,1024]{1,0:T(8,128)}, u32[]{:S(2)}) copy-start(f32[1024,1024]{1,0:T(8,128)} %copy-done.24) | copy-start | bytes 12582916
  361.8 15.3 %copy-start.26 = (f32[1024,1024]{1,0:T(8,128)S(1)}, f32[1024,1024]{1,0:T(8,128)}, u32[]{:S(2)}) copy-start(f32[1024,1024]{1,0:T(8,128)} %copy-done.24) | copy-start | bytes 12582916
  361.8 15.3 %copy-start.33 = (f32[1024,1024]{1,0:T(8,128)S(1)}, f32[1024,1024]{1,0:T(8,128)}, u32[]{:S(2)}) copy-start(f32[1024,1024]{1,0:T(8,128)} %get-tuple-element.125) | copy-start | bytes 12582916
  377.2 11.8 %slice-start = ((s8[8388608]{0:T(1024)(128)(4,1)}), s8[4194304]{0:T(1024)(128)(4,1)S(1)}, s32[]{:S(2)}) async-start(s8[8388608]{0:T(1024)(128)(4,1)} %bitcast.248), calls=%async_computation.1 | async-start | bytes 8388608
  380.6 8.4 %slice-start.1 = ((s8[8388608]{0:T(1024)(128)(4,1)}), s8[4194304]{0:T(1024)(128)(4,1)S(1)}, s32[]{:S(2)}) async-start(s8[8388608]{0:T(1024)(128)(4,1)} %bitcast.248), calls=%async_computation.2 | async-start | bytes 8388608
  389.0 13.2 %copy-start.9 = (bf16[2,1536,128]{2,1,0:T(8,128)(2,1)S(1)}, bf16[2,1536,128]{2,1,0:T(8,128)(2,1)}, u32[]{:S(2)}) copy-start(bf16[2,1536,128]{2,1,0:T(8,128)(2,1)} %copy-done.8) | copy-start | bytes 2359300
  389.0 13.2 %copy-start.13 = (bf16[1024,128]{1,0:T(8,128)(2,1)S(1)}, bf16[1024,128]{1,0:T(8,128)(2,1)}, u32[]{:S(2)}) copy-start(bf16[1024,128]{1,0:T(8,128)(2,1)} %copy-done.12) | copy-start | bytes 786436
  435.0 22.6 %copy-start.3 = (f32[2,512,128]{2,1,0:T(8,128)}, f32[2,512,128]{2,1,0:T(8,128)S(1)}, u32[]{:S(2)}) copy-start(f32[2,512,128]{2,1,0:T(8,128)S(1)} %get-tuple-element.66) | copy-start | bytes 1572868
  435.9 66.0 %collective-permute-start.2 = (bf16[2,512,128]{2,1,0:T(8,128)(2,1)}, bf16[2,512,128]{2,1,0:T(8,128)(2,1)S(1)}, u32[]{:S(2)}, u32[]{:S(2)}) collective-permute-start(bf16[2,512,128]{2,1,0:T(8,128)(2,1)} %get-tuple-element.109), channel_id=1, source_target_pairs={{1,0},{2,1},{3,2},{5,4},{6,5},{7,6},{9,8},{10,9},{11,10},{13,12},{... | collective-permute-start | bytes 786440 | tf_op jit(solution)/shard_map/ppermute | solution.py:203
  437.2 64.8 %collective-permute-start.3 = (bf16[2,512,128]{2,1,0:T(8,128)(2,1)S(1)}, bf16[2,512,128]{2,1,0:T(8,128)(2,1)S(1)}, u32[]{:S(2)}, u32[]{:S(2)}) collective-permute-start(bf16[2,512,128]{2,1,0:T(8,128)(2,1)S(1)} %get-tuple-element.110), channel_id=1, source_target_pairs={{2,0},{3,1},{6,4},{7,5},{10,8},{11,9},{14,12},{15,13},{18,16},{19,... | collective-permute-start | bytes 786440 | tf_op jit(solution)/shard_map/ppermute | solution.py:203
  457.7 25.2 %slice-start.2 = ((s8[8388608]{0:T(1024)(128)(4,1)}), s8[4194304]{0:T(1024)(128)(4,1)S(1)}, s32[]{:S(2)}) async-start(s8[8388608]{0:T(1024)(128)(4,1)} %bitcast.288), calls=%async_computation.3 | async-start | bytes 8388608
  460.2 79.3 %collective-permute-start.4 = (bf16[2,512,1024]{2,1,0:T(8,128)(2,1)}, bf16[2,512,1024]{2,1,0:T(8,128)(2,1)}, u32[]{:S(2)}, u32[]{:S(2)}) collective-permute-start(bf16[2,512,1024]{2,1,0:T(8,128)(2,1)} %get-tuple-element.104), channel_id=1, source_target_pairs={{1,0},{2,1},{3,2},{5,4},{6,5},{7,6},{9,8},{10,9},{11,10},{13,12},{... | collective-permute-start | bytes 6291464 | tf_op jit(solution)/shard_map/ppermute | solution.py:203
  461.7 77.9 %collective-permute-start.5 = (bf16[2,512,1024]{2,1,0:T(8,128)(2,1)}, bf16[2,512,1024]{2,1,0:T(8,128)(2,1)}, u32[]{:S(2)}, u32[]{:S(2)}) collective-permute-start(bf16[2,512,1024]{2,1,0:T(8,128)(2,1)} %get-tuple-element.105), channel_id=1, source_target_pairs={{2,0},{3,1},{6,4},{7,5},{10,8},{11,9},{14,12},{15,13},{18,16},{19,... | collective-permute-start | bytes 6291464 | tf_op jit(solution)/shard_map/ppermute | solution.py:203
  463.0 19.9 %copy-start.27 = (f32[1024,1024]{1,0:T(8,128)S(1)}, f32[1024,1024]{1,0:T(8,128)}, u32[]{:S(2)}) copy-start(f32[1024,1024]{1,0:T(8,128)} %copy-done.24) | copy-start | bytes 12582916
  463.0 19.9 %slice-start.3 = ((s8[8388608]{0:T(1024)(128)(4,1)}), s8[4194304]{0:T(1024)(128)(4,1)S(1)}, s32[]{:S(2)}) async-start(s8[8388608]{0:T(1024)(128)(4,1)} %bitcast.288), calls=%async_computation.4 | async-start | bytes 8388608
  482.9 12.3 %copy-start.32 = (bf16[1024,2048]{1,0:T(8,128)(2,1)S(1)}, bf16[1024,2048]{1,0:T(8,128)(2,1)}, u32[]{:S(2)}) copy-start(bf16[1024,2048]{1,0:T(8,128)(2,1)} %copy-done.31) | copy-start | bytes 12582916
  482.9 12.3 %copy-start.39 = (bf16[1024,1024]{1,0:T(8,128)(2,1)S(1)}, bf16[1024,1024]{1,0:T(8,128)(2,1)}, u32[]{:S(2)}) copy-start(bf16[1024,1024]{1,0:T(8,128)(2,1)} %get-tuple-element.98) | copy-start | bytes 6291460
  495.3 6.8 copy-start.43
  524.3 15.3 %copy-start.21 = (bf16[2,512,1024]{2,1,0:T(8,128)(2,1)S(1)}, bf16[2,512,1024]{2,1,0:T(8,128)(2,1)}, u32[]{:S(2)}) copy-start(bf16[2,512,1024]{2,1,0:T(8,128)(2,1)} %param.15) | copy-start | bytes 6291460
  524.3 15.3 %copy-start.29 = (f32[1024,1024]{1,0:T(8,128)S(1)}, f32[1024,1024]{1,0:T(8,128)}, u32[]{:S(2)}) copy-start(f32[1024,1024]{1,0:T(8,128)} %get-tuple-element.129) | copy-start | bytes 12582916
  524.3 15.3 %copy-start.51 = (f32[2,512]{1,0:T(2,128)S(1)}, f32[2,512]{1,0:T(2,128)}, u32[]{:S(2)}) copy-start(f32[2,512]{1,0:T(2,128)} %copy-done.50) | copy-start | bytes 12292
  524.3 15.3 %copy-start.53 = (f32[2,512]{1,0:T(2,128)S(1)}, f32[2,512]{1,0:T(2,128)}, u32[]{:S(2)}) copy-start(f32[2,512]{1,0:T(2,128)} %copy-done.52) | copy-start | bytes 12292
  524.3 15.3 %copy-start.58 = (f32[1,1024]{1,0:T(1,128)S(1)}, f32[1,1024]{1,0:T(1,128)}, u32[]{:S(2)}) copy-start(f32[1,1024]{1,0:T(1,128)} %copy-done.57) | copy-start | bytes 12292
  546.7 208.3 %copy-start.7 = (f32[16,1024]{1,0:T(8,128)S(1)}, f32[16,1024]{1,0:T(8,128)}, u32[]{:S(2)}) copy-start(f32[16,1024]{1,0:T(8,128)} %copy-done.6) | copy-start | bytes 196612
  546.7 208.3 %copy-start.41 = (f32[2,1024,16]{1,2,0:T(8,128)S(1)}, f32[2,1024,16]{1,2,0:T(8,128)}, u32[]{:S(2)}) copy-start(f32[2,1024,16]{1,2,0:T(8,128)} %param.25) | copy-start | bytes 393220
  546.7 208.3 %copy-start.47 = (f32[2,1024,16]{1,2,0:T(8,128)S(1)}, f32[2,1024,16]{1,2,0:T(8,128)}, u32[]{:S(2)}) copy-start(f32[2,1024,16]{1,2,0:T(8,128)} %param.26) | copy-start | bytes 393220
  546.7 213.0 %copy-start.55 = (f32[1,1024]{1,0:T(1,128)S(1)}, f32[1,1024]{1,0:T(1,128)}, u32[]{:S(2)}) copy-start(f32[1,1024]{1,0:T(1,128)} %copy-done.54) | copy-start | bytes 12292
  765.6 7.1 copy-start.48
  765.6 7.8 copy-start.45
  765.6 8.6 %copy-start.44 = (f32[128,1024]{1,0:T(8,128)S(1)}, f32[128,1024]{1,0:T(8,128)}, u32[]{:S(2)}) copy-start(f32[128,1024]{1,0:T(8,128)} %get-tuple-element.151) | copy-start | bytes 1572868
  (30 other events, 129.6 us)
Sparse Core Ops, SparseCore 0:
  219.9 87.1 all-gather.1

commit v5 on v4

--- a/solution.py
+++ b/solution.py
@@ -247,6 +247,17 @@
     return (rows, columns) if rows % 16 == 0 else (rows * columns // LANES, LANES)
 
 
+def chunks_of(pieces):
+    chunks = []
+    for at, (rows, columns) in enumerate(pieces):
+        if rows * columns >= 2**17:
+            half = columns // (2 * LANES) * LANES
+            chunks += [(at, pl.ds(0, half)), (at, pl.ds(half, columns - half))]
+        else:
+            chunks.append((at, pl.ds(0, columns)))
+    return chunks
+
+
 def share(total, parts, at):
     return total * at // parts, total * (at + 1) // parts
 
@@ -331,7 +342,7 @@
             pl.when(self.hands[0])(self.hands[1].wait_send)
 
 
-def gather_kernel(sizes, count, halo, hosts, *refs):
+def gather_kernel(sizes, count, halo, hosts, chunks, *refs):
     shards, (feed, keep, decay, gain, reach, power) = refs[:count], refs[count : count + 6]
     wholes, (window, entry, out) = refs[count + 6 : 2 * count + 6], refs[2 * count + 6 : 2 * count + 9]
     if hosts:
@@ -365,14 +376,18 @@
 
     def block(w, a_by=0, b_by=0, part=None):
         at = pl.ds(0, depth) if part is None else part
-        return wholes[w].at[at, c, lax.rem(a - a_by + down, down), lax.rem(b - b_by + across, across)]
+        whole, columns = chunks[w]
+        beside = lax.rem(a - a_by + down, down), lax.rem(b - b_by + across, across)
+        return wholes[whole].at[at, c, *beside, :, columns]
 
     front, back = pl.ds(0, half), pl.ds(half, depth - half)
     local, line, wide, tall, cross, twin = [], [], [], [], [], []
-    for w in range(count):
-        own = wholes[w].at[z, c, a, b]
-        local.append(pltpu.make_async_copy(shards[w], own, local_sem.at[w]))
-        line.append([copy(w, ("z", k), shards[w], own, 0, k) for k in range(1, depth)])
+    flat, count = len(chunks) - 1, len(chunks) - 1
+    for w, (whole, columns) in enumerate(chunks[:count]):
+        own = wholes[whole].at[z, c, a, b, :, columns]
+        shard = shards[whole].at[:, columns]
+        local.append(pltpu.make_async_copy(shard, own, local_sem.at[w]))
+        line.append([copy(w, ("z", k), shard, own, 0, k) for k in range(1, depth)])
         wide.append([copy(w, ("x", k), block(w), block(w), 3, k) for k in range(1, across)])
         tall.append([copy(w, ("y", l), block(w), block(w), 2, l) for l in range(1, down)])
         pairs = [(k, l) for k in range(1, across) for l in range(1, down)]
@@ -392,9 +407,33 @@
                 for k in range(across)
             }
         )
+    whole, columns = chunks[flat]
+
+    def plane(back_by=0):
+        return wholes[whole].at[lax.rem(z - back_by + depth, depth), c, :, :, :, columns]
+
+    def flat_copy(slot, source, target, device):
+        return pltpu.make_async_remote_copy(
+            src_ref=source,
+            dst_ref=target,
+            send_sem=send_sem.at[flat, slot],
+            recv_sem=recv_sem.at[flat, slot],
+            device_id=device,
+            device_id_type=MESH,
+        )
+
+    flat_shard, flat_own = shards[whole].at[:, columns], wholes[whole].at[z, c, a, b, :, columns]
+    flat_local = pltpu.make_async_copy(flat_shard, flat_own, local_sem.at[flat])
+    flat_row = [flat_copy(by - 1, flat_shard, flat_own, along(seqs, by)) for by in range(1, seqs)]
+    flat_line = [
+        flat_copy(seqs - 2 + k, plane(), plane(), peer_of(sizes, spot, 0, k)) for k in range(1, depth)
+    ]
+    flat_twin = [
+        flat_copy(seqs + depth - 2 + k, plane(k), plane(k), peer_of(sizes, spot, 1, 1)) for k in range(depth)
+    ]
     zero[...] = jnp.zeros_like(zero)
     around = Halo(halo, seqs, feed, window, zero, halo_send, halo_recv, halo_local, hand_send)
-    own = pltpu.make_async_copy(feed, window.at[:, halo], local_sem.at[count])
+    own = pltpu.make_async_copy(feed, window.at[:, halo], local_sem.at[count + 1])
     edges = spread_edge(seqs, edge, arrived, edge_send, edge_recv, True)
     for w in range(count):
         local[w].start()
@@ -402,6 +441,9 @@
         item.start()
     own.start()
     around.start()
+    flat_local.start()
+    for item in flat_row:
+        item.start()
     for w in range(1, min(2, count)):
         for item in line[w]:
             item.start()
@@ -502,6 +544,15 @@
             join_edges(arrived, reach, power, entry)
         if step == 1:
             around.hand_on()
+            flat_local.wait()
+            for item in flat_row:
+                item.wait_recv()
+            for item in flat_line + flat_twin[:1]:
+                item.start()
+        if step == count:
+            for item, on in zip(flat_line, flat_twin[1:]):
+                item.wait_recv()
+                on.start()
         lax.fori_loop(*share(units, count + 2, step), forward_unit, 0)
         if hosts and step == 2:
             for item in twin[0].values():
@@ -518,6 +569,10 @@
         for index in (blocks * tiles - 2, blocks * tiles - 1):
             for item in store_tiles(index):
                 item.wait()
+    for item in flat_twin:
+        item.wait()
+    for item in flat_row + flat_line:
+        item.wait_send()
     for w in range(count):
         for item in twin[w].values():
             item.wait_send()
@@ -552,6 +607,7 @@
     state = (rows, 16, chans)
     width = min(FORWARD_WIDTH, chans)
     hosts = pieces[0] == shards[0].shape
+    chunks = chunks_of(pieces)
     made, extra = [], []
     if hosts:
         wide = shards[0].shape[1]
@@ -566,7 +622,7 @@
             pltpu.SemaphoreType.DMA((2, 2)),
         ]
     results = pl.pallas_call(
-        functools.partial(gather_kernel, sizes, count, halo, hosts),
+        functools.partial(gather_kernel, sizes, count, halo, hosts, chunks),
         out_shape=[jax.ShapeDtypeStruct(sizes + piece, jnp.bfloat16) for piece in pieces]
         + [
             jax.ShapeDtypeStruct((rows, halo + 1, length, chans), jnp.bfloat16),
@@ -577,9 +633,9 @@
         in_specs=anywhere(count) + vmem(6),
         out_specs=anywhere(count + 1) + vmem(2) + anywhere(len(made)),
         scratch_shapes=[
-            pltpu.SemaphoreType.DMA((count, slots)),
-            pltpu.SemaphoreType.DMA((count, slots)),
-            pltpu.SemaphoreType.DMA((count + 1,)),
+            pltpu.SemaphoreType.DMA((len(chunks), slots)),
+            pltpu.SemaphoreType.DMA((len(chunks), slots)),
+            pltpu.SemaphoreType.DMA((len(chunks) + 1,)),
             pltpu.VMEM(state, jnp.float32),
             pltpu.VMEM((seqs - 1,) + state, jnp.float32),
             pltpu.SemaphoreType.DMA((seqs - 1,)),
@@ -616,7 +672,7 @@
     lax.fori_loop(0, rows // chunk, body, 0)
 
 
-def scatter_kernel(sizes, count, *refs):
+def scatter_kernel(sizes, count, chunks, *refs):
     grads, small = refs[:count], refs[count]
     feed, grad, keep, decay, gain, start, reach, power = refs[count + 1 : count + 9]
     refs = refs[count + 9 :]
@@ -628,9 +684,10 @@
     rows, length, chans = feed.shape
     width = wide.shape[0] * LANES
     seqs = sizes[2] * sizes[3]
+    count = len(chunks)
     names = ("arrive", "own", "first_a", "first_b", "second_a", "second_b", "third")
     held = {name: rest[at * count : (at + 1) * count] for at, name in enumerate(names)}
-    small_parts, send_sem, recv_sem, own_sem, small_send, small_recv = rest[len(names) * count :]
+    flat_planes, flat_pieces, small_parts, send_sem, recv_sem, own_sem, small_send, small_recv = rest[len(names) * count :]
     depth, cores, down, across = sizes
     spot = place_of()
     z, c, a, b = spot
@@ -659,7 +716,7 @@
     twin, first, second, third = [], [], [], []
     for w in range(count):
         arrive = held["arrive"][w]
-        twin.append(copy(w, "c", grads[w].at[:, 1 - c], arrive, 1, 1))
+        twin.append(copy(w, "c", grads[chunks[w][0]].at[:, 1 - c, :, :, :, chunks[w][1]], arrive, 1, 1))
         first.append(
             [
                 copy(w, ("a1", k), arrive.at[front, :, at_b(k)], held["first_a"][w].at[k - 1], 3, k)
@@ -703,7 +760,7 @@
         )
 
     def own_load(w, at):
-        return pltpu.make_async_copy(grads[w].at[at, c], held["own"][w].at[lax.rem(at, 2)], own_sem.at[w, lax.rem(at, 2)])
+        return pltpu.make_async_copy(grads[chunks[w][0]].at[at, c, :, :, :, chunks[w][1]], held["own"][w].at[lax.rem(at, 2)], own_sem.at[w, lax.rem(at, 2)])
 
     def add_own(w):
         own_load(w, 0).start()
@@ -722,6 +779,52 @@
 
         lax.fori_loop(0, depth, body, 0)
 
+    flat = count - 1
+    count = flat
+    flat_arrive = held["arrive"][flat]
+
+    def flat_copy(slot, source, target, device):
+        return pltpu.make_async_remote_copy(
+            src_ref=source,
+            dst_ref=target,
+            send_sem=send_sem.at[flat, slot],
+            recv_sem=recv_sem.at[flat, slot],
+            device_id=device,
+            device_id_type=MESH,
+        )
+
+    flat_line = [
+        flat_copy(k, flat_arrive.at[lax.rem(z + k, depth)], flat_planes.at[k - 1], peer_of(sizes, spot, 0, k))
+        for k in range(1, depth)
+    ]
+    flat_row = []
+    for by in range(1, seqs):
+        to = lax.rem(a * across + b + by, seqs)
+        source = flat_arrive.at[z, lax.div(to, across), lax.rem(to, across)]
+        flat_row.append(flat_copy(depth - 1 + by, source, flat_pieces.at[by - 1], along(seqs, by)))
+
+    def flat_pair():
+        twin[flat].wait_recv()
+        add_own(flat)
+        for item in flat_line:
+            item.start()
+
+    def flat_sum():
+        for item in flat_line:
+            item.wait_recv()
+        for down_at in range(down):
+            for across_at in range(across):
+                spot_ref = flat_arrive.at[z, down_at, across_at]
+                add_rows(spot_ref, spot_ref, [flat_planes.at[k, down_at, across_at] for k in range(depth - 1)])
+        for item in flat_row:
+            item.start()
+
+    def flat_finish():
+        for item in flat_row:
+            item.wait_recv()
+        out = outs[chunks[flat][0]].at[:, chunks[flat][1]]
+        add_rows(out, flat_arrive.at[z, a, b], [flat_pieces.at[at] for at in range(seqs - 1)])
+
     small_out[...] = small[...]
     edges = spread_edge(seqs, edge, arrived, edge_send, edge_recv, False)
     units = rows * (chans // width)
@@ -740,6 +843,7 @@
 
     for w in range(min(2, count)):
         twin[w].start()
+    twin[flat].start()
     lax.fori_loop(0, units, last_unit, 0)
     for item in edges:
         item.start()
@@ -753,6 +857,12 @@
             add_own(w)
             for item in first[w]:
                 item.start()
+        if step == 0:
+            flat_pair()
+        if step == 2:
+            flat_sum()
+        if step == 4:
+            flat_finish()
         if 1 <= step <= count:
             w = step - 1
             arrive = held["arrive"][w]
@@ -785,7 +895,7 @@
             w = step - 3
             for item in third[w]:
                 item.wait_recv()
-            add_rows(outs[w], held["arrive"][w].at[z, a, b], [held["third"][w].at[k] for k in range(depth - 1)])
+            add_rows(outs[chunks[w][0]].at[:, chunks[w][1]], held["arrive"][w].at[z, a, b], [held["third"][w].at[k] for k in range(depth - 1)])
         if step == 0:
             for item in edges:
                 item.wait()
@@ -800,6 +910,8 @@
             small_out[...] = small_out[...] + small_parts[stage]
             if stage + 1 < len(stages):
                 small_copy(stage + 1).start()
+    for item in [twin[flat]] + flat_line + flat_row:
+        item.wait_send()
     for w in range(count):
         for item in [twin[w]] + first[w] + second[w] + third[w]:
             item.wait_send()
@@ -821,14 +933,16 @@
         (across - 1, depth - half),
         (depth - 1,),
     )
-    slots = 1 + 2 * (across - 1 + down - 1) + depth - 1
+    slots = max(2 * (across - 1 + down - 1), down * across - 1) + depth
     stages = sum(size.bit_length() - 1 for size in sizes)
+    chunks = chunks_of(pieces)
+    parts = [(pieces[at][0], columns.size) for at, columns in chunks]
     rows, length, chans = feed.shape
     state = (rows, 16, chans)
     width = min(BACKWARD_WIDTH, chans)
     seqs = down * across
     results = pl.pallas_call(
-        functools.partial(scatter_kernel, sizes, count),
+        functools.partial(scatter_kernel, sizes, count, chunks),
         out_shape=[jax.ShapeDtypeStruct(piece, jnp.float32) for piece in pieces]
         + [
             jax.ShapeDtypeStruct(small.shape, jnp.float32),
@@ -836,12 +950,13 @@
         ],
         in_specs=anywhere(count) + vmem(9),
         out_specs=vmem(count + 2),
-        scratch_shapes=[pltpu.VMEM(lead + piece, jnp.bfloat16) for lead in leads for piece in pieces]
+        scratch_shapes=[pltpu.VMEM(lead + part, jnp.bfloat16) for lead in leads for part in parts]
+        + [pltpu.VMEM((depth - 1, down, across) + parts[-1], jnp.bfloat16), pltpu.VMEM((down * across - 1,) + parts[-1], jnp.bfloat16)]
         + [
             pltpu.VMEM((stages,) + small.shape, jnp.float32),
-            pltpu.SemaphoreType.DMA((count, slots)),
-            pltpu.SemaphoreType.DMA((count, slots)),
-            pltpu.SemaphoreType.DMA((count, 2)),
+            pltpu.SemaphoreType.DMA((len(chunks), slots)),
+            pltpu.SemaphoreType.DMA((len(chunks), slots)),
+            pltpu.SemaphoreType.DMA((len(chunks), 2)),
             pltpu.SemaphoreType.DMA((stages,)),
             pltpu.SemaphoreType.DMA((stages,)),
             pltpu.VMEM(state, jnp.float32),
@@ -1078,8 +1193,8 @@
     keep = jnp.broadcast_to(keep_own[:, None, :, None], (rows, 1, places, LANES)).reshape(rows, places, LANES)
     alive = jnp.min(keep_row.reshape(rows, seq_count, places), axis=2)
 
-    (value_full, mix_full, head_full, expand_full), normed_window, start, ema_low, *made = gather_weights(
-        (value_weight, mix_weight, head_weight, expand_weight),
+    (value_full, mix_full, expand_full, head_full), normed_window, start, ema_low, *made = gather_weights(
+        (value_weight, mix_weight, expand_weight, head_weight),
         normed_low,
         keep,
         decay,
@@ -1134,20 +1249,21 @@
     cot_low = cotangent.reshape(tokens, width)
     shrink_part = low(transposed(hidden_low, cot_low))
     d_expand = low(against(cot_low, shrink_full) * expand_slope)
-    expand_part = low(transposed(second_low, d_expand))
     d_first_norm, d_gain_two = second_pull(against(d_expand, expand_full))
     d_first = cot_low.astype(jnp.float32) + d_first_norm
     d_update = d_first * (candidate - residual_in) * update_gate * (1.0 - update_gate)
     d_direct = d_first * (1.0 - update_gate)
     d_head = d_first * update_gate * silu_slope(head_pre)
     d_head_low = low(d_head)
-    head_part = low(transposed(gated_low, d_head_low))
     d_gated = against(d_head_low, head_full)
     d_reset = d_gated * attended * silu_slope(reset_pre)
     d_attended = low(d_gated * reset_gate).reshape(rows, places, V)
     d_queries, key_term, d_value_pre = attend_back(
         queries_low, key_window, values_low, value_slope, d_attended, docs_row, docs_column, halo
     )
+    d_value_pre, second_late, gated_late = lax.optimization_barrier((d_value_pre, second_low, gated_low))
+    expand_part = low(transposed(second_late, d_expand))
+    head_part = low(transposed(gated_late, d_head_low))
     d_value_pre = d_value_pre.reshape(rows * window, V)
     d_keys = key_term[:, halo * places :]
     for by in range(1, halo + 1):
@@ -1187,8 +1303,8 @@
         ],
         axis=0,
     )
-    (shrink_grad, expand_grad, head_grad, value_grad, mix_grad), small_sum, d_feed = scatter_grads(
-        (shrink_part, expand_part, head_part, value_part, mix_part),
+    (shrink_grad, expand_grad, value_grad, mix_grad, head_grad), small_sum, d_feed = scatter_grads(
+        (shrink_part, expand_part, value_part, mix_part, head_part),
         small_part,
         normed_low,
         d_ema,

time: 791 us -> 769 us (0.972)
  Pallas kernels: 455 us -> 426 us
    pallas_call x1, Pallas kernels: 208 us -> 188 us  [scatter_grads(): pl.pallas_call(functools.partial(scatter_kernel, sizes, count, chunks), o...]
    pallas_call x1, Pallas kernels: 201 us -> 192 us  [gather_weights(): pl.pallas_call(functools.partial(gather_kernel, sizes, count, halo, hosts...]
  transfers between devices with their start and end apart: 7 -> 7, of which waited for: 0 -> 0; matrix products, arithmetic and copies ran while one was open for 23% -> 26% of each run, Pallas kernels for 2% -> 2%
where the time goes in v5:
time: 769 us; the launch traced here: 757 us
  Pallas kernels  426 us (55%)
  matrix products  222 us (29%)
  other arithmetic  58 us (8%)
  starting transfers between devices  18.4 us (2%)
  local copies, waits for them, and re-layouts  17.7 us (2%)
  between operations  15.4 us (2%)
    pallas_call x1, Pallas kernels, gather_weights(): pl.pallas_call(functools.partial(gather_kernel, sizes, count, halo, hosts...  192 us
    pallas_call x1, Pallas kernels, scatter_grads(): pl.pallas_call(functools.partial(scatter_kernel, sizes, count, chunks), o...  188 us
    dot_general x5, matrix products, against(): lax.dot_general(left, right, (((1,), (1,)), ((), ())), preferred_element_...  84.5 us
    dot_general x5, matrix products, transposed(): lax.dot_general(left, right, (((0,), (0,)), ((), ())), preferred_element_...  70.9 us
    dot_general x5, matrix products, product(): return jnp.dot(left, right, preferred_element_type=jnp.float32)  66.4 us
    pallas_call x1, Pallas kernels, attend_back(): pl.pallas_call(functools.partial(attend_back_kernel, halo * places), out_...  32.5 us
    ppermute x6, starting transfers between devices, shift_seq(): return lax.ppermute(values, 'seq', pairs)  18.4 us
  transfers between devices with their start and end apart: 7, of which 0 were waited for; matrix products, arithmetic and copies ran while one was open for 26% of the time, Pallas kernels for 2%

profile of v5, /device:TPU:0, one launch (start us, length us, event | category | flops | bytes accessed | tf_op | source)
XLA Modules:
  0.0 757.3 jit_solution(13530894454803806991)
XLA Ops:
  7.3 0.9 convert_subtract_fusion.1
  8.2 1.9 convert_reduce_fusion
  10.2 2.3 fusion.33
  12.9 2.7 fusion.27
  16.4 192.4 %gather_weights.1 = (bf16[4,2,2,2,32,2048]{5,4,3,2,1,0:T(8,128)(2,1)}, bf16[4,2,2,2,32,4224]{5,4,3,2,1,0:T(8,128)(2,1)}, bf16[4,2,2,2,32,4096]{5,4,3,2,1,0:T(8,1...) custom-call(bf16[32,2048]{1,0:T(8,128)(2,1)S(1)} %copy-done.16, ...), custom_call_target="tpu_custom_call" | custom-call | tf_op jit(solution)/shard_map/gather_weights/pallas_call | solution.py:624
  208.8 1.3 copy-done.1
  210.9 2.7 multiply_add_fusion
  213.6 1.1 fusion.18
  214.8 2.7 add_convert_fusion.2
  217.4 11.8 %collective-permute-start = (bf16[2,512,128]{2,1,0:T(8,128)(2,1)S(1)}, bf16[2,512,128]{2,1,0:T(8,128)(2,1)S(1)}, u32[]{:S(2)}, u32[]{:S(2)}) collective-permute-start(bf16[2,512,128]{2,1,0:T(8,128)(2,1)S(1)} %bitcast.264), channel_id=1, source_target_pairs={{0,2},{1,3},{4,6},{5,7},{8,10},{9,11},{12,14},{13,15},{16,18},{17,... | collective-permute-start | bytes 786440 | tf_op jit(solution)/shard_map/ppermute | solution.py:203
  229.2 1.5 collective-permute-start.1
  230.8 16.8 %fusion.74 = f32[1024,4224]{1,0:T(8,128)} fusion(bf16[1024,1024]{1,0:T(8,128)(2,1)} %copy-done.33, bf16[1024,4224]{1,0:T(8,128)(2,1)} %bitcast.287), kind=kOutput, calls=%fused_computation.170 | convolution fusion | flops 8858370048 | bytes 28049408 | tf_op jit(solution)/shard_map/dot_general | solution.py:185
  249.1 12.9 %attend.1 = f32[2,512,2048]{2,1,0:T(8,128)S(1)} custom-call(bf16[2,512,128]{2,1,0:T(8,128)(2,1)S(1)} %bitcast.252, bf16[2,1536,128]{2,1,0:T(8,128)(2,1)S(1)} %constant_dynamic-update-slice_fusion.key, bf16[2,1536,2048]{2,1,0:T(8,128)(2,1)} %bitcast.255, s32[2,1,1536]{2,1,0:T(1,128)S(1)} %broadcast_in_dim.20.key_docs, s32[2,512,1]{2,1,0:T(8,128)S(1)} %slice.138.query_docs), custom_call_target="tpu_custom_call" | custom-call | flops 5704253440 | bytes 20971520 | tf_op jit(solution)/shard_map/attend/pallas_call | solution.py:1025
  262.1 8.2 %fusion.3 = bf16[1024,2048]{1,0:T(8,128)(2,1)S(1)} fusion(f32[2,512,2048]{2,1,0:T(8,128)S(1)} %attend.1, f32[1024,4224]{1,0:T(8,128)} %fusion.74), kind=kLoop, calls=%fused_computation.11 | loop fusion | flops 12582912 | bytes 20971520 | tf_op jit(solution)/shard_map/convert_element_type | solution.py:197
  270.3 12.6 %fusion.69 = (f32[1024]{0:T(1024)S(1)}, f32[1024,1024]{1,0:T(8,128)S(1)}, f32[1024,1024]{1,0:T(8,128)}) fusion(f32[1024,4224]{1,0:T(8,128)} %fusion.74, bf16[2,512,1024]{2,1,0:T(8,128)(2,1)S(1)} %copy-done.19, bf16[1024,2048]{1,0:T(8,128)(2,1)S(1)} %fusion.3, bf16[2048,1024]{1,0:T(8,128)(2,1)} %bitcast.295), kind=kOutput, calls=%fused_computation.165 | convolution fusion | flops 4308597760 | bytes 27267072 | tf_op jit(solution)/shard_map/dot_general | solution.py:185
  284.1 0.8 copy-done.23
  284.9 21.5 %add_multiply_fusion = (f32[1024,4096]{1,0:T(8,128)}, bf16[1024,4096]{1,0:T(8,128)(2,1)}) fusion(bf16[1024,1024]{1,0:T(8,128)(2,1)S(1)} %multiply_convert_fusion.4, bf16[1024,4096]{1,0:T(8,128)(2,1)} %bitcast.291), kind=kOutput, calls=%fused_computation.2 | convolution fusion | flops 8627683328 | bytes 35651584 | tf_op jit(solution)/shard_map/dot_general | solution.py:185
  306.4 14.6 %convolution_convert_fusion.2 = bf16[4096,1024]{1,0:T(8,128)(2,1)} fusion(bf16[1024,4096]{1,0:T(8,128)(2,1)} %get-tuple-element.65, bf16[1024,1024]{1,0:T(8,128)(2,1)S(1)} %bitcast.263), kind=kOutput, calls=%fused_computation.18 | convolution fusion | flops 8594128896 | bytes 18874368 | tf_op jit(solution)/shard_map/dot_general | solution.py:193
  321.1 17.9 %fusion = bf16[1024,4096]{1,0:T(8,128)(2,1)} fusion(f32[1024,4096]{1,0:T(8,128)} %get-tuple-element.67, bf16[4096,1024]{1,0:T(8,128)(2,1)} %all-gather.2.cloned.1.call-done, bf16[1024,1024]{1,0:T(8,128)(2,1)} %bitcast.262), kind=kOutput, calls=%fused_computation.1 | convolution fusion | flops 8598323200 | bytes 35651584 | tf_op jit(solution)/shard_map/dot_general | solution.py:189
  339.0 16.4 %multiply_reduce_fusion = (f32[1024]{0:T(1024)}, f32[1024]{0:T(1024)S(1)}, f32[1024,1024]{1,0:T(8,128)}) fusion(f32[1024,1024]{1,0:T(8,128)S(1)} %copy-done.24, f32[1024]{0:T(1024)S(1)} %fusion.58, f32[1024]{0:T(1024)S(1)} %broadcast_multiply_fusion, f32[1024]{0:T(1024)S(1)} %bitcast.272, bf16[1024,4096]{1,0:T(8,128)(2,1)} %fusion, ...), kind=kOutput, calls=%fused_computation.59 | convolution fusion | flops 8597272576 | bytes 25186304 | tf_op jit(solution)/shard_map/dot_general | solution.py:189
  355.4 4.4 fusion.68
  361.3 8.4 %multiply_convert_fusion.2 = (bf16[1024,1024]{1,0:T(8,128)(2,1)}, bf16[1024,1024]{1,0:T(8,128)(2,1)}, f32[1024,1024]{1,0:T(8,128)}) fusion(bf16[2,512,1024]{2,1,0:T(8,128)(2,1)S(1)} %copy-done.20, f32[1024,1024]{1,0:T(8,128)S(1)} %copy-done.32, f32[1024,1024]{1,0:T(8,128)S(1)} %get-tuple-element.98, f32[1024]{0:T(1024)S(1)} %negate_multiply_fusion, ...), kind=kLoop, calls=%fused_computation.60 | loop fusion | flops 26214400 | bytes 25169920 | tf_op jit(solution)/shard_map/convert.5
  369.7 13.3 %fusion.5 = (bf16[1024,2048]{1,0:T(8,128)(2,1)}, bf16[1024,2048]{1,0:T(8,128)(2,1)}) fusion(f32[2,512,2048]{2,1,0:T(8,128)S(1)} %bitcast.251, f32[1024,4224]{1,0:T(8,128)} %fusion.74, bf16[1024,1024]{1,0:T(8,128)(2,1)} %get-tuple-element.104, bf16[2048,1024]{1,0:T(8,128)(2,1)} %bitcast.296), kind=kOutput, calls=%fused_computation.13 | convolution fusion | flops 4322230272 | bytes 31457280 | tf_op jit(solution)/shard_map/dot_general | solution.py:189
  383.1 32.5 %attend_back.1 = (f32[2,512,128]{2,1,0:T(8,128)S(1)}, f32[2,1536,128]{2,1,0:T(8,128)S(1)}, bf16[2,1536,2048]{2,1,0:T(8,128)(2,1)}) custom-call(bf16[2,512,128]{2,1,0:T(8,128)(2,1)S(1)} %bitcast.253, bf16[2,1536,128]{2,1,0:T(8,128)(2,1)S(1)} %copy-done.9, bf16[2,1536,2048]{2,1,0:T(8,128)(2,1)} %bitcast.256, bf16[2,1536,2048]{2,1,0:T(8,128)(2,1)} %bitcast.285, ...), custom_call_target="tpu_custom_call" | custom-call | flops 13690208256 | bytes 41943040 | tf_op jit(solution)/shard_map/attend_back/pallas_call | solution.py:1110
  416.4 1.3 collective-permute-start.2
  417.7 1.3 collective-permute-start.3
  419.0 19.2 %fusion.73 = (bf16[2,3,512,1024]{3,2,0,1:T(8,128)(2,1)S(1)}, f32[2,3,512,1024]{3,2,0,1:T(8,128)}) fusion(bf16[1024,2048]{1,0:T(8,128)(2,1)} %bitcast.294, bf16[2,3,512,2048]{3,2,1,0:T(8,128)(2,1)} %bitcast.297), kind=kOutput, calls=%fused_computation.168 | convolution fusion | flops 12888047616 | bytes 35651584 | tf_op jit(solution)/shard_map/dot_general | solution.py:189
  438.2 2.4 slice_bitcast_fusion.2
  440.6 1.3 collective-permute-start.4
  441.9 1.3 collective-permute-start.5
  443.2 14.9 %convolution_convert_fusion.1 = bf16[1024,4096]{1,0:T(8,128)(2,1)} fusion(bf16[1024,1024]{1,0:T(8,128)(2,1)S(1)} %copy-done.36, bf16[1024,4096]{1,0:T(8,128)(2,1)} %fusion), kind=kOutput, calls=%fused_computation.17 | convolution fusion | flops 8594128896 | bytes 18874368 | tf_op jit(solution)/shard_map/dot_general | solution.py:193
  458.1 19.7 %convolution_convert_fusion.3 = bf16[1024,2048]{1,0:T(8,128)(2,1)} fusion(bf16[3072,1024]{1,0:T(8,128)(2,1)} %bitcast.293, bf16[3072,2048]{1,0:T(8,128)(2,1)} %bitcast.298), kind=kOutput, calls=%fused_computation.70 | convolution fusion | flops 12886999040 | bytes 23068672 | tf_op jit(solution)/shard_map/dot_general | solution.py:193
  477.9 12.8 %add_convert_fusion = bf16[1024,1024]{1,0:T(8,128)(2,1)} fusion(f32[1024,1024]{1,0:T(8,128)S(1)} %copy-done.25, bf16[1024,4096]{1,0:T(8,128)(2,1)} %get-tuple-element.65, bf16[4096,1024]{1,0:T(8,128)(2,1)S(1)} %bitcast.290), kind=kOutput, calls=%fused_computation.64 | convolution fusion | flops 8592031744 | bytes 23068672 | tf_op jit(solution)/shard_map/dot_general | solution.py:185
  490.7 6.2 convolution_convert_fusion.4
  497.6 17.7 %fusion.13 = (f32[1024]{0:T(1024)S(1)}, f32[1024,1024]{1,0:T(8,128)}) fusion(f32[2,512,1024]{2,1,0:T(8,128)} %get-tuple-element.112, f32[2,512,1024]{2,1,0:T(8,128)} %copy-done.27, bf16[1024,4224]{1,0:T(8,128)(2,1)} %bitcast.288, bf16[1024,1024]{1,0:T(8,128)(2,1)} %get-tuple-element.103, bf16[1024,1024]{1,0:T(8,128)(2,1)} %get-tuple-element.104, ...), kind=kOutput, calls=%fused_computation.30 | convolution fusion | flops 8903457792 | bytes 29888512 | tf_op jit(solution)/shard_map/dot_general | solution.py:189
  515.3 4.0 bitcast_convert_fusion.refs_7_
  519.4 15.4 %convolution_convert_fusion = bf16[1024,4224]{1,0:T(8,128)(2,1)} fusion(bf16[1024,1024]{1,0:T(8,128)(2,1)S(1)} %copy-done.34, bf16[1024,1024]{1,0:T(8,128)(2,1)} %get-tuple-element.103, bf16[1024,1024]{1,0:T(8,128)(2,1)} %get-tuple-element.104, bf16[1024,2048]{1,0:T(8,128)(2,1)} %get-tuple-element.105, bf16[1024,128]{1,0:T(8,128)(2,1)S(1)} %get-tuple-element.114), kind=kOutput, calls=%fused_computation.7 | convolution fusion | flops 8897298432 | bytes 19398656 | tf_op jit(solution)/shard_map/dot_general | solution.py:193
  534.8 5.8 fusion.28
  540.6 1.3 concatenate.14.refs_5_
  541.9 188.2 %scatter_grads.1 = (f32[128,1024]{1,0:T(8,128)}, f32[32,4096]{1,0:T(8,128)}, f32[32,2048]{1,0:T(8,128)}, f32[32,4224]{1,0:T(8,128)}, f32[64,1024]{1,0:T(8,128)},...) custom-call(bf16[4,2,2,2,128,1024]{5,4,3,2,1,0:T(8,128)(2,1)} %bitcast.258, ...), custom_call_target="tpu_custom_call" | custom-call | tf_op jit(solution)/shard_map/scatter_grads/pallas_call | solution.py:944
  730.2 0.9 fusion.56
  731.2 0.9 multiply_reduce_fusion.3
  732.8 1.3 slice_reduce_fusion
  735.0 4.3 fusion.34
  739.3 0.9 copy-done.26
  740.9 4.8 fusion.32
  746.5 0.8 copy.60
  749.5 0.8 copy.64
  (204 shorter events, 12.8 us)
Async XLA Ops:
  7.2 313.9 %all-gather.2.cloned.1.call-start = ((), (), s32[]{:S(2)}) async-start(), calls=%async_computation | async-start | bytes 8650752 | tf_op jit(solution)/shard_map/all_gather | solution.py:1210
  10.2 200.7 %copy-start.50 = (f32[2,512]{1,0:T(2,128)}, f32[2,512]{1,0:T(2,128)S(1)}, u32[]{:S(2)}) copy-start(f32[2,512]{1,0:T(2,128)S(1)} %broadcast_multiply_fusion.3) | copy-start | bytes 12292
  12.5 198.4 %copy-start.52 = (f32[2,512]{1,0:T(2,128)}, f32[2,512]{1,0:T(2,128)S(1)}, u32[]{:S(2)}) copy-start(f32[2,512]{1,0:T(2,128)S(1)} %add_rsqrt_fusion) | copy-start | bytes 12292
  12.5 198.4 %copy-start.54 = (f32[1,1024]{1,0:T(1,128)}, f32[1,1024]{1,0:T(1,128)S(1)}, u32[]{:S(2)}) copy-start(f32[1,1024]{1,0:T(1,128)S(1)} %get-tuple-element.124) | copy-start | bytes 12292
  12.5 198.4 %copy-start.57 = (f32[1,1024]{1,0:T(1,128)}, f32[1,1024]{1,0:T(1,128)S(1)}, u32[]{:S(2)}) copy-start(f32[1,1024]{1,0:T(1,128)S(1)} %get-tuple-element.125) | copy-start | bytes 12292
  15.6 195.2 %copy-start.66 = (f32[3,128]{1,0:T(4,128)S(1)}, f32[3,128]{1,0:T(4,128)}, u32[]{:S(2)}) copy-start(f32[3,128]{1,0:T(4,128)} %param.27) | copy-start | bytes 4612
  16.1 194.7 %copy-start.5 = (f32[3,16,1024]{2,1,0:T(8,128)}, f32[3,16,1024]{2,1,0:T(8,128)S(1)}, u32[]{:S(2)}) copy-start(f32[3,16,1024]{2,1,0:T(8,128)S(1)} %pad_maximum_fusion.3.refs_9_.refs_13_) | copy-start | bytes 589828
  16.3 192.5 %copy-start.2 = (f32[2,512,128]{2,1,0:T(8,128)}, f32[2,512,128]{2,1,0:T(8,128)S(1)}, u32[]{:S(2)}) copy-start(f32[2,512,128]{2,1,0:T(8,128)S(1)} %reshape.264.refs_5_.refs_8_) | copy-start | bytes 1572868
  214.7 16.0 %copy-start.56 = (s32[2,2048]{1,0:T(2,128)S(1)}, s32[2,2048]{1,0:T(2,128)}, u32[]{:S(2)}) copy-start(s32[2,2048]{1,0:T(2,128)} %param.17) | copy-start | bytes 49156
  217.4 31.7 %copy-start.12 = (bf16[1024,128]{1,0:T(8,128)(2,1)}, bf16[1024,128]{1,0:T(8,128)(2,1)S(1)}, u32[]{:S(2)}) copy-start(bf16[1024,128]{1,0:T(8,128)(2,1)S(1)} %get-tuple-element.117) | copy-start | bytes 786436
  217.4 31.5 %collective-permute-start = (bf16[2,512,128]{2,1,0:T(8,128)(2,1)S(1)}, bf16[2,512,128]{2,1,0:T(8,128)(2,1)S(1)}, u32[]{:S(2)}, u32[]{:S(2)}) collective-permute-start(bf16[2,512,128]{2,1,0:T(8,128)(2,1)S(1)} %bitcast.264), channel_id=1, source_target_pairs={{0,2},{1,3},{4,6},{5,7},{8,10},{9,11},{12,14},{13,15},{16,18},{17,... | collective-permute-start | bytes 786440 | tf_op jit(solution)/shard_map/ppermute | solution.py:203
  229.2 19.8 %collective-permute-start.1 = (bf16[2,512,128]{2,1,0:T(8,128)(2,1)S(1)}, bf16[2,512,128]{2,1,0:T(8,128)(2,1)S(1)}, u32[]{:S(2)}, u32[]{:S(2)}) collective-permute-start(bf16[2,512,128]{2,1,0:T(8,128)(2,1)S(1)} %bitcast.265), channel_id=1, source_target_pairs={{0,1},{1,2},{2,3},{4,5},{5,6},{6,7},{8,9},{9,10},{10,11},{12,13},{... | collective-permute-start | bytes 786440 | tf_op jit(solution)/shard_map/ppermute | solution.py:203
  249.1 13.0 %copy-start.8 = (bf16[2,1536,128]{2,1,0:T(8,128)(2,1)}, bf16[2,1536,128]{2,1,0:T(8,128)(2,1)S(1)}, u32[]{:S(2)}) copy-start(bf16[2,1536,128]{2,1,0:T(8,128)(2,1)S(1)} %constant_dynamic-update-slice_fusion.key) | copy-start | bytes 2359300
  262.1 8.2 %copy-start = (f32[2,512,2048]{2,1,0:T(8,128)}, f32[2,512,2048]{2,1,0:T(8,128)S(1)}, u32[]{:S(2)}) copy-start(f32[2,512,2048]{2,1,0:T(8,128)S(1)} %attend.1) | copy-start | bytes 25165828
  262.1 8.2 %copy-start.19 = (bf16[2,512,1024]{2,1,0:T(8,128)(2,1)S(1)}, bf16[2,512,1024]{2,1,0:T(8,128)(2,1)}, u32[]{:S(2)}) copy-start(bf16[2,512,1024]{2,1,0:T(8,128)(2,1)} %param.15) | copy-start | bytes 6291460
  270.3 12.6 %copy-start.30 = (bf16[1024,2048]{1,0:T(8,128)(2,1)}, bf16[1024,2048]{1,0:T(8,128)(2,1)S(1)}, u32[]{:S(2)}) copy-start(bf16[1024,2048]{1,0:T(8,128)(2,1)S(1)} %fusion.3) | copy-start | bytes 12582916
  284.9 21.5 %copy-start.35 = (bf16[1024,1024]{1,0:T(8,128)(2,1)}, bf16[1024,1024]{1,0:T(8,128)(2,1)S(1)}, u32[]{:S(2)}) copy-start(bf16[1024,1024]{1,0:T(8,128)(2,1)S(1)} %multiply_convert_fusion.4) | copy-start | bytes 6291460
  284.9 21.5 %copy-start.37 = (bf16[2,512,1024]{2,1,0:T(8,128)(2,1)S(1)}, bf16[2,512,1024]{2,1,0:T(8,128)(2,1)}, u32[]{:S(2)}) copy-start(bf16[2,512,1024]{2,1,0:T(8,128)(2,1)} %param.16) | copy-start | bytes 6291460
  321.1 17.9 %copy-start.24 = (f32[1024,1024]{1,0:T(8,128)S(1)}, f32[1024,1024]{1,0:T(8,128)}, u32[]{:S(2)}) copy-start(f32[1024,1024]{1,0:T(8,128)} %copy-done.23) | copy-start | bytes 12582916
  355.4 14.3 %slice-start = ((s8[8388608]{0:T(1024)(128)(4,1)}), s8[4194304]{0:T(1024)(128)(4,1)S(1)}, s32[]{:S(2)}) async-start(s8[8388608]{0:T(1024)(128)(4,1)} %bitcast.250), calls=%async_computation.1 | async-start | bytes 8388608
  361.3 8.4 %slice-start.1 = ((s8[8388608]{0:T(1024)(128)(4,1)}), s8[4194304]{0:T(1024)(128)(4,1)S(1)}, s32[]{:S(2)}) async-start(s8[8388608]{0:T(1024)(128)(4,1)} %bitcast.250), calls=%async_computation.2 | async-start | bytes 8388608
  369.7 13.4 %copy-start.9 = (bf16[2,1536,128]{2,1,0:T(8,128)(2,1)S(1)}, bf16[2,1536,128]{2,1,0:T(8,128)(2,1)}, u32[]{:S(2)}) copy-start(bf16[2,1536,128]{2,1,0:T(8,128)(2,1)} %copy-done.8) | copy-start | bytes 2359300
  369.7 13.4 %copy-start.13 = (bf16[1024,128]{1,0:T(8,128)(2,1)S(1)}, bf16[1024,128]{1,0:T(8,128)(2,1)}, u32[]{:S(2)}) copy-start(bf16[1024,128]{1,0:T(8,128)(2,1)} %copy-done.12) | copy-start | bytes 786436
  415.6 22.6 %copy-start.3 = (f32[2,512,128]{2,1,0:T(8,128)}, f32[2,512,128]{2,1,0:T(8,128)S(1)}, u32[]{:S(2)}) copy-start(f32[2,512,128]{2,1,0:T(8,128)S(1)} %get-tuple-element.69) | copy-start | bytes 1572868
  416.4 80.6 %collective-permute-start.2 = (bf16[2,512,128]{2,1,0:T(8,128)(2,1)}, bf16[2,512,128]{2,1,0:T(8,128)(2,1)S(1)}, u32[]{:S(2)}, u32[]{:S(2)}) collective-permute-start(bf16[2,512,128]{2,1,0:T(8,128)(2,1)} %get-tuple-element.115), channel_id=1, source_target_pairs={{1,0},{2,1},{3,2},{5,4},{6,5},{7,6},{9,8},{10,9},{11,10},{13,12},{... | collective-permute-start | bytes 786440 | tf_op jit(solution)/shard_map/ppermute | solution.py:203
  417.7 79.3 %collective-permute-start.3 = (bf16[2,512,128]{2,1,0:T(8,128)(2,1)S(1)}, bf16[2,512,128]{2,1,0:T(8,128)(2,1)S(1)}, u32[]{:S(2)}, u32[]{:S(2)}) collective-permute-start(bf16[2,512,128]{2,1,0:T(8,128)(2,1)S(1)} %get-tuple-element.116), channel_id=1, source_target_pairs={{2,0},{3,1},{6,4},{7,5},{10,8},{11,9},{14,12},{15,13},{18,16},{19,... | collective-permute-start | bytes 786440 | tf_op jit(solution)/shard_map/ppermute | solution.py:203
  440.6 94.2 %collective-permute-start.4 = (bf16[2,512,1024]{2,1,0:T(8,128)(2,1)}, bf16[2,512,1024]{2,1,0:T(8,128)(2,1)}, u32[]{:S(2)}, u32[]{:S(2)}) collective-permute-start(bf16[2,512,1024]{2,1,0:T(8,128)(2,1)} %get-tuple-element.110), channel_id=1, source_target_pairs={{1,0},{2,1},{3,2},{5,4},{6,5},{7,6},{9,8},{10,9},{11,10},{13,12},{... | collective-permute-start | bytes 6291464 | tf_op jit(solution)/shard_map/ppermute | solution.py:203
  441.9 92.9 %collective-permute-start.5 = (bf16[2,512,1024]{2,1,0:T(8,128)(2,1)}, bf16[2,512,1024]{2,1,0:T(8,128)(2,1)}, u32[]{:S(2)}, u32[]{:S(2)}) collective-permute-start(bf16[2,512,1024]{2,1,0:T(8,128)(2,1)} %get-tuple-element.111), channel_id=1, source_target_pairs={{2,0},{3,1},{6,4},{7,5},{10,8},{11,9},{14,12},{15,13},{18,16},{19,... | collective-permute-start | bytes 6291464 | tf_op jit(solution)/shard_map/ppermute | solution.py:203
  443.2 34.7 %slice-start.2 = ((s8[8388608]{0:T(1024)(128)(4,1)}), s8[4194304]{0:T(1024)(128)(4,1)S(1)}, s32[]{:S(2)}) async-start(s8[8388608]{0:T(1024)(128)(4,1)} %bitcast.289), calls=%async_computation.3 | async-start | bytes 8388608
  458.1 19.7 %copy-start.25 = (f32[1024,1024]{1,0:T(8,128)S(1)}, f32[1024,1024]{1,0:T(8,128)}, u32[]{:S(2)}) copy-start(f32[1024,1024]{1,0:T(8,128)} %copy-done.23) | copy-start | bytes 12582916
  458.1 19.7 %slice-start.3 = ((s8[8388608]{0:T(1024)(128)(4,1)}), s8[4194304]{0:T(1024)(128)(4,1)S(1)}, s32[]{:S(2)}) async-start(s8[8388608]{0:T(1024)(128)(4,1)} %bitcast.289), calls=%async_computation.4 | async-start | bytes 8388608
  477.9 12.8 %copy-start.31 = (bf16[1024,2048]{1,0:T(8,128)(2,1)S(1)}, bf16[1024,2048]{1,0:T(8,128)(2,1)}, u32[]{:S(2)}) copy-start(bf16[1024,2048]{1,0:T(8,128)(2,1)} %copy-done.30) | copy-start | bytes 12582916
  477.9 12.8 %copy-start.39 = (bf16[1024,1024]{1,0:T(8,128)(2,1)S(1)}, bf16[1024,1024]{1,0:T(8,128)(2,1)}, u32[]{:S(2)}) copy-start(bf16[1024,1024]{1,0:T(8,128)(2,1)} %get-tuple-element.104) | copy-start | bytes 6291460
  490.7 6.5 copy-start.43
  490.7 6.5 copy-start.63
  490.7 6.5 copy-start.65
  519.3 15.5 %copy-start.21 = (bf16[2,512,1024]{2,1,0:T(8,128)(2,1)S(1)}, bf16[2,512,1024]{2,1,0:T(8,128)(2,1)}, u32[]{:S(2)}) copy-start(bf16[2,512,1024]{2,1,0:T(8,128)(2,1)} %param.15) | copy-start | bytes 6291460
  519.3 15.5 %copy-start.28 = (f32[1024,1024]{1,0:T(8,128)S(1)}, f32[1024,1024]{1,0:T(8,128)}, u32[]{:S(2)}) copy-start(f32[1024,1024]{1,0:T(8,128)} %get-tuple-element.135) | copy-start | bytes 12582916
  519.3 15.5 %copy-start.51 = (f32[2,512]{1,0:T(2,128)S(1)}, f32[2,512]{1,0:T(2,128)}, u32[]{:S(2)}) copy-start(f32[2,512]{1,0:T(2,128)} %copy-done.50) | copy-start | bytes 12292
  519.3 15.5 %copy-start.53 = (f32[2,512]{1,0:T(2,128)S(1)}, f32[2,512]{1,0:T(2,128)}, u32[]{:S(2)}) copy-start(f32[2,512]{1,0:T(2,128)} %copy-done.52) | copy-start | bytes 12292
  519.3 15.5 %copy-start.58 = (f32[1,1024]{1,0:T(1,128)S(1)}, f32[1,1024]{1,0:T(1,128)}, u32[]{:S(2)}) copy-start(f32[1,1024]{1,0:T(1,128)} %copy-done.57) | copy-start | bytes 12292
  541.9 188.3 %copy-start.7 = (f32[16,1024]{1,0:T(8,128)S(1)}, f32[16,1024]{1,0:T(8,128)}, u32[]{:S(2)}) copy-start(f32[16,1024]{1,0:T(8,128)} %copy-done.6) | copy-start | bytes 196612
  541.9 188.3 %copy-start.41 = (f32[2,1024,16]{1,2,0:T(8,128)S(1)}, f32[2,1024,16]{1,2,0:T(8,128)}, u32[]{:S(2)}) copy-start(f32[2,1024,16]{1,2,0:T(8,128)} %param.25) | copy-start | bytes 393220
  541.9 188.3 %copy-start.47 = (f32[2,1024,16]{1,2,0:T(8,128)S(1)}, f32[2,1024,16]{1,2,0:T(8,128)}, u32[]{:S(2)}) copy-start(f32[2,1024,16]{1,2,0:T(8,128)} %param.26) | copy-start | bytes 393220
  541.9 193.0 %copy-start.55 = (f32[1,1024]{1,0:T(1,128)S(1)}, f32[1,1024]{1,0:T(1,128)}, u32[]{:S(2)}) copy-start(f32[1,1024]{1,0:T(1,128)} %copy-done.54) | copy-start | bytes 12292
  740.9 7.1 copy-start.48
  740.9 7.8 %copy-start.45 = (f32[32,4096]{1,0:T(8,128)S(1)}, f32[32,4096]{1,0:T(8,128)}, u32[]{:S(2)}) copy-start(f32[32,4096]{1,0:T(8,128)} %get-tuple-element.156) | copy-start | bytes 1572868
  740.9 8.6 %copy-start.44 = (f32[128,1024]{1,0:T(8,128)S(1)}, f32[128,1024]{1,0:T(8,128)}, u32[]{:S(2)}) copy-start(f32[128,1024]{1,0:T(8,128)} %get-tuple-element.157) | copy-start | bytes 1572868
  (30 other events, 130.2 us)
Sparse Core Ops, SparseCore 0:
  211.0 88.6 all-gather.1

commit v6 on v5

--- a/solution.py
+++ b/solution.py
@@ -17,6 +17,7 @@
 FORWARD_WIDTH = 512
 BACKWARD_WIDTH = 256
 HOST_TILE = 512
+PROJECT_TILE = 384
 
 
 def lanes_at(base, group):
@@ -343,12 +344,19 @@
 
 
 def gather_kernel(sizes, count, halo, hosts, chunks, *refs):
+    hosts_in = refs[count + 6 : count + 8] if hosts else ()
+    refs = refs[: count + 6] + refs[count + 6 + len(hosts_in) :]
     shards, (feed, keep, decay, gain, reach, power) = refs[:count], refs[count : count + 6]
     wholes, (window, entry, out) = refs[count + 6 : 2 * count + 6], refs[2 * count + 6 : 2 * count + 9]
     if hosts:
-        values, slopes = refs[2 * count + 9 : 2 * count + 11]
+        skip, key_gain = hosts_in
+        values, slopes, mixed_out, projected, key_window = refs[2 * count + 9 : 2 * count + 14]
         weight, block_in, value_tile, slope_tile, weight_sem, in_sem, out_sem = refs[-7:]
-        refs = refs[: 2 * count + 9] + refs[2 * count + 11 : -7]
+        (
+            mix_full, mix_sem, skip_in, skip_sem, mixed, project_tile, project_sem, keys, keys_sem, mixed_sem,
+            key_send, key_recv, key_local, key_hand,
+        ) = refs[-21:-7]
+        refs = refs[: 2 * count + 9] + refs[2 * count + 14 : -21]
     (
         send_sem, recv_sem, local_sem, edge, arrived, edge_send, edge_recv,
         zero, halo_send, halo_recv, halo_local, hand_send, wide_feed, part,
@@ -503,6 +511,47 @@
         slope_tile[slot] = low(squash * (1.0 + before * (1.0 - squash)))
         for item in store_tiles(index):
             item.start()
+        return carry
+
+    if hosts:
+        near = Halo(
+            halo, seqs, keys, key_window, zero.at[:, :, pl.ds(0, Z)], key_send, key_recv, key_local, key_hand
+        )
+        key_own = pltpu.make_async_copy(keys, key_window.at[:, halo], keys_sem.at[0])
+        project_units = rows * (wholes[1].shape[-1] // PROJECT_TILE)
+        mixed_copy = pltpu.make_async_copy(mixed, mixed_out, mixed_sem.at[0])
+
+    def mix_row(row, carry):
+        load = pltpu.make_async_copy(skip.at[row], skip_in, skip_sem.at[0])
+        load.start()
+        load.wait()
+        before = out[row].astype(jnp.float32) + skip_in[...]
+        mixed[row] = low(jax.nn.silu(before))
+        return carry
+
+    def store_project(index):
+        slot = lax.rem(index, 2)
+        columns = pl.ds(pl.multiple_of(lax.div(index, rows) * PROJECT_TILE, LANES), PROJECT_TILE)
+        return pltpu.make_async_copy(
+            project_tile.at[slot], projected.at[lax.rem(index, rows), :, columns], project_sem.at[slot]
+        )
+
+    def project_unit(index, carry):
+        row, slot = lax.rem(index, rows), lax.rem(index, 2)
+        columns = pl.ds(pl.multiple_of(lax.div(index, rows) * PROJECT_TILE, LANES), PROJECT_TILE)
+        part_weight = mix_full[:, :, :, :, :, columns].reshape(chans, PROJECT_TILE)
+        result = product(mixed[row], part_weight)
+
+        @pl.when(index < rows)
+        def _():
+            keys[row] = low(jax.nn.silu(result[:, :Z]) * key_gain[...])
+
+        @pl.when(index >= 2)
+        def _():
+            store_project(index - 2).wait()
+
+        project_tile[slot] = result
+        store_project(index).start()
         return carry
 
     lax.fori_loop(0, units, last_unit, 0)
@@ -553,7 +602,8 @@
             for item, on in zip(flat_line, flat_twin[1:]):
                 item.wait_recv()
                 on.start()
-        lax.fori_loop(*share(units, count + 2, step), forward_unit, 0)
+        if step < count - 1:
+            lax.fori_loop(*share(units, count - 1, step), forward_unit, 0)
         if hosts and step == 2:
             for item in twin[0].values():
                 item.wait_recv()
@@ -563,12 +613,34 @@
             around.wait()
             load_block(0).start()
             full.wait()
-        if hosts and step >= 2:
-            lax.fori_loop(*share(blocks * tiles, count, step - 2), value_unit, 0)
+        if hosts and 2 <= step < count:
+            lax.fori_loop(*share(blocks * tiles, count - 2, step - 2), value_unit, 0)
+        if hosts and step == count - 1:
+            lax.fori_loop(0, rows, mix_row, 0)
+            mixed_copy.start()
+            for w in (1, 2):
+                for item in twin[w].values():
+                    item.wait_recv()
+            full_mix = pltpu.make_async_copy(wholes[1], mix_full, mix_sem.at[0])
+            full_mix.start()
+        if hosts and step == count:
+            full_mix.wait()
+            lax.fori_loop(0, rows, project_unit, 0)
+            near.start()
+            key_own.start()
+            lax.fori_loop(rows, project_units // 2, project_unit, 0)
+            near.hand_on()
+        if hosts and step == count + 1:
+            lax.fori_loop(project_units // 2, project_units, project_unit, 0)
     if hosts:
         for index in (blocks * tiles - 2, blocks * tiles - 1):
             for item in store_tiles(index):
                 item.wait()
+        for index in (project_units - 2, project_units - 1):
+            store_project(index).wait()
+        near.wait()
+        key_own.wait()
+        mixed_copy.wait()
     for item in flat_twin:
         item.wait()
     for item in flat_row + flat_line:
@@ -576,7 +648,7 @@
     for w in range(count):
         for item in twin[w].values():
             item.wait_send()
-            if w or not hosts:
+            if w > 2 or not hosts:
                 item.wait_recv()
         for item in line[w] + wide[w] + tall[w]:
             item.wait_send()
@@ -596,7 +668,7 @@
     return [pl.BlockSpec(memory_space=pl.ANY)] * count
 
 
-def gather_weights(shards, feed, keep, decay, gain, reach, power, halo):
+def gather_weights(shards, feed, keep, decay, gain, reach, power, halo, skip, key_gain):
     sizes = shape_of()
     depth, cores, down, across = sizes
     seqs = down * across
@@ -606,13 +678,32 @@
     rows, length, chans = feed.shape
     state = (rows, 16, chans)
     width = min(FORWARD_WIDTH, chans)
-    hosts = pieces[0] == shards[0].shape
+    hosts = pieces[0] == shards[0].shape and shards[1].shape[1] % PROJECT_TILE == 0
     chunks = chunks_of(pieces)
     made, extra = [], []
     if hosts:
         wide = shards[0].shape[1]
         made = [jax.ShapeDtypeStruct((rows, halo + 1, length, wide), jnp.bfloat16)] * 2
+        made += [
+            jax.ShapeDtypeStruct(feed.shape, jnp.bfloat16),
+            jax.ShapeDtypeStruct((rows, length, shards[1].shape[1]), jnp.float32),
+            jax.ShapeDtypeStruct((rows, halo + 1, length, Z), jnp.bfloat16),
+        ]
         extra = [
+            pltpu.VMEM(sizes + pieces[1], jnp.bfloat16),
+            pltpu.SemaphoreType.DMA((1,)),
+            pltpu.VMEM((length, chans), jnp.float32),
+            pltpu.SemaphoreType.DMA((1,)),
+            pltpu.VMEM(feed.shape, jnp.bfloat16),
+            pltpu.VMEM((2, length, PROJECT_TILE), jnp.float32),
+            pltpu.SemaphoreType.DMA((2,)),
+            pltpu.VMEM((rows, length, Z), jnp.bfloat16),
+            pltpu.SemaphoreType.DMA((1,)),
+            pltpu.SemaphoreType.DMA((1,)),
+            pltpu.SemaphoreType.DMA((halo,)),
+            pltpu.SemaphoreType.DMA((halo,)),
+            pltpu.SemaphoreType.DMA((halo,)),
+            pltpu.SemaphoreType.DMA((1,)),
             pltpu.VMEM(sizes + pieces[0], jnp.bfloat16),
             pltpu.VMEM((2, length, chans), jnp.bfloat16),
             pltpu.VMEM((2, length, HOST_TILE), jnp.bfloat16),
@@ -630,7 +721,7 @@
             jax.ShapeDtypeStruct(feed.shape, jnp.bfloat16),
         ]
         + made,
-        in_specs=anywhere(count) + vmem(6),
+        in_specs=anywhere(count) + vmem(6) + (anywhere(1) + vmem(1) if hosts else []),
         out_specs=anywhere(count + 1) + vmem(2) + anywhere(len(made)),
         scratch_shapes=[
             pltpu.SemaphoreType.DMA((len(chunks), slots)),
@@ -651,7 +742,7 @@
         ],
         compiler_params=pltpu.CompilerParams(collective_id=0, has_side_effects=True, vmem_limit_bytes=48 * 2**20),
         name="gather_weights",
-    )(*[shard.reshape(piece) for shard, piece in zip(shards, pieces)], feed, keep, decay, gain, reach, power)
+    )(*[shard.reshape(piece) for shard, piece in zip(shards, pieces)], feed, keep, decay, gain, reach, power, *([skip, key_gain] if hosts else []))
     total = depth * cores * down * across
     wholes = [whole.reshape(total * shard.shape[0], shard.shape[1]) for whole, shard in zip(results, shards)]
     return wholes, *results[count:]
@@ -1202,6 +1293,8 @@
         passed_on(alive, True),
         power,
         halo,
+        chan_vectors[2] * normed,
+        z_affine[2:3],
     )
     normed_window = normed_window.reshape(rows * window, width)
     value_full, mix_full, head_full, expand_full, shrink_late = lax.optimization_barrier(
@@ -1210,20 +1303,26 @@
     shrink_full = lax.all_gather(shrink_late, BOTH, axis=0, tiled=True)
 
     premix = (ema_low.astype(jnp.float32) + chan_vectors[2] * normed).reshape(tokens, width)
-    mixed_low = low(jax.nn.silu(premix))
     if made:
-        values_low, value_slope = (item.reshape(rows, window, V) for item in made)
+        values_low, value_slope = (item.reshape(rows, window, V) for item in made[:2])
+        mixed_low = made[2].reshape(tokens, width)
+        projected = made[3].reshape(tokens, made[3].shape[2])
+        key_window = made[4].reshape(rows, window, Z)
+        shared_pre = projected[:, :Z]
+        shared = jax.nn.silu(shared_pre)
+        queries_low = low(shared * z_affine[0] + z_affine[1]).reshape(rows, places, Z)
     else:
+        mixed_low = low(jax.nn.silu(premix))
         value_pre = product(normed_window, value_full)
         values_low = low(jax.nn.silu(value_pre)).reshape(rows, window, V)
         value_slope = low(silu_slope(value_pre)).reshape(rows, window, V)
-    shared_pre = product(mixed_low, mix_full[:, :Z])
-    shared = jax.nn.silu(shared_pre)
-    queries_low = low(shared * z_affine[0] + z_affine[1]).reshape(rows, places, Z)
-    keys_low = low(shared * z_affine[2]).reshape(rows, places, Z)
-    keys_low, mixed_low = lax.optimization_barrier((keys_low, mixed_low))
-    key_window = jnp.concatenate([shift_seq(keys_low, by) for by in range(halo, 0, -1)] + [keys_low], axis=1)
-    projected = product(mixed_low, mix_full)
+        projected = product(mixed_low, mix_full)
+        shared_pre = projected[:, :Z]
+        shared = jax.nn.silu(shared_pre)
+        queries_low = low(shared * z_affine[0] + z_affine[1]).reshape(rows, places, Z)
+        keys_low = low(shared * z_affine[2]).reshape(rows, places, Z)
+        keys_sent = [shift_seq(keys_low, by) for by in range(halo, 0, -1)]
+        key_window = jnp.concatenate(keys_sent + [keys_low], axis=1)
     reset_pre = projected[:, Z : Z + V]
     head_base = projected[:, Z + V : Z + V + width]
     update_pre = projected[:, Z + V + width :]

time: 769 us -> 756 us (0.983)
  matrix products: 222 us -> 199 us
  Pallas kernels: 426 us -> 440 us
  starting transfers between devices: 18.4 us -> 5.19 us
    dot_general x5 -> x3, matrix products: 66.4 us -> 46.3 us  [product(): return jnp.dot(left, right, preferred_element_type=jnp.float32)]
    ppermute x6 -> x4, starting transfers between devices: 18.4 us -> 5.16 us  [shift_seq(): return lax.ppermute(values, 'seq', pairs)]
    pallas_call x1, Pallas kernels: 188 us -> 196 us  [scatter_grads(): pl.pallas_call(functools.partial(scatter_kernel, sizes, count, chunks), o...]
  transfers between devices with their start and end apart: 7 -> 5, of which waited for: 0 -> 1; matrix products, arithmetic and copies ran while one was open for 26% -> 24% of each run, Pallas kernels for 2% -> 2%
where the time goes in v6:
time: 756 us; the launch traced here: 749 us
  Pallas kernels  440 us (58%)
  matrix products  199 us (26%)
  other arithmetic  64.5 us (9%)
  local copies, waits for them, and re-layouts  18.5 us (2%)
  between operations  15.5 us (2%)
    pallas_call x1, Pallas kernels, gather_weights(): pl.pallas_call(functools.partial(gather_kernel, sizes, count, halo, hosts...  199 us
    pallas_call x1, Pallas kernels, scatter_grads(): pl.pallas_call(functools.partial(scatter_kernel, sizes, count, chunks), o...  196 us
    dot_general x5, matrix products, against(): lax.dot_general(left, right, (((1,), (1,)), ((), ())), preferred_element_...  84.2 us
    dot_general x5, matrix products, transposed(): lax.dot_general(left, right, (((0,), (0,)), ((), ())), preferred_element_...  68.3 us
    dot_general x3, matrix products, product(): return jnp.dot(left, right, preferred_element_type=jnp.float32)  46.3 us
    pallas_call x1, Pallas kernels, attend_back(): pl.pallas_call(functools.partial(attend_back_kernel, halo * places), out_...  32.8 us
  transfers between devices with their start and end apart: 5, of which 1 were waited for; matrix products, arithmetic and copies ran while one was open for 24% of the time, Pallas kernels for 2%

profile of v6, /device:TPU:0, one launch (start us, length us, event | category | flops | bytes accessed | tf_op | source)
XLA Modules:
  0.0 748.6 jit_solution(3873544544170952936)
XLA Ops:
  7.3 0.9 convert_subtract_fusion.1
  8.2 1.9 convert_reduce_fusion
  10.2 2.3 fusion.32
  13.9 3.6 broadcast_multiply_fusion
  17.8 198.7 %gather_weights.1 = (bf16[4,2,2,2,32,2048]{5,4,3,2,1,0:T(8,128)(2,1)}, bf16[4,2,2,2,32,4224]{5,4,3,2,1,0:T(8,128)(2,1)}, bf16[4,2,2,2,32,4096]{5,4,3,2,1,0:T(8,1...) custom-call(bf16[32,2048]{1,0:T(8,128)(2,1)S(1)} %copy-done.15, ...), custom_call_target="tpu_custom_call" | custom-call | tf_op jit(solution)/shard_map/gather_weights/pallas_call | solution.py:715
  216.6 0.8 copy-done.1
  217.4 1.3 copy-done.4
  220.0 1.2 add_convert_fusion.2
  221.3 12.8 %attend.1 = f32[2,512,2048]{2,1,0:T(8,128)S(1)} custom-call(bf16[2,512,128]{2,1,0:T(8,128)(2,1)S(1)} %bitcast.246, bf16[2,1536,128]{2,1,0:T(8,128)(2,1)S(1)} %bitcast.248, bf16[2,1536,2048]{2,1,0:T(8,128)(2,1)} %bitcast.251, s32[2,1,1536]{2,1,0:T(1,128)S(1)} %broadcast_in_dim.20.key_docs, s32[2,512,1]{2,1,0:T(8,128)S(1)} %slice.140.query_docs), custom_call_target="tpu_custom_call" | custom-call | flops 5704253440 | bytes 20971520 | tf_op jit(solution)/shard_map/attend/pallas_call | solution.py:1116
  234.1 8.2 %fusion.3 = bf16[1024,2048]{1,0:T(8,128)(2,1)S(1)} fusion(f32[2,512,2048]{2,1,0:T(8,128)S(1)} %attend.1, f32[1024,4224]{1,0:T(8,128)} %bitcast.254), kind=kLoop, calls=%fused_computation.11 | loop fusion | flops 12582912 | bytes 20971520 | tf_op jit(solution)/shard_map/convert_element_type | solution.py:198
  242.3 12.7 %fusion.66 = (f32[1024]{0:T(1024)S(1)}, f32[1024,1024]{1,0:T(8,128)S(1)}, f32[1024,1024]{1,0:T(8,128)}) fusion(f32[1024,4224]{1,0:T(8,128)} %bitcast.255, bf16[2,512,1024]{2,1,0:T(8,128)(2,1)S(1)} %copy-done.19, bf16[1024,2048]{1,0:T(8,128)(2,1)S(1)} %fusion.3, bf16[2048,1024]{1,0:T(8,128)(2,1)} %bitcast.293), kind=kOutput, calls=%fused_computation.158 | convolution fusion | flops 4308597760 | bytes 27267072 | tf_op jit(solution)/shard_map/dot_general | solution.py:186
  256.2 0.9 copy-done.23
  257.1 21.1 %add_multiply_fusion = (f32[1024,4096]{1,0:T(8,128)}, bf16[1024,4096]{1,0:T(8,128)(2,1)}) fusion(bf16[1024,1024]{1,0:T(8,128)(2,1)S(1)} %multiply_convert_fusion.4, bf16[1024,4096]{1,0:T(8,128)(2,1)} %bitcast.289), kind=kOutput, calls=%fused_computation.2 | convolution fusion | flops 8627683328 | bytes 35651584 | tf_op jit(solution)/shard_map/dot_general | solution.py:186
  279.0 7.2 fusion.26
  286.5 11.4 %convolution_convert_fusion.2 = bf16[4096,1024]{1,0:T(8,128)(2,1)} fusion(bf16[1024,4096]{1,0:T(8,128)(2,1)S(1)} %copy-done.63, bf16[1024,1024]{1,0:T(8,128)(2,1)S(1)} %bitcast.265), kind=kOutput, calls=%fused_computation.18 | convolution fusion | flops 8594128896 | bytes 18874368 | tf_op jit(solution)/shard_map/dot_general | solution.py:194
  297.8 5.6 all-gather.2.cloned.1.call-done
  303.4 17.6 %fusion = bf16[1024,4096]{1,0:T(8,128)(2,1)} fusion(f32[1024,4096]{1,0:T(8,128)} %get-tuple-element.66, bf16[4096,1024]{1,0:T(8,128)(2,1)} %all-gather.2.cloned.1.call-done, bf16[1024,1024]{1,0:T(8,128)(2,1)} %bitcast.264), kind=kOutput, calls=%fused_computation.1 | convolution fusion | flops 8598323200 | bytes 35651584 | tf_op jit(solution)/shard_map/dot_general | solution.py:190
  321.0 16.4 %multiply_reduce_fusion = (f32[1024]{0:T(1024)}, f32[1024]{0:T(1024)S(1)}, f32[1024,1024]{1,0:T(8,128)}) fusion(f32[1024,1024]{1,0:T(8,128)S(1)} %copy-done.24, f32[1024]{0:T(1024)S(1)} %fusion.55, f32[1024]{0:T(1024)S(1)} %broadcast_multiply_fusion.1, f32[1024]{0:T(1024)S(1)} %bitcast.274, bf16[1024,4096]{1,0:T(8,128)(2,1)} %fusion, ...), kind=kOutput, calls=%fused_computation.57 | convolution fusion | flops 8597272576 | bytes 25186304 | tf_op jit(solution)/shard_map/dot_general | solution.py:190
  337.4 4.4 fusion.65
  343.3 8.3 %multiply_convert_fusion.2 = (bf16[1024,1024]{1,0:T(8,128)(2,1)}, bf16[1024,1024]{1,0:T(8,128)(2,1)}, f32[1024,1024]{1,0:T(8,128)}) fusion(bf16[2,512,1024]{2,1,0:T(8,128)(2,1)S(1)} %copy-done.20, f32[1024,1024]{1,0:T(8,128)S(1)} %copy-done.31, f32[1024,1024]{1,0:T(8,128)S(1)} %get-tuple-element.100, f32[1024]{0:T(1024)S(1)} %negate_multiply_fusion, ...), kind=kLoop, calls=%fused_computation.59 | loop fusion | flops 26214400 | bytes 25169920 | tf_op jit(solution)/shard_map/convert.5
  351.7 13.3 %fusion.5 = (bf16[1024,2048]{1,0:T(8,128)(2,1)}, bf16[1024,2048]{1,0:T(8,128)(2,1)}) fusion(f32[2,512,2048]{2,1,0:T(8,128)S(1)} %bitcast.245, f32[1024,4224]{1,0:T(8,128)} %bitcast.257, bf16[1024,1024]{1,0:T(8,128)(2,1)} %get-tuple-element.106, bf16[2048,1024]{1,0:T(8,128)(2,1)} %bitcast.294), kind=kOutput, calls=%fused_computation.13 | convolution fusion | flops 4322230272 | bytes 31457280 | tf_op jit(solution)/shard_map/dot_general | solution.py:190
  365.0 32.8 %attend_back.1 = (f32[2,512,128]{2,1,0:T(8,128)S(1)}, f32[2,1536,128]{2,1,0:T(8,128)S(1)}, bf16[2,1536,2048]{2,1,0:T(8,128)(2,1)}) custom-call(bf16[2,512,128]{2,1,0:T(8,128)(2,1)S(1)} %bitcast.247, bf16[2,1536,128]{2,1,0:T(8,128)(2,1)S(1)} %bitcast.249, bf16[2,1536,2048]{2,1,0:T(8,128)(2,1)} %bitcast.252, bf16[2,1536,2048]{2,1,0:T(8,128)(2,1)} %bitcast.285, ...), custom_call_target="tpu_custom_call" | custom-call | flops 13690208256 | bytes 41943040 | tf_op jit(solution)/shard_map/attend_back/pallas_call | solution.py:1201
  397.9 1.3 collective-permute-start
  399.2 1.3 collective-permute-start.1
  400.5 19.2 %fusion.70 = (bf16[2,3,512,1024]{3,2,0,1:T(8,128)(2,1)S(1)}, f32[2,3,512,1024]{3,2,0,1:T(8,128)}) fusion(bf16[1024,2048]{1,0:T(8,128)(2,1)} %bitcast.292, bf16[2,3,512,2048]{3,2,1,0:T(8,128)(2,1)} %bitcast.296), kind=kOutput, calls=%fused_computation.161 | convolution fusion | flops 12888047616 | bytes 35651584 | tf_op jit(solution)/shard_map/dot_general | solution.py:190
  419.7 2.4 slice_bitcast_fusion.2
  422.2 1.3 collective-permute-start.2
  423.5 1.3 collective-permute-start.3
  424.8 15.0 %convolution_convert_fusion.1 = bf16[1024,4096]{1,0:T(8,128)(2,1)} fusion(bf16[1024,1024]{1,0:T(8,128)(2,1)S(1)} %copy-done.33, bf16[1024,4096]{1,0:T(8,128)(2,1)} %fusion), kind=kOutput, calls=%fused_computation.17 | convolution fusion | flops 8594128896 | bytes 18874368 | tf_op jit(solution)/shard_map/dot_general | solution.py:194
  439.8 19.7 %convolution_convert_fusion.3 = bf16[1024,2048]{1,0:T(8,128)(2,1)} fusion(bf16[3072,1024]{1,0:T(8,128)(2,1)} %bitcast.291, bf16[3072,2048]{1,0:T(8,128)(2,1)} %bitcast.297), kind=kOutput, calls=%fused_computation.68 | convolution fusion | flops 12886999040 | bytes 23068672 | tf_op jit(solution)/shard_map/dot_general | solution.py:194
  459.5 12.5 %add_convert_fusion = bf16[1024,1024]{1,0:T(8,128)(2,1)} fusion(f32[1024,1024]{1,0:T(8,128)S(1)} %copy-done.25, bf16[1024,4096]{1,0:T(8,128)(2,1)} %get-tuple-element.64, bf16[4096,1024]{1,0:T(8,128)(2,1)S(1)} %bitcast.288), kind=kOutput, calls=%fused_computation.63 | convolution fusion | flops 8592031744 | bytes 23068672 | tf_op jit(solution)/shard_map/dot_general | solution.py:186
  472.1 6.2 convolution_convert_fusion.4
  478.6 1.4 fusion.39
  480.0 17.8 %fusion.13 = (f32[1024]{0:T(1024)S(1)}, f32[1024,1024]{1,0:T(8,128)}) fusion(f32[2,512,1024]{2,1,0:T(8,128)} %get-tuple-element.115, f32[2,512,1024]{2,1,0:T(8,128)} %get-tuple-element.116, bf16[1024,4224]{1,0:T(8,128)(2,1)} %bitcast.286, bf16[1024,1024]{1,0:T(8,128)(2,1)} %get-tuple-element.105, bf16[1024,1024]{1,0:T(8,128)(2,1)} %get-tuple-element.106, ...), kind=kOutput, calls=%fused_computation.30 | convolution fusion | flops 8903457792 | bytes 29888512 | tf_op jit(solution)/shard_map/dot_general | solution.py:190
  497.8 4.0 bitcast_convert_fusion.refs_7_
  501.8 16.1 %convolution_convert_fusion = bf16[1024,4224]{1,0:T(8,128)(2,1)} fusion(bf16[1024,1024]{1,0:T(8,128)(2,1)} %bitcast.295, bf16[1024,1024]{1,0:T(8,128)(2,1)S(1)} %copy-done.36, bf16[1024,1024]{1,0:T(8,128)(2,1)} %get-tuple-element.106, bf16[1024,2048]{1,0:T(8,128)(2,1)} %get-tuple-element.107, bf16[1024,128]{1,0:T(8,128)(2,1)S(1)} %get-tuple-element.110), kind=kOutput, calls=%fused_computation.7 | convolution fusion | flops 8897298432 | bytes 19398656 | tf_op jit(solution)/shard_map/dot_general | solution.py:194
  518.0 5.8 fusion.27
  523.8 1.3 concatenate.10.refs_5_
  525.1 196.1 %scatter_grads.1 = (f32[128,1024]{1,0:T(8,128)}, f32[32,4096]{1,0:T(8,128)}, f32[32,2048]{1,0:T(8,128)}, f32[32,4224]{1,0:T(8,128)}, f32[64,1024]{1,0:T(8,128)},...) custom-call(bf16[4,2,2,2,128,1024]{5,4,3,2,1,0:T(8,128)(2,1)} %bitcast.260, ...), custom_call_target="tpu_custom_call" | custom-call | tf_op jit(solution)/shard_map/scatter_grads/pallas_call | solution.py:1035
  721.2 0.9 fusion.53
  722.2 0.9 multiply_reduce_fusion.3
  723.8 1.3 slice_reduce_fusion
  726.0 4.3 fusion.33
  730.3 0.9 copy-done.26
  731.9 4.9 fusion.31
  737.5 0.8 copy.58
  739.7 0.8 copy.61
  740.5 0.8 copy.62
  (189 shorter events, 11.5 us)
Async XLA Ops:
  7.2 6.6 copy-start.18
  7.2 296.2 %all-gather.2.cloned.1.call-start = ((), (), s32[]{:S(2)}) async-start(), calls=%async_computation | async-start | bytes 8650752 | tf_op jit(solution)/shard_map/all_gather | solution.py:1303
  10.2 268.8 %copy-start.47 = (f32[2,512]{1,0:T(2,128)}, f32[2,512]{1,0:T(2,128)S(1)}, u32[]{:S(2)}) copy-start(f32[2,512]{1,0:T(2,128)S(1)} %broadcast_multiply_fusion.4) | copy-start | bytes 12292
  12.5 266.5 %copy-start.49 = (f32[2,512]{1,0:T(2,128)}, f32[2,512]{1,0:T(2,128)S(1)}, u32[]{:S(2)}) copy-start(f32[2,512]{1,0:T(2,128)S(1)} %add_rsqrt_fusion) | copy-start | bytes 12292
  12.5 266.5 %copy-start.51 = (f32[1,1024]{1,0:T(1,128)}, f32[1,1024]{1,0:T(1,128)S(1)}, u32[]{:S(2)}) copy-start(f32[1,1024]{1,0:T(1,128)S(1)} %get-tuple-element.126) | copy-start | bytes 12292
  12.5 266.5 %copy-start.54 = (f32[1,1024]{1,0:T(1,128)}, f32[1,1024]{1,0:T(1,128)S(1)}, u32[]{:S(2)}) copy-start(f32[1,1024]{1,0:T(1,128)S(1)} %get-tuple-element.127) | copy-start | bytes 12292
  13.3 206.7 %copy-start.58 = (f32[128]{0:T(128)}, f32[128]{0:T(128)S(1)}, u32[]{:S(2)}) copy-start(f32[128]{0:T(128)S(1)} %get-tuple-element.131) | copy-start | bytes 1540
  17.5 199.0 %copy-start.5 = (f32[3,16,1024]{2,1,0:T(8,128)}, f32[3,16,1024]{2,1,0:T(8,128)S(1)}, u32[]{:S(2)}) copy-start(f32[3,16,1024]{2,1,0:T(8,128)S(1)} %pad_maximum_fusion.3.refs_9_.refs_13_) | copy-start | bytes 589828
  17.7 201.6 %copy-start.53 = (s32[2,2048]{1,0:T(2,128)S(1)}, s32[2,2048]{1,0:T(2,128)}, u32[]{:S(2)}) copy-start(s32[2,2048]{1,0:T(2,128)} %param.17) | copy-start | bytes 49156
  219.3 14.7 %copy-start.11 = (bf16[2,3,512,128]{3,2,1,0:T(8,128)(2,1)}, bf16[2,3,512,128]{3,2,1,0:T(8,128)(2,1)S(1)}, u32[]{:S(2)}) copy-start(bf16[2,3,512,128]{3,2,1,0:T(8,128)(2,1)S(1)} %get-tuple-element.56) | copy-start | bytes 2359300
  221.3 12.8 %copy-start.8 = (bf16[1024,128]{1,0:T(8,128)(2,1)}, bf16[1024,128]{1,0:T(8,128)(2,1)S(1)}, u32[]{:S(2)}) copy-start(bf16[1024,128]{1,0:T(8,128)(2,1)S(1)} %add_convert_fusion.2) | copy-start | bytes 786436
  234.1 8.2 %copy-start = (f32[2,512,2048]{2,1,0:T(8,128)}, f32[2,512,2048]{2,1,0:T(8,128)S(1)}, u32[]{:S(2)}) copy-start(f32[2,512,2048]{2,1,0:T(8,128)S(1)} %attend.1) | copy-start | bytes 25165828
  234.1 8.2 %copy-start.19 = (bf16[2,512,1024]{2,1,0:T(8,128)(2,1)S(1)}, bf16[2,512,1024]{2,1,0:T(8,128)(2,1)}, u32[]{:S(2)}) copy-start(bf16[2,512,1024]{2,1,0:T(8,128)(2,1)} %param.15) | copy-start | bytes 6291460
  242.3 12.7 %copy-start.29 = (bf16[1024,2048]{1,0:T(8,128)(2,1)}, bf16[1024,2048]{1,0:T(8,128)(2,1)S(1)}, u32[]{:S(2)}) copy-start(bf16[1024,2048]{1,0:T(8,128)(2,1)S(1)} %fusion.3) | copy-start | bytes 12582916
  257.0 21.1 %copy-start.32 = (bf16[1024,1024]{1,0:T(8,128)(2,1)}, bf16[1024,1024]{1,0:T(8,128)(2,1)S(1)}, u32[]{:S(2)}) copy-start(bf16[1024,1024]{1,0:T(8,128)(2,1)S(1)} %multiply_convert_fusion.4) | copy-start | bytes 6291460
  279.0 7.2 copy-start.34
  279.0 7.4 copy-start.63
  303.4 17.6 %copy-start.24 = (f32[1024,1024]{1,0:T(8,128)S(1)}, f32[1024,1024]{1,0:T(8,128)}, u32[]{:S(2)}) copy-start(f32[1024,1024]{1,0:T(8,128)} %copy-done.23) | copy-start | bytes 12582916
  337.4 14.2 %slice-start = ((s8[8388608]{0:T(1024)(128)(4,1)}), s8[4194304]{0:T(1024)(128)(4,1)S(1)}, s32[]{:S(2)}) async-start(s8[8388608]{0:T(1024)(128)(4,1)} %bitcast.244), calls=%async_computation.1 | async-start | bytes 8388608
  343.3 8.3 %slice-start.1 = ((s8[8388608]{0:T(1024)(128)(4,1)}), s8[4194304]{0:T(1024)(128)(4,1)S(1)}, s32[]{:S(2)}) async-start(s8[8388608]{0:T(1024)(128)(4,1)} %bitcast.244), calls=%async_computation.2 | async-start | bytes 8388608
  351.6 13.3 %copy-start.9 = (bf16[1024,128]{1,0:T(8,128)(2,1)S(1)}, bf16[1024,128]{1,0:T(8,128)(2,1)}, u32[]{:S(2)}) copy-start(bf16[1024,128]{1,0:T(8,128)(2,1)} %copy-done.8) | copy-start | bytes 786436
  351.7 13.3 %copy-start.12 = (bf16[2,3,512,128]{3,2,1,0:T(8,128)(2,1)S(1)}, bf16[2,3,512,128]{3,2,1,0:T(8,128)(2,1)}, u32[]{:S(2)}) copy-start(bf16[2,3,512,128]{3,2,1,0:T(8,128)(2,1)} %copy-done.11) | copy-start | bytes 2359300
  397.8 21.9 %copy-start.2 = (f32[2,512,128]{2,1,0:T(8,128)}, f32[2,512,128]{2,1,0:T(8,128)S(1)}, u32[]{:S(2)}) copy-start(f32[2,512,128]{2,1,0:T(8,128)S(1)} %get-tuple-element.68) | copy-start | bytes 1572868
  397.9 80.5 %collective-permute-start = (bf16[2,512,128]{2,1,0:T(8,128)(2,1)S(1)}, bf16[2,512,128]{2,1,0:T(8,128)(2,1)S(1)}, u32[]{:S(2)}, u32[]{:S(2)}) collective-permute-start(bf16[2,512,128]{2,1,0:T(8,128)(2,1)S(1)} %get-tuple-element.119), channel_id=1, source_target_pairs={{1,0},{2,1},{3,2},{5,4},{6,5},{7,6},{9,8},{10,9},{11,10},{13,12},{... | collective-permute-start | bytes 786440 | tf_op jit(solution)/shard_map/ppermute | solution.py:204
  399.2 79.2 %collective-permute-start.1 = (bf16[2,512,128]{2,1,0:T(8,128)(2,1)S(1)}, bf16[2,512,128]{2,1,0:T(8,128)(2,1)S(1)}, u32[]{:S(2)}, u32[]{:S(2)}) collective-permute-start(bf16[2,512,128]{2,1,0:T(8,128)(2,1)S(1)} %get-tuple-element.120), channel_id=1, source_target_pairs={{2,0},{3,1},{6,4},{7,5},{10,8},{11,9},{14,12},{15,13},{18,16},{19,... | collective-permute-start | bytes 786440 | tf_op jit(solution)/shard_map/ppermute | solution.py:204
  422.2 95.7 %collective-permute-start.2 = (bf16[2,512,1024]{2,1,0:T(8,128)(2,1)}, bf16[2,512,1024]{2,1,0:T(8,128)(2,1)}, u32[]{:S(2)}, u32[]{:S(2)}) collective-permute-start(bf16[2,512,1024]{2,1,0:T(8,128)(2,1)} %get-tuple-element.113), channel_id=1, source_target_pairs={{1,0},{2,1},{3,2},{5,4},{6,5},{7,6},{9,8},{10,9},{11,10},{13,12},{... | collective-permute-start | bytes 6291464 | tf_op jit(solution)/shard_map/ppermute | solution.py:204
  423.5 94.4 %collective-permute-start.3 = (bf16[2,512,1024]{2,1,0:T(8,128)(2,1)}, bf16[2,512,1024]{2,1,0:T(8,128)(2,1)}, u32[]{:S(2)}, u32[]{:S(2)}) collective-permute-start(bf16[2,512,1024]{2,1,0:T(8,128)(2,1)} %get-tuple-element.114), channel_id=1, source_target_pairs={{2,0},{3,1},{6,4},{7,5},{10,8},{11,9},{14,12},{15,13},{18,16},{19,... | collective-permute-start | bytes 6291464 | tf_op jit(solution)/shard_map/ppermute | solution.py:204
  424.8 34.7 %slice-start.2 = ((s8[8388608]{0:T(1024)(128)(4,1)}), s8[4194304]{0:T(1024)(128)(4,1)S(1)}, s32[]{:S(2)}) async-start(s8[8388608]{0:T(1024)(128)(4,1)} %bitcast.287), calls=%async_computation.3 | async-start | bytes 8388608
  439.8 19.7 %copy-start.25 = (f32[1024,1024]{1,0:T(8,128)S(1)}, f32[1024,1024]{1,0:T(8,128)}, u32[]{:S(2)}) copy-start(f32[1024,1024]{1,0:T(8,128)} %copy-done.23) | copy-start | bytes 12582916
  439.8 19.7 %slice-start.3 = ((s8[8388608]{0:T(1024)(128)(4,1)}), s8[4194304]{0:T(1024)(128)(4,1)S(1)}, s32[]{:S(2)}) async-start(s8[8388608]{0:T(1024)(128)(4,1)} %bitcast.287), calls=%async_computation.4 | async-start | bytes 8388608
  459.5 12.5 %copy-start.30 = (bf16[1024,2048]{1,0:T(8,128)(2,1)S(1)}, bf16[1024,2048]{1,0:T(8,128)(2,1)}, u32[]{:S(2)}) copy-start(bf16[1024,2048]{1,0:T(8,128)(2,1)} %copy-done.29) | copy-start | bytes 12582916
  459.5 12.5 %copy-start.37 = (bf16[1024,1024]{1,0:T(8,128)(2,1)S(1)}, bf16[1024,1024]{1,0:T(8,128)(2,1)}, u32[]{:S(2)}) copy-start(bf16[1024,1024]{1,0:T(8,128)(2,1)} %get-tuple-element.106) | copy-start | bytes 6291460
  472.1 6.2 copy-start.3
  472.1 6.5 copy-start.59
  472.1 6.5 copy-start.61
  501.8 16.1 %copy-start.21 = (bf16[2,512,1024]{2,1,0:T(8,128)(2,1)S(1)}, bf16[2,512,1024]{2,1,0:T(8,128)(2,1)}, u32[]{:S(2)}) copy-start(bf16[2,512,1024]{2,1,0:T(8,128)(2,1)} %param.15) | copy-start | bytes 6291460
  501.8 16.1 %copy-start.27 = (f32[1024,1024]{1,0:T(8,128)S(1)}, f32[1024,1024]{1,0:T(8,128)}, u32[]{:S(2)}) copy-start(f32[1024,1024]{1,0:T(8,128)} %get-tuple-element.137) | copy-start | bytes 12582916
  501.8 16.1 %copy-start.48 = (f32[2,512]{1,0:T(2,128)S(1)}, f32[2,512]{1,0:T(2,128)}, u32[]{:S(2)}) copy-start(f32[2,512]{1,0:T(2,128)} %copy-done.47) | copy-start | bytes 12292
  501.8 16.1 %copy-start.50 = (f32[2,512]{1,0:T(2,128)S(1)}, f32[2,512]{1,0:T(2,128)}, u32[]{:S(2)}) copy-start(f32[2,512]{1,0:T(2,128)} %copy-done.49) | copy-start | bytes 12292
  501.8 16.1 %copy-start.55 = (f32[1,1024]{1,0:T(1,128)S(1)}, f32[1,1024]{1,0:T(1,128)}, u32[]{:S(2)}) copy-start(f32[1,1024]{1,0:T(1,128)} %copy-done.54) | copy-start | bytes 12292
  525.1 196.1 %copy-start.7 = (f32[16,1024]{1,0:T(8,128)S(1)}, f32[16,1024]{1,0:T(8,128)}, u32[]{:S(2)}) copy-start(f32[16,1024]{1,0:T(8,128)} %copy-done.6) | copy-start | bytes 196612
  525.1 196.1 %copy-start.39 = (f32[2,1024,16]{1,2,0:T(8,128)S(1)}, f32[2,1024,16]{1,2,0:T(8,128)}, u32[]{:S(2)}) copy-start(f32[2,1024,16]{1,2,0:T(8,128)} %param.25) | copy-start | bytes 393220
  525.1 196.1 %copy-start.44 = (f32[2,1024,16]{1,2,0:T(8,128)S(1)}, f32[2,1024,16]{1,2,0:T(8,128)}, u32[]{:S(2)}) copy-start(f32[2,1024,16]{1,2,0:T(8,128)} %param.26) | copy-start | bytes 393220
  525.1 200.9 %copy-start.52 = (f32[1,1024]{1,0:T(1,128)S(1)}, f32[1,1024]{1,0:T(1,128)}, u32[]{:S(2)}) copy-start(f32[1,1024]{1,0:T(1,128)} %copy-done.51) | copy-start | bytes 12292
  731.9 6.4 copy-start.46
  731.9 7.1 copy-start.45
  731.9 7.8 %copy-start.42 = (f32[32,4096]{1,0:T(8,128)S(1)}, f32[32,4096]{1,0:T(8,128)}, u32[]{:S(2)}) copy-start(f32[32,4096]{1,0:T(8,128)} %get-tuple-element.158) | copy-start | bytes 1572868
  731.9 8.6 %copy-start.41 = (f32[128,1024]{1,0:T(8,128)S(1)}, f32[128,1024]{1,0:T(8,128)}, u32[]{:S(2)}) copy-start(f32[128,1024]{1,0:T(8,128)} %get-tuple-element.159) | copy-start | bytes 1572868
  (25 other events, 108.4 us)
Sparse Core Ops, SparseCore 0:
  219.5 83.8 all-gather.1

commit v7 on v6

--- a/solution.py
+++ b/solution.py
@@ -935,9 +935,6 @@
     for w in range(min(2, count)):
         twin[w].start()
     twin[flat].start()
-    lax.fori_loop(0, units, last_unit, 0)
-    for item in edges:
-        item.start()
     busy = count - 1
     for step in range(max(count + 3, busy + len(stages))):
         if step < count:
@@ -988,11 +985,15 @@
                 item.wait_recv()
             add_rows(outs[chunks[w][0]].at[:, chunks[w][1]], held["arrive"][w].at[z, a, b], [held["third"][w].at[k] for k in range(depth - 1)])
         if step == 0:
+            lax.fori_loop(0, units, last_unit, 0)
+            for item in edges:
+                item.start()
+        if step == 1:
             for item in edges:
                 item.wait()
             join_edges(arrived, reach, power, end)
-        if step < busy:
-            lax.fori_loop(*share(units, busy, step), backward_unit, 0)
+        if 1 <= step < busy:
+            lax.fori_loop(*share(units, busy - 1, step - 1), backward_unit, 0)
         stage = step - busy
         if stage == -1:
             small_copy(0).start()
@@ -1084,11 +1085,11 @@
 
 
 QUERY_BLOCK = 256
-KEY_BLOCK = 512
+KEY_BLOCK = 768
 VALUE_BLOCK = 1024
 
 
-def attend_kernel(halo_span, query, key, value, key_docs, query_docs, out, probs):
+def attend_kernel(halo_span, query, key, value, key_docs, query_docs, gates, out, gated, probs):
     size, span = probs.shape
     first = pl.program_id(1) * size
     keys = pl.ds(pl.multiple_of(first, LANES), span)
@@ -1102,20 +1103,26 @@
 
     def body(at, carry):
         columns = pl.ds(pl.multiple_of(at * VALUE_BLOCK, VALUE_BLOCK), VALUE_BLOCK)
-        out[0, :, columns] = product(probs[...], value[0, keys, columns])
+        gate = jax.nn.silu(gates[0, :, pl.ds(pl.multiple_of(Z + at * VALUE_BLOCK, LANES), VALUE_BLOCK)])
+        local = product(probs[...], value[0, keys, columns])
+        out[0, :, columns] = local
+        gated[0, :, columns] = low(gate * local)
         return carry
 
     lax.fori_loop(0, out.shape[2] // VALUE_BLOCK, body, 0)
 
 
-def attend(query, key, value, docs_row, docs_column, halo):
+def attend(query, key, value, docs_row, docs_column, gates, halo):
     rows, places, _ = query.shape
     window, wide = value.shape[1:]
     size = min(QUERY_BLOCK, places)
     span = halo * places + size
     return pl.pallas_call(
         functools.partial(attend_kernel, halo * places),
-        out_shape=jax.ShapeDtypeStruct((rows, places, wide), jnp.float32),
+        out_shape=[
+            jax.ShapeDtypeStruct((rows, places, wide), jnp.float32),
+            jax.ShapeDtypeStruct((rows, places, wide), jnp.bfloat16),
+        ],
         grid=(rows, places // size),
         in_specs=[
             pl.BlockSpec((1, size, Z), lambda r, i: (r, i, 0)),
@@ -1123,17 +1130,18 @@
             pl.BlockSpec((1, window, wide), lambda r, i: (r, 0, 0)),
             pl.BlockSpec((1, 1, window), lambda r, i: (r, 0, 0)),
             pl.BlockSpec((1, size, 1), lambda r, i: (r, i, 0)),
+            pl.BlockSpec((1, size, gates.shape[2]), lambda r, i: (r, i, 0)),
         ],
-        out_specs=pl.BlockSpec((1, size, wide), lambda r, i: (r, i, 0)),
+        out_specs=[pl.BlockSpec((1, size, wide), lambda r, i: (r, i, 0))] * 2,
         scratch_shapes=[pltpu.VMEM((size, span), jnp.bfloat16)],
-        compiler_params=pltpu.CompilerParams(vmem_limit_bytes=40 * 2**20),
+        compiler_params=pltpu.CompilerParams(vmem_limit_bytes=48 * 2**20),
         cost_estimate=pl.CostEstimate(
             flops=2 * rows * places * span * (wide + Z),
             bytes_accessed=rows * (window * wide * 2 + places * wide * 4),
             transcendentals=rows * places * span,
         ),
         name="attend",
-    )(query, key, value, docs_row, docs_column[:, halo * places :])
+    )(query, key, value, docs_row, docs_column[:, halo * places :], gates)
 
 
 def attend_back_kernel(
@@ -1165,11 +1173,11 @@
             chances[keys, :] = expo
             return total + jnp.sum(expo, axis=0, keepdims=True)
 
-        total = lax.fori_loop(0, window // step, weigh, jnp.zeros((1, places), jnp.float32))
+        portion = 1.0 / lax.fori_loop(0, window // step, weigh, jnp.zeros((1, places), jnp.float32))
 
         def pull(at, held):
             keys = pl.ds(pl.multiple_of(at * step, step), step)
-            probs = chances[keys, :] / total
+            probs = chances[keys, :] * portion
             chances[keys, :] = probs
             local = against(value[0, keys, :], pulled[0])
             pulls[keys, :] = local
@@ -1197,7 +1205,7 @@
 def attend_back(query, key, value, slope, pulled, docs_row, docs_column, halo):
     rows, places, _ = query.shape
     window, wide = value.shape[1:]
-    step = min(KEY_BLOCK, places)
+    step = KEY_BLOCK if window % KEY_BLOCK == 0 else places
     return pl.pallas_call(
         functools.partial(attend_back_kernel, halo * places),
         out_shape=[
@@ -1332,8 +1340,9 @@
     padded_docs = jnp.pad(doc_ids, ((0, 0), (halo * places, 0)), constant_values=-1)
     key_docs = lax.dynamic_slice_in_dim(padded_docs, seq_place * places, window, 1)
     docs_row, docs_column = key_docs[:, None, :], key_docs[:, :, None]
-    attended = attend(queries_low, key_window, values_low, docs_row, docs_column, halo).reshape(tokens, V)
-    gated_low = low(reset_gate * attended)
+    gates = projected.reshape(rows, places, projected.shape[1])
+    attended, gated_low = attend(queries_low, key_window, values_low, docs_row, docs_column, gates, halo)
+    attended, gated_low = attended.reshape(tokens, V), gated_low.reshape(tokens, V)
     head_pre = head_base + product(gated_low, head_full)
     candidate = jax.nn.silu(head_pre)
     residual_in = inputs32.reshape(tokens, width)

time: 756 us -> 753 us (level)
  other arithmetic: 64.5 us -> 53.5 us
    convert_element_type x5 -> x4, other arithmetic: 14.1 us -> 5.88 us  [low(): return values.astype(jnp.bfloat16)]
  transfers between devices with their start and end apart: 5 -> 5, of which waited for: 1 -> 1; matrix products, arithmetic and copies ran while one was open for 24% -> 23% of each run, Pallas kernels for 2% -> 2%
where the time goes in v7:
time: 753 us; the launch traced here: 746 us
  Pallas kernels  445 us (59%)
  matrix products  199 us (26%)
  other arithmetic  53.5 us (7%)
  local copies, waits for them, and re-layouts  18.6 us (2%)
  between operations  15.4 us (2%)
  waiting for transfers between devices  9.17 us (1%)
    pallas_call x1, Pallas kernels, gather_weights(): pl.pallas_call(functools.partial(gather_kernel, sizes, count, halo, hosts...  199 us
    pallas_call x1, Pallas kernels, scatter_grads(): pl.pallas_call(functools.partial(scatter_kernel, sizes, count, chunks), o...  196 us
    dot_general x5, matrix products, against(): lax.dot_general(left, right, (((1,), (1,)), ((), ())), preferred_element_...  85.1 us
    dot_general x5, matrix products, transposed(): lax.dot_general(left, right, (((0,), (0,)), ((), ())), preferred_element_...  68.4 us
    dot_general x3, matrix products, product(): return jnp.dot(left, right, preferred_element_type=jnp.float32)  45.6 us
    pallas_call x1, Pallas kernels, attend_back(): pl.pallas_call(functools.partial(attend_back_kernel, halo * places), out_...  31.5 us
    pallas_call x1, Pallas kernels, attend(): pl.pallas_call(functools.partial(attend_kernel, halo * places), out_shape...  18.4 us
  transfers between devices with their start and end apart: 5, of which 1 were waited for; matrix products, arithmetic and copies ran while one was open for 23% of the time, Pallas kernels for 2%

profile of v7, /device:TPU:0, one launch (start us, length us, event | category | flops | bytes accessed | tf_op | source)
XLA Modules:
  0.0 745.6 jit_solution(2616931820057038840)
XLA Ops:
  7.3 0.9 convert_subtract_fusion.1
  8.2 1.9 convert_reduce_fusion
  10.2 2.3 fusion.30
  13.9 3.6 broadcast_multiply_fusion
  17.8 198.7 %gather_weights.1 = (bf16[4,2,2,2,32,2048]{5,4,3,2,1,0:T(8,128)(2,1)}, bf16[4,2,2,2,32,4224]{5,4,3,2,1,0:T(8,128)(2,1)}, bf16[4,2,2,2,32,4096]{5,4,3,2,1,0:T(8,1...) custom-call(bf16[32,2048]{1,0:T(8,128)(2,1)S(1)} %copy-done.14, ...), custom_call_target="tpu_custom_call" | custom-call | tf_op jit(solution)/shard_map/gather_weights/pallas_call | solution.py:715
  216.5 0.8 copy-done
  217.3 1.3 copy-done.3
  220.0 1.2 add_convert_fusion.2
  221.2 18.4 %attend.1 = (f32[2,512,2048]{2,1,0:T(8,128)}, bf16[2,512,2048]{2,1,0:T(8,128)(2,1)S(1)}) custom-call(bf16[2,512,128]{2,1,0:T(8,128)(2,1)S(1)} %bitcast.242, bf16[2,1536,128]{2,1,0:T(8,128)(2,1)S(1)} %bitcast.244, bf16[2,1536,2048]{2,1,0:T(8,128)(2,1)} %bitcast.254, s32[2,1,1536]{2,1,0:T(1,128)S(1)} %broadcast_in_dim.20.key_docs, ...), custom_call_target="tpu_custom_call" | custom-call | flops 5704253440 | bytes 20971520 | tf_op jit(solution)/shard_map/attend/pallas_call | solution.py:1120
  239.6 11.5 %fusion.64 = (f32[1024]{0:T(1024)S(1)}, f32[1024,1024]{1,0:T(8,128)S(1)}, f32[1024,1024]{1,0:T(8,128)}) fusion(f32[1024,4224]{1,0:T(8,128)} %bitcast.249, bf16[2,512,1024]{2,1,0:T(8,128)(2,1)S(1)} %copy-done.20, bf16[1024,2048]{1,0:T(8,128)(2,1)S(1)} %bitcast.246, bf16[2048,1024]{1,0:T(8,128)(2,1)S(1)} %bitcast.291), kind=kOutput, calls=%fused_computation.155 | convolution fusion | flops 4308597760 | bytes 27267072 | tf_op jit(solution)/shard_map/dot_general | solution.py:186
  252.3 0.9 copy-done.24
  253.2 21.4 %add_multiply_fusion = (f32[1024,4096]{1,0:T(8,128)}, bf16[1024,4096]{1,0:T(8,128)(2,1)}) fusion(bf16[1024,1024]{1,0:T(8,128)(2,1)S(1)} %multiply_convert_fusion.4, bf16[1024,4096]{1,0:T(8,128)(2,1)} %bitcast.286), kind=kOutput, calls=%fused_computation.2 | convolution fusion | flops 8627683328 | bytes 35651584 | tf_op jit(solution)/shard_map/dot_general | solution.py:186
  275.5 7.1 fusion.24
  282.9 11.3 %convolution_convert_fusion.2 = bf16[4096,1024]{1,0:T(8,128)(2,1)} fusion(bf16[1024,4096]{1,0:T(8,128)(2,1)S(1)} %copy-done.62, bf16[1024,1024]{1,0:T(8,128)(2,1)S(1)} %bitcast.262), kind=kOutput, calls=%fused_computation.15 | convolution fusion | flops 8594128896 | bytes 18874368 | tf_op jit(solution)/shard_map/dot_general | solution.py:194
  294.2 9.1 %all-gather.2.cloned.1.call-done = bf16[4096,1024]{1,0:T(8,128)(2,1)} async-done(((bf16[128,1024]{1,0:T(8,128)(2,1)}), bf16[4096,1024]{1,0:T(8,128)(2,1)}) %all-gather.2.cloned.1.call-update) | async-done | bytes 8388624 | tf_op jit(solution)/shard_map/all_gather | solution.py:1311
  303.3 17.4 %fusion = bf16[1024,4096]{1,0:T(8,128)(2,1)} fusion(f32[1024,4096]{1,0:T(8,128)} %get-tuple-element.69, bf16[4096,1024]{1,0:T(8,128)(2,1)} %all-gather.2.cloned.1.call-done, bf16[1024,1024]{1,0:T(8,128)(2,1)} %bitcast.261), kind=kOutput, calls=%fused_computation.1 | convolution fusion | flops 8598323200 | bytes 35651584 | tf_op jit(solution)/shard_map/dot_general | solution.py:190
  320.7 15.3 %multiply_reduce_fusion = (f32[1024]{0:T(1024)}, f32[1024]{0:T(1024)S(1)}, f32[1024,1024]{1,0:T(8,128)S(1)}) fusion(f32[1024,1024]{1,0:T(8,128)S(1)} %copy-done.25, f32[1024]{0:T(1024)S(1)} %fusion.53, f32[1024]{0:T(1024)S(1)} %broadcast_multiply_fusion.1, f32[1024]{0:T(1024)S(1)} %bitcast.271, bf16[1024,4096]{1,0:T(8,128)(2,1)} %fusion, ...), kind=kOutput, calls=%fused_computation.54 | convolution fusion | flops 8597272576 | bytes 25186304 | tf_op jit(solution)/shard_map/dot_general | solution.py:190
  336.0 1.8 fusion.63
  337.9 0.9 copy-done.29
  339.5 8.1 %multiply_convert_fusion.2 = (bf16[1024,1024]{1,0:T(8,128)(2,1)}, bf16[1024,1024]{1,0:T(8,128)(2,1)}, f32[1024,1024]{1,0:T(8,128)}) fusion(bf16[2,512,1024]{2,1,0:T(8,128)(2,1)S(1)} %copy-done.21, f32[1024,1024]{1,0:T(8,128)S(1)} %copy-done.29, f32[1024,1024]{1,0:T(8,128)S(1)} %get-tuple-element.104, f32[1024]{0:T(1024)S(1)} %negate_multiply_fusion, ...), kind=kLoop, calls=%fused_computation.56 | loop fusion | flops 26214400 | bytes 25169920 | tf_op jit(solution)/shard_map/convert.5
  347.6 15.5 %fusion.4 = (bf16[1024,2048]{1,0:T(8,128)(2,1)}, bf16[1024,2048]{1,0:T(8,128)(2,1)}) fusion(f32[2,512,2048]{2,1,0:T(8,128)} %get-tuple-element.73, f32[1024,4224]{1,0:T(8,128)} %bitcast.251, bf16[1024,1024]{1,0:T(8,128)(2,1)} %get-tuple-element.110, bf16[2048,1024]{1,0:T(8,128)(2,1)} %bitcast.290), kind=kOutput, calls=%fused_computation.11 | convolution fusion | flops 4322230272 | bytes 31457280 | tf_op jit(solution)/shard_map/dot_general | solution.py:190
  363.1 31.5 %attend_back.1 = (f32[2,512,128]{2,1,0:T(8,128)S(1)}, f32[2,1536,128]{2,1,0:T(8,128)S(1)}, bf16[2,1536,2048]{2,1,0:T(8,128)(2,1)}) custom-call(bf16[2,512,128]{2,1,0:T(8,128)(2,1)S(1)} %bitcast.243, bf16[2,1536,128]{2,1,0:T(8,128)(2,1)S(1)} %bitcast.245, bf16[2,1536,2048]{2,1,0:T(8,128)(2,1)} %bitcast.255, bf16[2,1536,2048]{2,1,0:T(8,128)(2,1)} %bitcast.282, ...), custom_call_target="tpu_custom_call" | custom-call | flops 13690208256 | bytes 41943040 | tf_op jit(solution)/shard_map/attend_back/pallas_call | solution.py:1209
  394.8 1.3 collective-permute-start
  396.1 1.3 collective-permute-start.1
  397.4 19.2 %fusion.68 = (bf16[2,3,512,1024]{3,2,0,1:T(8,128)(2,1)S(1)}, f32[2,3,512,1024]{3,2,0,1:T(8,128)}) fusion(bf16[1024,2048]{1,0:T(8,128)(2,1)} %bitcast.289, bf16[2,3,512,2048]{3,2,1,0:T(8,128)(2,1)} %bitcast.293), kind=kOutput, calls=%fused_computation.158 | convolution fusion | flops 12888047616 | bytes 35651584 | tf_op jit(solution)/shard_map/dot_general | solution.py:190
  416.5 2.4 slice_bitcast_fusion.2
  418.9 1.3 collective-permute-start.2
  420.2 1.3 collective-permute-start.3
  421.6 15.0 %convolution_convert_fusion.1 = bf16[1024,4096]{1,0:T(8,128)(2,1)} fusion(bf16[1024,1024]{1,0:T(8,128)(2,1)S(1)} %copy-done.31, bf16[1024,4096]{1,0:T(8,128)(2,1)} %fusion), kind=kOutput, calls=%fused_computation.14 | convolution fusion | flops 8594128896 | bytes 18874368 | tf_op jit(solution)/shard_map/dot_general | solution.py:194
  436.5 19.7 %convolution_convert_fusion.3 = bf16[1024,2048]{1,0:T(8,128)(2,1)} fusion(bf16[3072,1024]{1,0:T(8,128)(2,1)} %bitcast.288, bf16[3072,2048]{1,0:T(8,128)(2,1)} %bitcast.294), kind=kOutput, calls=%fused_computation.65 | convolution fusion | flops 12886999040 | bytes 23068672 | tf_op jit(solution)/shard_map/dot_general | solution.py:194
  456.3 12.7 %add_convert_fusion = bf16[1024,1024]{1,0:T(8,128)(2,1)} fusion(f32[1024,1024]{1,0:T(8,128)S(1)} %copy-done.25, bf16[1024,4096]{1,0:T(8,128)(2,1)} %get-tuple-element.67, bf16[4096,1024]{1,0:T(8,128)(2,1)S(1)} %bitcast.285), kind=kOutput, calls=%fused_computation.60 | convolution fusion | flops 8592031744 | bytes 23068672 | tf_op jit(solution)/shard_map/dot_general | solution.py:186
  469.0 6.3 convolution_convert_fusion.4
  475.6 1.4 fusion.37
  477.0 17.8 %fusion.11 = (f32[1024]{0:T(1024)S(1)}, f32[1024,1024]{1,0:T(8,128)}) fusion(f32[2,512,1024]{2,1,0:T(8,128)} %get-tuple-element.119, f32[2,512,1024]{2,1,0:T(8,128)} %get-tuple-element.120, bf16[1024,4224]{1,0:T(8,128)(2,1)} %bitcast.283, bf16[1024,1024]{1,0:T(8,128)(2,1)} %get-tuple-element.109, bf16[1024,1024]{1,0:T(8,128)(2,1)} %get-tuple-element.110, ...), kind=kOutput, calls=%fused_computation.27 | convolution fusion | flops 8903457792 | bytes 29888512 | tf_op jit(solution)/shard_map/dot_general | solution.py:190
  494.9 4.0 bitcast_convert_fusion.refs_7_
  498.9 16.1 %convolution_convert_fusion = bf16[1024,4224]{1,0:T(8,128)(2,1)} fusion(bf16[1024,1024]{1,0:T(8,128)(2,1)} %bitcast.292, bf16[1024,1024]{1,0:T(8,128)(2,1)S(1)} %copy-done.34, bf16[1024,1024]{1,0:T(8,128)(2,1)} %get-tuple-element.110, bf16[1024,2048]{1,0:T(8,128)(2,1)} %get-tuple-element.111, bf16[1024,128]{1,0:T(8,128)(2,1)S(1)} %get-tuple-element.114), kind=kOutput, calls=%fused_computation.7 | convolution fusion | flops 8897298432 | bytes 19398656 | tf_op jit(solution)/shard_map/dot_general | solution.py:194
  515.0 5.8 fusion.25
  520.8 1.3 concatenate.10.refs_5_
  522.2 196.0 %scatter_grads.1 = (f32[128,1024]{1,0:T(8,128)}, f32[32,4096]{1,0:T(8,128)}, f32[32,2048]{1,0:T(8,128)}, f32[32,4224]{1,0:T(8,128)}, f32[64,1024]{1,0:T(8,128)},...) custom-call(bf16[4,2,2,2,128,1024]{5,4,3,2,1,0:T(8,128)(2,1)} %bitcast.257, ...), custom_call_target="tpu_custom_call" | custom-call | tf_op jit(solution)/shard_map/scatter_grads/pallas_call | solution.py:1036
  718.2 0.9 fusion.51
  719.2 0.9 multiply_reduce_fusion.3
  720.8 1.3 slice_reduce_fusion
  723.0 4.3 fusion.31
  727.3 0.9 copy-done.26
  728.9 4.9 fusion.29
  734.5 0.8 copy.58
  736.7 0.8 copy.61
  737.5 0.8 copy.62
  (181 shorter events, 10.7 us)
Async XLA Ops:
  7.2 6.6 copy-start.19
  7.2 296.1 %all-gather.2.cloned.1.call-start = ((), (), s32[]{:S(2)}) async-start(), calls=%async_computation | async-start | bytes 8650752 | tf_op jit(solution)/shard_map/all_gather | solution.py:1311
  10.2 265.3 %copy-start.45 = (f32[2,512]{1,0:T(2,128)}, f32[2,512]{1,0:T(2,128)S(1)}, u32[]{:S(2)}) copy-start(f32[2,512]{1,0:T(2,128)S(1)} %broadcast_multiply_fusion.4) | copy-start | bytes 12292
  12.5 263.0 %copy-start.47 = (f32[2,512]{1,0:T(2,128)}, f32[2,512]{1,0:T(2,128)S(1)}, u32[]{:S(2)}) copy-start(f32[2,512]{1,0:T(2,128)S(1)} %add_rsqrt_fusion) | copy-start | bytes 12292
  12.5 263.0 %copy-start.49 = (f32[1,1024]{1,0:T(1,128)}, f32[1,1024]{1,0:T(1,128)S(1)}, u32[]{:S(2)}) copy-start(f32[1,1024]{1,0:T(1,128)S(1)} %get-tuple-element.130) | copy-start | bytes 12292
  12.5 262.9 %copy-start.52 = (f32[1,1024]{1,0:T(1,128)}, f32[1,1024]{1,0:T(1,128)S(1)}, u32[]{:S(2)}) copy-start(f32[1,1024]{1,0:T(1,128)S(1)} %get-tuple-element.131) | copy-start | bytes 12292
  13.3 206.7 %copy-start.56 = (f32[128]{0:T(128)}, f32[128]{0:T(128)S(1)}, u32[]{:S(2)}) copy-start(f32[128]{0:T(128)S(1)} %get-tuple-element.135) | copy-start | bytes 1540
  17.5 199.0 %copy-start.4 = (f32[3,16,1024]{2,1,0:T(8,128)}, f32[3,16,1024]{2,1,0:T(8,128)S(1)}, u32[]{:S(2)}) copy-start(f32[3,16,1024]{2,1,0:T(8,128)S(1)} %pad_maximum_fusion.3.refs_9_.refs_13_) | copy-start | bytes 589828
  17.7 201.6 %copy-start.51 = (s32[2,2048]{1,0:T(2,128)S(1)}, s32[2,2048]{1,0:T(2,128)}, u32[]{:S(2)}) copy-start(s32[2,2048]{1,0:T(2,128)} %param.17) | copy-start | bytes 49156
  219.3 20.3 %copy-start.10 = (bf16[2,3,512,128]{3,2,1,0:T(8,128)(2,1)}, bf16[2,3,512,128]{3,2,1,0:T(8,128)(2,1)S(1)}, u32[]{:S(2)}) copy-start(bf16[2,3,512,128]{3,2,1,0:T(8,128)(2,1)S(1)} %get-tuple-element.58) | copy-start | bytes 2359300
  221.2 18.4 %copy-start.7 = (bf16[1024,128]{1,0:T(8,128)(2,1)}, bf16[1024,128]{1,0:T(8,128)(2,1)S(1)}, u32[]{:S(2)}) copy-start(bf16[1024,128]{1,0:T(8,128)(2,1)S(1)} %add_convert_fusion.2) | copy-start | bytes 786436
  221.2 18.4 %copy-start.20 = (bf16[2,512,1024]{2,1,0:T(8,128)(2,1)S(1)}, bf16[2,512,1024]{2,1,0:T(8,128)(2,1)}, u32[]{:S(2)}) copy-start(bf16[2,512,1024]{2,1,0:T(8,128)(2,1)} %param.15) | copy-start | bytes 6291460
  221.2 18.4 %copy-start.61 = (bf16[4,2,2,2,64,1024]{5,4,3,2,1,0:T(8,128)(2,1)S(1)}, bf16[4,2,2,2,64,1024]{5,4,3,2,1,0:T(8,128)(2,1)}, u32[]{:S(2)}) copy-start(bf16[4,2,2,2,64,1024]{5,4,3,2,1,0:T(8,128)(2,1)} %get-tuple-element.63) | copy-start | bytes 12582916
  239.6 11.6 %copy-start.17 = (bf16[2,512,2048]{2,1,0:T(8,128)(2,1)}, bf16[2,512,2048]{2,1,0:T(8,128)(2,1)S(1)}, u32[]{:S(2)}) copy-start(bf16[2,512,2048]{2,1,0:T(8,128)(2,1)S(1)} %get-tuple-element.60) | copy-start | bytes 12582916
  253.2 21.4 %copy-start.30 = (bf16[1024,1024]{1,0:T(8,128)(2,1)}, bf16[1024,1024]{1,0:T(8,128)(2,1)S(1)}, u32[]{:S(2)}) copy-start(bf16[1024,1024]{1,0:T(8,128)(2,1)S(1)} %multiply_convert_fusion.4) | copy-start | bytes 6291460
  275.5 7.2 copy-start.32
  275.5 7.4 copy-start.62
  303.3 17.4 %copy-start.25 = (f32[1024,1024]{1,0:T(8,128)S(1)}, f32[1024,1024]{1,0:T(8,128)}, u32[]{:S(2)}) copy-start(f32[1024,1024]{1,0:T(8,128)} %copy-done.24) | copy-start | bytes 12582916
  347.6 15.5 %copy-start.8 = (bf16[1024,128]{1,0:T(8,128)(2,1)S(1)}, bf16[1024,128]{1,0:T(8,128)(2,1)}, u32[]{:S(2)}) copy-start(bf16[1024,128]{1,0:T(8,128)(2,1)} %copy-done.7) | copy-start | bytes 786436
  347.6 15.5 %copy-start.11 = (bf16[2,3,512,128]{3,2,1,0:T(8,128)(2,1)S(1)}, bf16[2,3,512,128]{3,2,1,0:T(8,128)(2,1)}, u32[]{:S(2)}) copy-start(bf16[2,3,512,128]{3,2,1,0:T(8,128)(2,1)} %copy-done.10) | copy-start | bytes 2359300
  394.6 21.9 %copy-start.1 = (f32[2,512,128]{2,1,0:T(8,128)}, f32[2,512,128]{2,1,0:T(8,128)S(1)}, u32[]{:S(2)}) copy-start(f32[2,512,128]{2,1,0:T(8,128)S(1)} %get-tuple-element.71) | copy-start | bytes 1572868
  394.8 80.7 %collective-permute-start = (bf16[2,512,128]{2,1,0:T(8,128)(2,1)S(1)}, bf16[2,512,128]{2,1,0:T(8,128)(2,1)S(1)}, u32[]{:S(2)}, u32[]{:S(2)}) collective-permute-start(bf16[2,512,128]{2,1,0:T(8,128)(2,1)S(1)} %get-tuple-element.123), channel_id=1, source_target_pairs={{1,0},{2,1},{3,2},{5,4},{6,5},{7,6},{9,8},{10,9},{11,10},{13,12},{... | collective-permute-start | bytes 786440 | tf_op jit(solution)/shard_map/ppermute | solution.py:204
  396.1 79.4 %collective-permute-start.1 = (bf16[2,512,128]{2,1,0:T(8,128)(2,1)S(1)}, bf16[2,512,128]{2,1,0:T(8,128)(2,1)S(1)}, u32[]{:S(2)}, u32[]{:S(2)}) collective-permute-start(bf16[2,512,128]{2,1,0:T(8,128)(2,1)S(1)} %get-tuple-element.124), channel_id=1, source_target_pairs={{2,0},{3,1},{6,4},{7,5},{10,8},{11,9},{14,12},{15,13},{18,16},{19,... | collective-permute-start | bytes 786440 | tf_op jit(solution)/shard_map/ppermute | solution.py:204
  418.9 96.0 %collective-permute-start.2 = (bf16[2,512,1024]{2,1,0:T(8,128)(2,1)}, bf16[2,512,1024]{2,1,0:T(8,128)(2,1)}, u32[]{:S(2)}, u32[]{:S(2)}) collective-permute-start(bf16[2,512,1024]{2,1,0:T(8,128)(2,1)} %get-tuple-element.117), channel_id=1, source_target_pairs={{1,0},{2,1},{3,2},{5,4},{6,5},{7,6},{9,8},{10,9},{11,10},{13,12},{... | collective-permute-start | bytes 6291464 | tf_op jit(solution)/shard_map/ppermute | solution.py:204
  420.2 94.7 %collective-permute-start.3 = (bf16[2,512,1024]{2,1,0:T(8,128)(2,1)}, bf16[2,512,1024]{2,1,0:T(8,128)(2,1)}, u32[]{:S(2)}, u32[]{:S(2)}) collective-permute-start(bf16[2,512,1024]{2,1,0:T(8,128)(2,1)} %get-tuple-element.118), channel_id=1, source_target_pairs={{2,0},{3,1},{6,4},{7,5},{10,8},{11,9},{14,12},{15,13},{18,16},{19,... | collective-permute-start | bytes 6291464 | tf_op jit(solution)/shard_map/ppermute | solution.py:204
  421.5 34.7 %slice-start = ((s8[8388608]{0:T(1024)(128)(4,1)}), s8[4194304]{0:T(1024)(128)(4,1)S(1)}, s32[]{:S(2)}) async-start(s8[8388608]{0:T(1024)(128)(4,1)} %bitcast.284), calls=%async_computation.1 | async-start | bytes 8388608
  436.5 19.7 %slice-start.1 = ((s8[8388608]{0:T(1024)(128)(4,1)}), s8[4194304]{0:T(1024)(128)(4,1)S(1)}, s32[]{:S(2)}) async-start(s8[8388608]{0:T(1024)(128)(4,1)} %bitcast.284), calls=%async_computation.2 | async-start | bytes 8388608
  456.3 12.7 %copy-start.18 = (bf16[2,512,2048]{2,1,0:T(8,128)(2,1)S(1)}, bf16[2,512,2048]{2,1,0:T(8,128)(2,1)}, u32[]{:S(2)}) copy-start(bf16[2,512,2048]{2,1,0:T(8,128)(2,1)} %copy-done.17) | copy-start | bytes 12582916
  456.3 12.7 %copy-start.35 = (bf16[1024,1024]{1,0:T(8,128)(2,1)S(1)}, bf16[1024,1024]{1,0:T(8,128)(2,1)}, u32[]{:S(2)}) copy-start(bf16[1024,1024]{1,0:T(8,128)(2,1)} %get-tuple-element.110) | copy-start | bytes 6291460
  469.0 6.3 copy-start.2
  469.0 6.6 copy-start.57
  469.0 6.6 copy-start.59
  498.8 16.1 %copy-start.22 = (bf16[2,512,1024]{2,1,0:T(8,128)(2,1)S(1)}, bf16[2,512,1024]{2,1,0:T(8,128)(2,1)}, u32[]{:S(2)}) copy-start(bf16[2,512,1024]{2,1,0:T(8,128)(2,1)} %param.15) | copy-start | bytes 6291460
  498.8 16.1 %copy-start.27 = (f32[1024,1024]{1,0:T(8,128)S(1)}, f32[1024,1024]{1,0:T(8,128)}, u32[]{:S(2)}) copy-start(f32[1024,1024]{1,0:T(8,128)} %get-tuple-element.141) | copy-start | bytes 12582916
  498.8 16.1 %copy-start.46 = (f32[2,512]{1,0:T(2,128)S(1)}, f32[2,512]{1,0:T(2,128)}, u32[]{:S(2)}) copy-start(f32[2,512]{1,0:T(2,128)} %copy-done.45) | copy-start | bytes 12292
  498.8 16.1 %copy-start.48 = (f32[2,512]{1,0:T(2,128)S(1)}, f32[2,512]{1,0:T(2,128)}, u32[]{:S(2)}) copy-start(f32[2,512]{1,0:T(2,128)} %copy-done.47) | copy-start | bytes 12292
  498.8 16.1 %copy-start.53 = (f32[1,1024]{1,0:T(1,128)S(1)}, f32[1,1024]{1,0:T(1,128)}, u32[]{:S(2)}) copy-start(f32[1,1024]{1,0:T(1,128)} %copy-done.52) | copy-start | bytes 12292
  515.0 5.8 copy-start.58
  522.1 196.1 %copy-start.6 = (f32[16,1024]{1,0:T(8,128)S(1)}, f32[16,1024]{1,0:T(8,128)}, u32[]{:S(2)}) copy-start(f32[16,1024]{1,0:T(8,128)} %copy-done.5) | copy-start | bytes 196612
  522.1 196.1 %copy-start.37 = (f32[2,1024,16]{1,2,0:T(8,128)S(1)}, f32[2,1024,16]{1,2,0:T(8,128)}, u32[]{:S(2)}) copy-start(f32[2,1024,16]{1,2,0:T(8,128)} %param.25) | copy-start | bytes 393220
  522.1 196.1 %copy-start.42 = (f32[2,1024,16]{1,2,0:T(8,128)S(1)}, f32[2,1024,16]{1,2,0:T(8,128)}, u32[]{:S(2)}) copy-start(f32[2,1024,16]{1,2,0:T(8,128)} %param.26) | copy-start | bytes 393220
  522.2 200.8 %copy-start.50 = (f32[1,1024]{1,0:T(1,128)S(1)}, f32[1,1024]{1,0:T(1,128)}, u32[]{:S(2)}) copy-start(f32[1,1024]{1,0:T(1,128)} %copy-done.49) | copy-start | bytes 12292
  723.0 5.9 copy-start.28
  728.9 5.6 copy-start.38
  728.9 6.4 copy-start.44
  728.9 7.1 copy-start.43
  728.9 7.8 %copy-start.40 = (f32[32,4096]{1,0:T(8,128)S(1)}, f32[32,4096]{1,0:T(8,128)}, u32[]{:S(2)}) copy-start(f32[32,4096]{1,0:T(8,128)} %get-tuple-element.162) | copy-start | bytes 1572868
  728.9 8.6 %copy-start.39 = (f32[128,1024]{1,0:T(8,128)S(1)}, f32[128,1024]{1,0:T(8,128)}, u32[]{:S(2)}) copy-start(f32[128,1024]{1,0:T(8,128)} %get-tuple-element.163) | copy-start | bytes 1572868
  (22 other events, 83.4 us)
Sparse Core Ops, SparseCore 0:
  219.4 83.8 all-gather.1
